TPU v7x, 32 devices: a whole 2x2x4 slice. The times are simulated.
32 devices in a mesh: grp: 2 (over x), tile: 16 (over z, y, core).
Axes of the slice: x: 2, y: 2, z: 4, core: 2. Of those that a mesh axis runs over, the one named last changes fastest.
Arguments:
- features: bfloat16 [384, 64, 2048], P('tile', 'grp'), may hold values from -6 to 6
- occupancy: int32 [192, 2, 16], P('tile', 'grp'), may hold values 0 or 1
- link_weights: int32 [4, 384, 64], P(None, 'tile', 'grp'), may hold values from 0 to 3
- basis_cols: bfloat16 [2048, 256], replicated, may hold values from -0.125 to 0.125
Outputs:
- product: float32 [2048, 256], P('tile')
All inputs are finite; a program needn't handle non-finite values. No bound on the sum of `occupancy` on one device may be relied on, other than what follows from the above.
Results may differ from a plain program's by a relative error of at most 0.004.
Values may be sent and summed in bfloat16 or wider, within the bound.
No kernel may reach another device: no remote copies, remote signals or barrier semaphores. Data moves between devices by JAX's collectives and lax.ppermute only.
A program may use at most 64 MiB of HBM per device.

v0:
```python
import math

import jax
import jax.numpy as jnp
from jax import lax
from jax.sharding import PartitionSpec as P


def extended(cells, sides, width):
    for axis, dim in sides:
        count = lax.axis_size(axis)
        ends = count - 1
        head = lax.slice_in_dim(cells, 0, width, axis=dim)
        tail = lax.slice_in_dim(cells, cells.shape[dim] - width, cells.shape[dim], axis=dim)
        cells = jnp.concatenate(
            [
                lax.ppermute(tail, axis, [(i, (i + 1) % count) for i in range(ends)]),
                cells,
                lax.ppermute(head, axis, [((i + 1) % count, i) for i in range(ends)]),
            ],
            axis=dim,
        )
    return cells


def apply_mask(feat_rows, mask_rows):
    lat_rows, lon_cols, word_count = feat_rows.shape
    groups = mask_rows.shape[1]
    word_blocks = mask_rows.shape[2]
    shaped = feat_rows.reshape(
        lat_rows // 2, 2, groups, lon_cols // groups, word_blocks, word_count // word_blocks
    )
    gate = mask_rows.astype(jnp.bfloat16)[:, None, :, None, :, None]
    return (shaped * gate).reshape(lat_rows * lon_cols, word_count)


def spatial_average(padded, link_weights):
    weights = link_weights.astype(jnp.float32)
    north_side = padded[:-2, 1:-1].astype(jnp.float32)
    south_side = padded[2:, 1:-1].astype(jnp.float32)
    west_side = padded[1:-1, :-2].astype(jnp.float32)
    east_side = padded[1:-1, 2:].astype(jnp.float32)
    weighted = weights[0][:, :, None] * north_side + weights[1][:, :, None] * south_side
    weighted = weighted + weights[2][:, :, None] * west_side + weights[3][:, :, None] * east_side
    weight_total = jnp.maximum(jnp.sum(weights, axis=0), 1.0)
    return (weighted / weight_total[:, :, None]).astype(jnp.bfloat16)


def per_device(features, occupancy, link_weights, basis_cols):
    lat_rows, lon_cols, word_count = features.shape
    rank_width = basis_cols.shape[1]
    masked = apply_mask(features, occupancy)
    projected = jnp.dot(masked, basis_cols, preferred_element_type=jnp.float32).astype(jnp.bfloat16)
    projected = projected.reshape(lat_rows, lon_cols, rank_width)
    padded = extended(projected, (("grp", 1), ("tile", 0)), 1)
    smooth = spatial_average(padded, link_weights).reshape(lat_rows * lon_cols, rank_width)
    scaling = 1.0 / math.sqrt(lat_rows * lon_cols * lax.axis_size("grp") * lax.axis_size("tile"))
    share_rows = word_count // lax.axis_size("tile")
    local_term = lax.dot_general(
        masked, smooth, (((0,), (0,)), ((), ())), preferred_element_type=jnp.float32
    )
    summed = lax.psum(local_term, ("grp", "tile"))
    own_rows = lax.dynamic_slice_in_dim(summed, lax.axis_index("tile") * share_rows, share_rows, 0)
    return own_rows * scaling


def solution(mesh):
    placed = (P("tile", "grp", None), P("tile", "grp", None), P(None, "tile", "grp"), P())
    return jax.shard_map(
        per_device, mesh=mesh, in_specs=placed, out_specs=P("tile", None), check_vma=False
    )
```

profile of v0, /device:TPU:0, one launch (start us, length us, event | category | flops | bytes accessed | tf_op | source)
XLA Modules:
  0.0 175.5 jit_solution(12780380878305803182)
XLA Ops:
  6.5 0.0 copy-start
  6.5 0.0 all-reduce.2.cloned.1.call-start
  6.5 0.0 copy-start.2
  6.5 0.8 convert_element_type.24
  7.4 0.5 mul.80
  7.9 0.0 copy-done
  7.9 0.9 copy-done.2
  8.8 0.0 copy-start.1
  8.8 1.0 fusion.8
  9.8 4.9 %collective-permute-start = (bf16[24,1,256]{2,1,0:T(2,128)(2,1)S(1)}, bf16[24,1,256]{2,1,0:T(2,128)(2,1)S(1)}, u32[]{:S(2)}, u32[]{:S(2)}) collective-permute-start(bf16[24,1,256]{2,1,0:T(2,128)(2,1)S(1)} %get-tuple-element.7), channel_id=1, source_target_pairs={{0,16},{1,17},{2,18},{3,19},{4,20},{5,21},{6,22},{7,23},{8,24},{9,... | collective-permute-start | bytes 36872 | tf_op jit(solution)/shard_map/ppermute | solution.py:17
  14.7 1.3 collective-permute-start.1
  16.0 0.0 copy-done.1
  16.1 0.1 collective-permute-done
  16.2 4.2 %collective-permute-done.1 = bf16[24,1,256]{2,1,0:T(2,128)(2,1)S(1)} collective-permute-done((bf16[24,1,256]{2,1,0:T(2,128)(2,1)S(1)}, bf16[24,1,256]{2,1,0:T(2,128)(2,1)S(1)}, u32[]{:S(2)}, u32[]{:S(2)}) %collective-permute-start.1) | collective-permute-done | bytes 12320 | tf_op jit(solution)/shard_map/ppermute | solution.py:19
  20.5 1.3 collective-permute-start.2
  21.8 1.3 collective-permute-start.3
  23.1 0.1 mul.74
  23.2 0.0 collective-permute-done.2
  23.2 3.4 %collective-permute-done.3 = bf16[1,34,256]{2,1,0:T(8,128)(2,1)S(1)} collective-permute-done((bf16[1,34,256]{2,1,0:T(8,128)(2,1)S(1)}, bf16[1,34,256]{2,1,0:T(8,128)(2,1)S(1)}, u32[]{:S(2)}, u32[]{:S(2)}) %collective-permute-start.3) | collective-permute-done | bytes 17440 | tf_op jit(solution)/shard_map/ppermute | solution.py:19
  26.6 3.2 %fusion.4 = f32[2048,256]{1,0:T(8,128)} fusion(bf16[24,32,2048]{2,1,0:T(8,128)(2,1)S(1)} %copy-done.2, bf16[24,2048]{1,0:T(8,128)(2,1)S(1)} %bitcast.34, bf16[24,1,256]{2,1,0:T(2,128)(2,1)S(1)} %collective-permute-done.1, bf16[24,32,256]{2,1,0:T(8,128)(2,1)S(1)} %bitcast.32, bf16[24,1,256]{2,1,0:T(2,128)(2,1)S(1)} %collective-permute-done, ...), kind=kOutput, calls=%fused_computation.5 | convolution fusion | flops 813367296 | bytes 5809152 | tf_op jit(solution)/shard_map/dot_general | solution.py:59
  29.8 0.0 all-reduce.2.cloned.1.call-update
  29.8 137.3 %all-reduce.2.cloned.1.call-done = f32[2048,256]{1,0:T(8,128)} async-done(((f32[2048,256]{1,0:T(8,128)}), f32[2048,256]{1,0:T(8,128)}) %all-reduce.2.cloned.1.call-update) | async-done | bytes 2097168 | tf_op jit(solution)/shard_map/psum | solution.py:62
  167.1 1.6 dynamic-slice_multiply_fusion
  (8 shorter events, 0.1 us)
Async XLA Ops:
  6.5 1.3 copy-start
  6.5 160.6 %all-reduce.2.cloned.1.call-start = ((), (), s32[]{:S(2)}) async-start(), calls=%async_computation | async-start | bytes 4194304 | tf_op jit(solution)/shard_map/psum | solution.py:62
  6.5 2.2 %copy-start.2 = (bf16[24,32,2048]{2,1,0:T(8,128)(2,1)S(1)}, bf16[24,32,2048]{2,1,0:T(8,128)(2,1)}, u32[]{:S(2)}) copy-start(bf16[24,32,2048]{2,1,0:T(8,128)(2,1)} %param.4) | copy-start | bytes 9437188
  8.8 7.3 %copy-start.1 = (s32[4,24,32]{2,1,0:T(8,128)S(1)}, s32[4,24,32]{2,1,0:T(8,128)}, u32[]{:S(2)}) copy-start(s32[4,24,32]{2,1,0:T(8,128)} %param.6) | copy-start | bytes 36868
  9.8 6.4 %collective-permute-start = (bf16[24,1,256]{2,1,0:T(2,128)(2,1)S(1)}, bf16[24,1,256]{2,1,0:T(2,128)(2,1)S(1)}, u32[]{:S(2)}, u32[]{:S(2)}) collective-permute-start(bf16[24,1,256]{2,1,0:T(2,128)(2,1)S(1)} %get-tuple-element.7), channel_id=1, source_target_pairs={{0,16},{1,17},{2,18},{3,19},{4,20},{5,21},{6,22},{7,23},{8,24},{9,... | collective-permute-start | bytes 36872 | tf_op jit(solution)/shard_map/ppermute | solution.py:17
  14.7 5.7 %collective-permute-start.1 = (bf16[24,1,256]{2,1,0:T(2,128)(2,1)S(1)}, bf16[24,1,256]{2,1,0:T(2,128)(2,1)S(1)}, u32[]{:S(2)}, u32[]{:S(2)}) collective-permute-start(bf16[24,1,256]{2,1,0:T(2,128)(2,1)S(1)} %get-tuple-element.8), channel_id=1, source_target_pairs={{16,0},{17,1},{18,2},{19,3},{20,4},{21,5},{22,6},{23,7},{24,8},{25... | collective-permute-start | bytes 36872 | tf_op jit(solution)/shard_map/ppermute | solution.py:19
  20.5 2.7 %collective-permute-start.2 = (bf16[1,34,256]{2,1,0:T(8,128)(2,1)S(1)}, bf16[1,34,256]{2,1,0:T(8,128)(2,1)S(1)}, u32[]{:S(2)}, u32[]{:S(2)}) collective-permute-start(bf16[1,34,256]{2,1,0:T(8,128)(2,1)S(1)} %get-tuple-element.5), channel_id=1, source_target_pairs={{0,1},{1,2},{2,3},{3,4},{4,5},{5,6},{6,7},{7,8},{8,9},{9,10},{10,1... | collective-permute-start | bytes 52232 | tf_op jit(solution)/shard_map/ppermute | solution.py:17
  21.8 4.8 %collective-permute-start.3 = (bf16[1,34,256]{2,1,0:T(8,128)(2,1)S(1)}, bf16[1,34,256]{2,1,0:T(8,128)(2,1)S(1)}, u32[]{:S(2)}, u32[]{:S(2)}) collective-permute-start(bf16[1,34,256]{2,1,0:T(8,128)(2,1)S(1)} %get-tuple-element.6), channel_id=1, source_target_pairs={{1,0},{2,1},{3,2},{4,3},{5,4},{6,5},{7,6},{8,7},{9,8},{10,9},{11,1... | collective-permute-start | bytes 52232 | tf_op jit(solution)/shard_map/ppermute | solution.py:19
Sparse Core Ops, SparseCore 0:
  29.9 137.1 all-reduce.1
where the time goes:
time: 176 us
  waiting for transfers between devices  145 us (82%)
  between operations  13.5 us (8%)
  starting transfers between devices  8.75 us (5%)
  matrix products  4.18 us (2%)
  other arithmetic  2.46 us (1%)
    psum x1, waiting for transfers between devices, per_device(): summed = lax.psum(local_term, ('grp', 'tile'))  137 us
    ppermute x2, waiting for transfers between devices, extended(): lax.ppermute(head, axis, [((i + 1) % count, i) for i in range(ends)])  7.61 us
    ppermute x2, starting transfers between devices, extended(): lax.ppermute(tail, axis, [(i, (i + 1) % count) for i in range(ends)])  6.16 us
  transfers between devices with their start and end apart: 5, of which 4 were waited for; matrix products, arithmetic and copies ran while one was open for 0% of the time, Pallas kernels for 0%

commit v1 on v0

v1 whole, which is shorter than its diff:
```python
import functools
import math

import jax
import jax.numpy as jnp
from jax import lax
from jax.experimental import pallas as pl
from jax.experimental.pallas import tpu as pltpu
from jax.sharding import PartitionSpec as P

F32 = jnp.float32
BF16 = jnp.bfloat16
AXES = ("grp", "tile")
IN_HBM = pl.BlockSpec(memory_space=pltpu.HBM)
IN_VMEM = pl.BlockSpec(memory_space=pltpu.VMEM)
KERNEL_VMEM = 24 << 20
WORD_CHUNK = 512


def project_kernel(occ_hbm, feat_hbm, basis_hbm, masked, proj, *rest):
    *edges, basis, total, occ, sems = rest
    row_a, row_b = edges[:2]
    lat, lon, words = masked.shape
    blocks = occ.shape[2]
    block = words // blocks
    chunk = min(WORD_CHUNK, words)
    count = words // chunk
    occ_copy = pltpu.make_async_copy(occ_hbm, occ, sems.at[2 * count])
    occ_copy.start()
    copies = []
    for k in range(count):
        part = pl.ds(k * chunk, chunk)
        basis_copy = pltpu.make_async_copy(basis_hbm.at[part], basis.at[part], sems.at[count + k])
        feat_copy = pltpu.make_async_copy(feat_hbm.at[:, :, part], masked.at[:, :, part], sems.at[k])
        basis_copy.start()
        feat_copy.start()
        copies.append((basis_copy, feat_copy))
    occ_copy.wait()
    for k in range(count):
        copies[k][0].wait()
        copies[k][1].wait()
        for i in range(lat // 2):
            for b in range(k * chunk // block, (k + 1) * chunk // block):
                gate = occ[i, 0, b].astype(F32).astype(BF16)
                spot = (pl.ds(2 * i, 2), slice(None), pl.ds(b * block, block))
                masked[spot] = masked[spot] * gate
        part = pl.ds(k * chunk, chunk)
        term = jnp.dot(
            masked[:, :, part].reshape(lat * lon, chunk), basis[part, :], preferred_element_type=F32
        )
        if k:
            term = total[...] + term
        if k < count - 1:
            total[...] = term
    rounded = term.astype(BF16)
    proj[...] = rounded.reshape(proj.shape)
    north, south = rounded[:lon], rounded[-lon:]
    even = lax.rem(lax.axis_index("tile"), 2) == 0
    row_a[...] = jnp.where(even, south, north)
    row_b[...] = jnp.where(even, north, south)
    grid = term.reshape(lat, lon, -1)
    west, east = grid[:, 0, :], grid[:, lon - 1, :]
    even = lax.rem(lax.axis_index("grp"), 2) == 0
    edges[2][...] = jnp.where(even, east, west).astype(BF16)
    if len(edges) > 3:
        edges[3][...] = jnp.where(even, west, east).astype(BF16)


def project(occupancy, features, basis_cols, columns):
    lat, lon, words = features.shape
    rank = basis_cols.shape[1]
    count = words // min(WORD_CHUNK, words)
    operands = [pltpu.with_memory_space_constraint(v, pltpu.HBM) for v in (occupancy, features, basis_cols)]
    return pl.pallas_call(
        project_kernel,
        out_shape=(
            pltpu.VMEM((lat, lon, words), BF16),
            pltpu.VMEM((lat, lon, rank), BF16),
            pltpu.VMEM((lon, rank), BF16),
            pltpu.VMEM((lon, rank), BF16),
        ) + (pltpu.VMEM((lat, rank), BF16),) * columns,
        in_specs=[IN_HBM] * 3,
        out_specs=(IN_VMEM,) * (4 + columns),
        scratch_shapes=[
            pltpu.VMEM(basis_cols.shape, BF16),
            pltpu.VMEM((lat * lon, rank), F32),
            pltpu.SMEM(occupancy.shape, jnp.int32),
            pltpu.SemaphoreType.DMA((2 * count + 1,)),
        ],
        compiler_params=pltpu.CompilerParams(vmem_limit_bytes=KERNEL_VMEM),
        cost_estimate=pl.CostEstimate(
            flops=2 * lat * lon * words * rank, bytes_accessed=2 * lat * lon * words, transcendentals=0
        ),
    )(*operands)


def smooth_rows(proj, north, south, west, east, links, smooth):
    lat, lon, rank = proj.shape
    weights = links[...].astype(F32)
    weights = weights / jnp.maximum(jnp.sum(weights, axis=0), 1.0)
    columns = [jnp.transpose(weights[k]) for k in range(4)]
    place = lax.broadcasted_iota(jnp.int32, (lon, rank), 0)
    for i in range(lat):
        row = proj[i].astype(F32)
        above = proj[i - 1].astype(F32) if i else north
        below = proj[i + 1].astype(F32) if i < lat - 1 else south
        left = jnp.where(place == 0, west[i:i + 1, :], pltpu.roll(row, 1, 0))
        right = jnp.where(place == lon - 1, east[i:i + 1, :], pltpu.roll(row, lon - 1, 0))
        link = [jnp.broadcast_to(columns[k][:, i:i + 1], (lon, rank)) for k in range(4)]
        value = link[0] * above + link[1] * below + link[2] * left + link[3] * right
        smooth[pl.ds(i * lon, lon), :] = value.astype(BF16)


def partial_kernel(orders, masked, proj, halo_row_a, halo_row_b, *rest):
    *halo_cols, links, send, keep, smooth = rest
    lat, lon, words = masked.shape
    rank = proj.shape[2]
    pairs, share = send.shape[:2]
    row_a, row_b = halo_row_a[...].astype(F32), halo_row_b[...].astype(F32)
    odd = lax.rem(lax.axis_index("tile"), 2)
    north = jnp.where(odd == 0, row_b, row_a)
    south = jnp.where(odd == 0, row_a, row_b)
    col_a = halo_cols[0][...].astype(F32)
    col_b = halo_cols[1][...].astype(F32) if len(halo_cols) > 1 else jnp.zeros_like(col_a)
    even = lax.rem(lax.axis_index("grp"), 2) == 0
    west = jnp.where(even, col_b, col_a)
    east = jnp.where(even, col_a, col_b)
    smooth_rows(proj, north, south, west, east, links, smooth)
    values = smooth[...]
    step = 256
    for first in range(0, words, step):
        part = masked[:, :, pl.ds(first, step)].reshape(lat * lon, step)
        term = lax.dot_general(part, values, (((0,), (0,)), ((), ())), preferred_element_type=F32)
        for at in range(0, step, 2 * share):
            pair = (first + at) // (2 * share)
            here = jnp.where(odd == 0, orders[0][pair], orders[1][pair])
            there = jnp.where(odd == 0, orders[1][pair], orders[0][pair])
            low, high = term[at:at + share], term[at + share:at + 2 * share]
            send[there] = jnp.where(odd == 0, high, low).astype(BF16)
            keep[here] = jnp.where(odd == 0, low, high)


def partial_product(orders, share, masked, proj, rows, cols, link_weights):
    lat, lon, words = masked.shape
    rank = proj.shape[2]
    pairs = words // share // 2
    return pl.pallas_call(
        functools.partial(partial_kernel, orders),
        out_shape=(pltpu.VMEM((pairs, share, rank), BF16), pltpu.VMEM((pairs, share, rank), F32)),
        in_specs=[IN_VMEM] * (5 + len(cols)),
        out_specs=(IN_VMEM,) * 2,
        scratch_shapes=[pltpu.VMEM((lat * lon, rank), BF16)],
        compiler_params=pltpu.CompilerParams(vmem_limit_bytes=KERNEL_VMEM),
        cost_estimate=pl.CostEstimate(
            flops=2 * lat * lon * words * rank, bytes_accessed=2 * lat * lon * words, transcendentals=0
        ),
    )(masked, proj, *rows, *cols, link_weights)


def bit_orders(bits):
    plain = list(range(1, bits))
    turned = plain[1::-1] + plain[2:]
    return plain, turned


def block_places(order):
    steps = len(order)
    places = []
    for pair in range(1 << steps):
        tile = pair << 1
        places.append(sum(((tile >> bit) & 1) << (steps - 1 - j) for j, bit in enumerate(order)))
    return tuple(places)


def per_device(groups, tiles, features, occupancy, link_weights, basis_cols):
    lat, lon, words = features.shape
    share = words // tiles
    bits = tiles.bit_length() - 1
    orders = bit_orders(bits)
    tile = lax.axis_index("tile")
    core = lax.rem(tile, 2)

    def exchange(values, partner):
        pairs = []
        for g in range(groups):
            for t in range(tiles):
                to_g, to_t = partner(g, t)
                if 0 <= to_g < groups and 0 <= to_t < tiles:
                    pairs.append((g * tiles + t, to_g * tiles + to_t))
        return lax.ppermute(values, AXES, pairs)

    masked, proj, row_a, row_b, *cols = project(occupancy, features, basis_cols, 1 if groups <= 2 else 2)
    halo_row_b = exchange(row_b, lambda g, t: (g, t - 1 + 2 * (t % 2)))
    halo_cols = [exchange(cols[0], lambda g, t: (g + 1 - 2 * (g % 2), t))]
    if groups > 2:
        halo_cols.append(exchange(cols[1], lambda g, t: (g - 1 + 2 * (g % 2), t)))
    halo_row_a = exchange(row_a, lambda g, t: (g, t ^ 1))
    send, held = partial_product(
        tuple(block_places(order) for order in orders),
        share, masked, proj, (halo_row_a, halo_row_b), halo_cols, link_weights,
    )
    got = exchange(send, lambda g, t: (g, t ^ 1))
    pick = functools.partial(lax.dynamic_index_in_dim, axis=0, keepdims=False)
    for j in range(bits - 1):
        bit = jnp.where(core == 0, orders[0][j], orders[1][j])
        mine = lax.rem(lax.shift_right_logical(tile, bit), 2)
        halves = (2, held.shape[0] // 2) + held.shape[1:]
        held, got = held.reshape(halves), got.reshape(halves)
        send = (pick(held, 1 - mine) + pick(got, 1 - mine).astype(F32)).astype(BF16)
        held = pick(held, mine) + pick(got, mine).astype(F32)
        got = exchange(send, lambda g, t: (g, t ^ (1 << orders[t % 2][j])))
    held, got = held[0], got[0]
    total = held + got.astype(F32)
    step = 1
    while step < groups:
        send = total.astype(BF16)
        got = exchange(send, lambda g, t: (g ^ step, t))
        total = send.astype(F32) + got.astype(F32)
        step *= 2
    return total * (1.0 / math.sqrt(lat * lon * groups * tiles))


def solution(mesh):
    groups, tiles = mesh.shape["grp"], mesh.shape["tile"]
    placed = (P("tile", "grp", None), P("tile", "grp", None), P(None, "tile", "grp"), P())
    return jax.shard_map(
        functools.partial(per_device, groups, tiles),
        mesh=mesh, in_specs=placed, out_specs=P("tile", None), check_vma=False,
    )
```

time: 176 us -> 37.4 us (0.21)
  waiting for transfers between devices: 145 us -> 15.8 us
  between operations: 13.5 us -> 0.05 us
  starting transfers between devices: 8.75 us -> 15.6 us
  Pallas kernels: 0 us -> 4.95 us
  matrix products: 4.18 us -> 0 us
    psum x1 -> x0, waiting for transfers between devices: 137 us -> none  [per_device(): summed = lax.psum(local_term, ('grp', 'tile'))]
    ppermute x4 -> x8, waiting for transfers between devices: 7.75 us -> 15.8 us  [exchange(): return lax.ppermute(values, AXES, pairs)]
    ppermute x4 -> x8, starting transfers between devices: 8.75 us -> 15.6 us  [exchange(): return lax.ppermute(values, AXES, pairs)]
    pallas_call x0 -> x2, Pallas kernels: none -> 4.95 us  [the longest x1 3.37 us: project(): pl.pallas_call(project_kernel, out_shape=(pltpu.VMEM((lat, lon, words), B...]
    dot_general x2 -> x0, matrix products: 4.18 us -> none  [the longest x1 3.16 us: per_device(): lax.dot_general(masked, smooth, (((0,), (0,)), ((), ())), preferred_eleme...]
  transfers between devices with their start and end apart: 5 -> 8, of which waited for: 4 -> 6; matrix products, arithmetic and copies ran while one was open for 0% -> 0% of each run, Pallas kernels for 0% -> 0%
where the time goes in v1:
time: 37.4 us; the launch traced here: 37.3 us
  waiting for transfers between devices  15.8 us (42%)
  starting transfers between devices  15.6 us (42%)
  Pallas kernels  4.95 us (13%)
  other arithmetic  0.88 us (2%)
    ppermute x8, waiting for transfers between devices, exchange(): return lax.ppermute(values, AXES, pairs)  15.8 us
    ppermute x8, starting transfers between devices, exchange(): return lax.ppermute(values, AXES, pairs)  15.6 us
    pallas_call x1, Pallas kernels, project(): pl.pallas_call(project_kernel, out_shape=(pltpu.VMEM((lat, lon, words), B...  3.37 us
    pallas_call x1, Pallas kernels, partial_product(): pl.pallas_call(functools.partial(partial_kernel, orders), out_shape=(pltp...  1.58 us
  transfers between devices with their start and end apart: 8, of which 6 were waited for; matrix products, arithmetic and copies ran while one was open for 0% of the time, Pallas kernels for 0%

profile of v1, /device:TPU:0, one launch (start us, length us, event | category | flops | bytes accessed | tf_op | source)
XLA Modules:
  0.0 37.3 jit_solution(6629807687114192545)
XLA Ops:
  0.0 0.0 copy-start
  0.0 3.4 %shard_map.46 = (bf16[24,32,2048]{2,1,0:T(8,128)(2,1)S(1)}, bf16[24,32,256]{2,1,0:T(8,128)(2,1)S(1)}, bf16[32,256]{1,0:T(8,128)(2,1)S(1)}, bf16[32,256]{1,0:T(8,128)(2,1)S(1)}, bf16[24,256]{1,0:T(8,128)(2,1)S(1)}) custom-call(s32[12,1,16]{2,1,0:T(1,128)} %occ_hbm.1, bf16[24,32,2048]{2,1,0:T(8,128)(2,1)} %feat_hbm.1, bf16[2048,256]{1,0:T(8,128)(2,1)} %basis_hbm.1), custom_call_target="tpu_custom_call" | custom-call | flops 805306368 | bytes 3145728 | tf_op jit(solution)/shard_map/pallas_call | solution.py:74
  3.4 0.6 %collective-permute-start = (bf16[32,256]{1,0:T(8,128)(2,1)S(1)}, bf16[32,256]{1,0:T(8,128)(2,1)S(1)}, u32[]{:S(2)}, u32[]{:S(2)}) collective-permute-start(bf16[32,256]{1,0:T(8,128)(2,1)S(1)} %get-tuple-element.14), channel_id=1, source_target_pairs={{0,1},{1,0},{2,3},{3,2},{4,5},{5,4},{6,7},{7,6},{8,9},{9,8},{10,11... | collective-permute-start | bytes 49160 | tf_op jit(solution)/shard_map/ppermute | solution.py:190
  3.9 0.7 %collective-permute-start.1 = (bf16[32,256]{1,0:T(8,128)(2,1)S(1)}, bf16[32,256]{1,0:T(8,128)(2,1)S(1)}, u32[]{:S(2)}, u32[]{:S(2)}) collective-permute-start(bf16[32,256]{1,0:T(8,128)(2,1)S(1)} %get-tuple-element.15), channel_id=1, source_target_pairs={{1,2},{2,1},{3,4},{4,3},{5,6},{6,5},{7,8},{8,7},{9,10},{10,9},{11,... | collective-permute-start | bytes 49160 | tf_op jit(solution)/shard_map/ppermute | solution.py:190
  4.6 2.6 %collective-permute-start.2 = (bf16[24,256]{1,0:T(8,128)(2,1)S(1)}, bf16[24,256]{1,0:T(8,128)(2,1)S(1)}, u32[]{:S(2)}, u32[]{:S(2)}) collective-permute-start(bf16[24,256]{1,0:T(8,128)(2,1)S(1)} %get-tuple-element.16), channel_id=1, source_target_pairs={{0,16},{1,17},{2,18},{3,19},{4,20},{5,21},{6,22},{7,23},{8,24},{9,... | collective-permute-start | bytes 36872 | tf_op jit(solution)/shard_map/ppermute | solution.py:190
  7.2 1.7 %collective-permute-done.2.rest_0_ = bf16[24,256]{1,0:T(8,128)(2,1)S(1)} collective-permute-done((bf16[24,256]{1,0:T(8,128)(2,1)S(1)}, bf16[24,256]{1,0:T(8,128)(2,1)S(1)}, u32[]{:S(2)}, u32[]{:S(2)}) %collective-permute-start.2) | collective-permute-done | bytes 12320 | tf_op jit(solution)/shard_map/ppermute | solution.py:190
  8.8 0.0 collective-permute-done.halo_row_a
  8.8 0.0 collective-permute-done.1.halo_row_b
  8.8 0.0 copy-done
  8.9 1.6 %shard_map.47 = (bf16[8,128,256]{2,1,0:T(8,128)(2,1)S(1)}, f32[8,128,256]{2,1,0:T(8,128)S(1)}) custom-call(bf16[24,32,2048]{2,1,0:T(8,128)(2,1)S(1)} %get-tuple-element.12.masked, bf16[24,32,256]{2,1,0:T(8,128)(2,1)S(1)} %get-tuple-element.13.proj, bf16[32,256]{1,0:T(8,128)(2,1)S(1)} %collective-permute-done.halo_row_a, ...), custom_call_target="tpu_custom_call" | custom-call | flops 805306368 | bytes 3145728 | tf_op jit(solution)/shard_map/pallas_call | solution.py:147
  10.4 2.3 %collective-permute-start.3 = (bf16[8,128,256]{2,1,0:T(8,128)(2,1)S(1)}, bf16[8,128,256]{2,1,0:T(8,128)(2,1)S(1)}, u32[]{:S(2)}, u32[]{:S(2)}) collective-permute-start(bf16[8,128,256]{2,1,0:T(8,128)(2,1)S(1)} %get-tuple-element.18), channel_id=1, source_target_pairs={{0,1},{1,0},{2,3},{3,2},{4,5},{5,4},{6,7},{7,6},{8,9},{9,8},{10,11... | collective-permute-start | bytes 1572872 | tf_op jit(solution)/shard_map/ppermute | solution.py:190
  12.8 1.5 %collective-permute-done.3 = bf16[8,128,256]{2,1,0:T(8,128)(2,1)S(1)} collective-permute-done((bf16[8,128,256]{2,1,0:T(8,128)(2,1)S(1)}, bf16[8,128,256]{2,1,0:T(8,128)(2,1)S(1)}, u32[]{:S(2)}, u32[]{:S(2)}) %collective-permute-start.3) | collective-permute-done | bytes 524320 | tf_op jit(solution)/shard_map/ppermute | solution.py:190
  14.3 0.1 fusion
  14.4 1.9 %collective-permute-start.4 = (bf16[4,128,256]{2,1,0:T(8,128)(2,1)S(1)}, bf16[4,128,256]{2,1,0:T(8,128)(2,1)S(1)}, u32[]{:S(2)}, u32[]{:S(2)}) collective-permute-start(bf16[4,128,256]{2,1,0:T(8,128)(2,1)S(1)} %get-tuple-element.19), channel_id=1, source_target_pairs={{0,2},{1,5},{2,0},{3,7},{4,6},{5,1},{6,4},{7,3},{8,10},{9,13},{10,... | collective-permute-start | bytes 786440 | tf_op jit(solution)/shard_map/ppermute | solution.py:190
  16.3 4.6 %collective-permute-done.4 = bf16[4,128,256]{2,1,0:T(8,128)(2,1)S(1)} collective-permute-done((bf16[4,128,256]{2,1,0:T(8,128)(2,1)S(1)}, bf16[4,128,256]{2,1,0:T(8,128)(2,1)S(1)}, u32[]{:S(2)}, u32[]{:S(2)}) %collective-permute-start.4) | collective-permute-done | bytes 262176 | tf_op jit(solution)/shard_map/ppermute | solution.py:190
  20.9 0.1 fusion.1
  20.9 3.0 %collective-permute-start.5 = (bf16[2,128,256]{2,1,0:T(8,128)(2,1)S(1)}, bf16[2,128,256]{2,1,0:T(8,128)(2,1)S(1)}, u32[]{:S(2)}, u32[]{:S(2)}) collective-permute-start(bf16[2,128,256]{2,1,0:T(8,128)(2,1)S(1)} %get-tuple-element.21), channel_id=1, source_target_pairs={{0,4},{1,3},{2,6},{3,1},{4,0},{5,7},{6,2},{7,5},{8,12},{9,11},{10,... | collective-permute-start | bytes 393224 | tf_op jit(solution)/shard_map/ppermute | solution.py:190
  23.9 2.9 %collective-permute-done.5 = bf16[2,128,256]{2,1,0:T(8,128)(2,1)S(1)} collective-permute-done((bf16[2,128,256]{2,1,0:T(8,128)(2,1)S(1)}, bf16[2,128,256]{2,1,0:T(8,128)(2,1)S(1)}, u32[]{:S(2)}, u32[]{:S(2)}) %collective-permute-start.5) | collective-permute-done | bytes 131104 | tf_op jit(solution)/shard_map/ppermute | solution.py:190
  26.9 3.1 %collective-permute-start.6 = (bf16[1,128,256]{2,1,0:T(8,128)(2,1)S(1)}, bf16[1,128,256]{2,1,0:T(8,128)(2,1)S(1)}, u32[]{:S(2)}, u32[]{:S(2)}) collective-permute-start(bf16[1,128,256]{2,1,0:T(8,128)(2,1)S(1)} %fusion.2), channel_id=1, source_target_pairs={{0,8},{1,9},{2,10},{3,11},{4,12},{5,13},{6,14},{7,15},{8,0},{9,1},... | collective-permute-start | bytes 196616 | tf_op jit(solution)/shard_map/ppermute | solution.py:190
  30.0 2.2 %collective-permute-done.6 = bf16[1,128,256]{2,1,0:T(8,128)(2,1)S(1)} collective-permute-done((bf16[1,128,256]{2,1,0:T(8,128)(2,1)S(1)}, bf16[1,128,256]{2,1,0:T(8,128)(2,1)S(1)}, u32[]{:S(2)}, u32[]{:S(2)}) %collective-permute-start.6) | collective-permute-done | bytes 65568 | tf_op jit(solution)/shard_map/ppermute | solution.py:190
  32.3 1.6 %collective-permute-start.7 = (bf16[128,256]{1,0:T(8,128)(2,1)S(1)}, bf16[128,256]{1,0:T(8,128)(2,1)S(1)}, u32[]{:S(2)}, u32[]{:S(2)}) collective-permute-start(bf16[128,256]{1,0:T(8,128)(2,1)S(1)} %fusion.5), channel_id=1, source_target_pairs={{0,16},{1,17},{2,18},{3,19},{4,20},{5,21},{6,22},{7,23},{8,24},{9,... | collective-permute-start | bytes 196616 | tf_op jit(solution)/shard_map/ppermute | solution.py:190
  33.8 2.8 %collective-permute-done.7 = bf16[128,256]{1,0:T(8,128)(2,1)S(1)} collective-permute-done((bf16[128,256]{1,0:T(8,128)(2,1)S(1)}, bf16[128,256]{1,0:T(8,128)(2,1)S(1)}, u32[]{:S(2)}, u32[]{:S(2)}) %collective-permute-start.7) | collective-permute-done | bytes 65568 | tf_op jit(solution)/shard_map/ppermute | solution.py:190
  36.6 0.7 %add_multiply_fusion = f32[128,256]{1,0:T(8,128)} fusion(bf16[128,256]{1,0:T(8,128)(2,1)S(1)} %collective-permute-done.7, bf16[128,256]{1,0:T(8,128)(2,1)S(1)} %fusion.5), kind=kLoop, calls=%fused_computation.11 | loop fusion | flops 131072 | bytes 262144 | tf_op jit(solution)/shard_map/mul | solution.py:220
  (2 shorter events, 0.0 us)
Async XLA Ops:
  0.0 8.8 %copy-start = (s32[4,24,32]{2,1,0:T(8,128)S(1)}, s32[4,24,32]{2,1,0:T(8,128)}, u32[]{:S(2)}) copy-start(s32[4,24,32]{2,1,0:T(8,128)} %rest_1_.1) | copy-start | bytes 36868
  3.4 5.5 %collective-permute-start = (bf16[32,256]{1,0:T(8,128)(2,1)S(1)}, bf16[32,256]{1,0:T(8,128)(2,1)S(1)}, u32[]{:S(2)}, u32[]{:S(2)}) collective-permute-start(bf16[32,256]{1,0:T(8,128)(2,1)S(1)} %get-tuple-element.14), channel_id=1, source_target_pairs={{0,1},{1,0},{2,3},{3,2},{4,5},{5,4},{6,7},{7,6},{8,9},{9,8},{10,11... | collective-permute-start | bytes 49160 | tf_op jit(solution)/shard_map/ppermute | solution.py:190
  3.9 4.9 %collective-permute-start.1 = (bf16[32,256]{1,0:T(8,128)(2,1)S(1)}, bf16[32,256]{1,0:T(8,128)(2,1)S(1)}, u32[]{:S(2)}, u32[]{:S(2)}) collective-permute-start(bf16[32,256]{1,0:T(8,128)(2,1)S(1)} %get-tuple-element.15), channel_id=1, source_target_pairs={{1,2},{2,1},{3,4},{4,3},{5,6},{6,5},{7,8},{8,7},{9,10},{10,9},{11,... | collective-permute-start | bytes 49160 | tf_op jit(solution)/shard_map/ppermute | solution.py:190
  4.6 4.2 %collective-permute-start.2 = (bf16[24,256]{1,0:T(8,128)(2,1)S(1)}, bf16[24,256]{1,0:T(8,128)(2,1)S(1)}, u32[]{:S(2)}, u32[]{:S(2)}) collective-permute-start(bf16[24,256]{1,0:T(8,128)(2,1)S(1)} %get-tuple-element.16), channel_id=1, source_target_pairs={{0,16},{1,17},{2,18},{3,19},{4,20},{5,21},{6,22},{7,23},{8,24},{9,... | collective-permute-start | bytes 36872 | tf_op jit(solution)/shard_map/ppermute | solution.py:190
  10.4 3.9 %collective-permute-start.3 = (bf16[8,128,256]{2,1,0:T(8,128)(2,1)S(1)}, bf16[8,128,256]{2,1,0:T(8,128)(2,1)S(1)}, u32[]{:S(2)}, u32[]{:S(2)}) collective-permute-start(bf16[8,128,256]{2,1,0:T(8,128)(2,1)S(1)} %get-tuple-element.18), channel_id=1, source_target_pairs={{0,1},{1,0},{2,3},{3,2},{4,5},{5,4},{6,7},{7,6},{8,9},{9,8},{10,11... | collective-permute-start | bytes 1572872 | tf_op jit(solution)/shard_map/ppermute | solution.py:190
  14.4 6.4 %collective-permute-start.4 = (bf16[4,128,256]{2,1,0:T(8,128)(2,1)S(1)}, bf16[4,128,256]{2,1,0:T(8,128)(2,1)S(1)}, u32[]{:S(2)}, u32[]{:S(2)}) collective-permute-start(bf16[4,128,256]{2,1,0:T(8,128)(2,1)S(1)} %get-tuple-element.19), channel_id=1, source_target_pairs={{0,2},{1,5},{2,0},{3,7},{4,6},{5,1},{6,4},{7,3},{8,10},{9,13},{10,... | collective-permute-start | bytes 786440 | tf_op jit(solution)/shard_map/ppermute | solution.py:190
  20.9 6.0 %collective-permute-start.5 = (bf16[2,128,256]{2,1,0:T(8,128)(2,1)S(1)}, bf16[2,128,256]{2,1,0:T(8,128)(2,1)S(1)}, u32[]{:S(2)}, u32[]{:S(2)}) collective-permute-start(bf16[2,128,256]{2,1,0:T(8,128)(2,1)S(1)} %get-tuple-element.21), channel_id=1, source_target_pairs={{0,4},{1,3},{2,6},{3,1},{4,0},{5,7},{6,2},{7,5},{8,12},{9,11},{10,... | collective-permute-start | bytes 393224 | tf_op jit(solution)/shard_map/ppermute | solution.py:190
  26.9 5.3 %collective-permute-start.6 = (bf16[1,128,256]{2,1,0:T(8,128)(2,1)S(1)}, bf16[1,128,256]{2,1,0:T(8,128)(2,1)S(1)}, u32[]{:S(2)}, u32[]{:S(2)}) collective-permute-start(bf16[1,128,256]{2,1,0:T(8,128)(2,1)S(1)} %fusion.2), channel_id=1, source_target_pairs={{0,8},{1,9},{2,10},{3,11},{4,12},{5,13},{6,14},{7,15},{8,0},{9,1},... | collective-permute-start | bytes 196616 | tf_op jit(solution)/shard_map/ppermute | solution.py:190
  32.3 4.3 %collective-permute-start.7 = (bf16[128,256]{1,0:T(8,128)(2,1)S(1)}, bf16[128,256]{1,0:T(8,128)(2,1)S(1)}, u32[]{:S(2)}, u32[]{:S(2)}) collective-permute-start(bf16[128,256]{1,0:T(8,128)(2,1)S(1)} %fusion.5), channel_id=1, source_target_pairs={{0,16},{1,17},{2,18},{3,19},{4,20},{5,21},{6,22},{7,23},{8,24},{9,... | collective-permute-start | bytes 196616 | tf_op jit(solution)/shard_map/ppermute | solution.py:190

commit v2 on v1

--- a/solution.py
+++ b/solution.py
@@ -15,6 +15,7 @@
 IN_VMEM = pl.BlockSpec(memory_space=pltpu.VMEM)
 KERNEL_VMEM = 24 << 20
 WORD_CHUNK = 512
+CHUNKS = 2
 
 
 def project_kernel(occ_hbm, feat_hbm, basis_hbm, masked, proj, *rest):
@@ -111,11 +112,60 @@
         smooth[pl.ds(i * lon, lon), :] = value.astype(BF16)
 
 
+def block_of(order, half, slot):
+    steps = len(order)
+    tile = sum(((slot >> (steps - 1 - j)) & 1) << bit for j, bit in enumerate(order))
+    return tile + (half ^ (bin(tile).count("1") & 1))
+
+
+def half_blocks(orders, sent, masked, values, outs):
+    lat, lon, words = masked.shape
+    slots, rows = outs[0].shape[:2]
+    share = rows * len(outs)
+    half = tile_parity() ^ sent
+    contract = (((0,), (0,)), ((), ()))
+
+    def put(slot, term):
+        for k, out in enumerate(outs):
+            out[slot] = term[k * rows:(k + 1) * rows].astype(out.dtype)
+
+    if share % 128 == 0:
+        count = max(1, 256 // share)
+        for slot in range(0, slots, count):
+            parts = []
+            for at in range(slot, slot + count):
+                first = jnp.where(half == 0, block_of(orders[0], 0, at), block_of(orders[1], 1, at)) * share
+                part = masked[:, :, pl.ds(pl.multiple_of(first, share), share)]
+                parts.append(part.reshape(lat * lon, share))
+            part = jnp.concatenate(parts, axis=1) if count > 1 else parts[0]
+            term = lax.dot_general(part, values, contract, preferred_element_type=F32)
+            for at in range(count):
+                put(slot + at, term[at * share:(at + 1) * share])
+        return
+    slot_of = [{block_of(order, h, at) // 2: at for at in range(slots)} for h, order in enumerate(orders)]
+    step = 256
+    for first in range(0, words, step):
+        part = masked[:, :, pl.ds(first, step)].reshape(lat * lon, step)
+        term = lax.dot_general(part, values, contract, preferred_element_type=F32)
+        for at in range(0, step, 2 * share):
+            pair = (first + at) // (2 * share)
+            odd = bin(pair).count("1") & 1
+            low, high = term[at:at + share], term[at + share:at + 2 * share]
+            put(jnp.where(half == 0, slot_of[0][pair], slot_of[1][pair]), jnp.where(half == odd, low, high))
+
+
+def tile_parity():
+    tile = lax.axis_index("tile")
+    parity = lax.rem(tile, 2)
+    for bit in range(1, (lax.axis_size("tile") - 1).bit_length()):
+        parity = parity ^ lax.rem(lax.shift_right_logical(tile, bit), 2)
+    return parity
+
+
 def partial_kernel(orders, masked, proj, halo_row_a, halo_row_b, *rest):
-    *halo_cols, links, send, keep, smooth = rest
-    lat, lon, words = masked.shape
-    rank = proj.shape[2]
-    pairs, share = send.shape[:2]
+    *rest, smooth = rest
+    rest, sends, keeps = rest[:-2 * CHUNKS], rest[-2 * CHUNKS:-CHUNKS], rest[-CHUNKS:]
+    *halo_cols, links = rest
     row_a, row_b = halo_row_a[...].astype(F32), halo_row_b[...].astype(F32)
     odd = lax.rem(lax.axis_index("tile"), 2)
     north = jnp.where(odd == 0, row_b, row_a)
@@ -127,49 +177,32 @@
     east = jnp.where(even, col_a, col_b)
     smooth_rows(proj, north, south, west, east, links, smooth)
     values = smooth[...]
-    step = 256
-    for first in range(0, words, step):
-        part = masked[:, :, pl.ds(first, step)].reshape(lat * lon, step)
-        term = lax.dot_general(part, values, (((0,), (0,)), ((), ())), preferred_element_type=F32)
-        for at in range(0, step, 2 * share):
-            pair = (first + at) // (2 * share)
-            here = jnp.where(odd == 0, orders[0][pair], orders[1][pair])
-            there = jnp.where(odd == 0, orders[1][pair], orders[0][pair])
-            low, high = term[at:at + share], term[at + share:at + 2 * share]
-            send[there] = jnp.where(odd == 0, high, low).astype(BF16)
-            keep[here] = jnp.where(odd == 0, low, high)
+    half_blocks(orders, 1, masked, values, sends)
+    half_blocks(orders, 0, masked, values, keeps)
 
 
 def partial_product(orders, share, masked, proj, rows, cols, link_weights):
     lat, lon, words = masked.shape
     rank = proj.shape[2]
-    pairs = words // share // 2
-    return pl.pallas_call(
+    shape = (words // share // 2, share // CHUNKS, rank)
+    outs = pl.pallas_call(
         functools.partial(partial_kernel, orders),
-        out_shape=(pltpu.VMEM((pairs, share, rank), BF16), pltpu.VMEM((pairs, share, rank), F32)),
+        out_shape=(pltpu.VMEM(shape, BF16),) * CHUNKS + (pltpu.VMEM(shape, F32),) * CHUNKS,
         in_specs=[IN_VMEM] * (5 + len(cols)),
-        out_specs=(IN_VMEM,) * 2,
+        out_specs=(IN_VMEM,) * (2 * CHUNKS),
         scratch_shapes=[pltpu.VMEM((lat * lon, rank), BF16)],
         compiler_params=pltpu.CompilerParams(vmem_limit_bytes=KERNEL_VMEM),
         cost_estimate=pl.CostEstimate(
             flops=2 * lat * lon * words * rank, bytes_accessed=2 * lat * lon * words, transcendentals=0
         ),
     )(masked, proj, *rows, *cols, link_weights)
+    return outs[:CHUNKS], outs[CHUNKS:]
 
 
 def bit_orders(bits):
     plain = list(range(1, bits))
     turned = plain[1::-1] + plain[2:]
     return plain, turned
-
-
-def block_places(order):
-    steps = len(order)
-    places = []
-    for pair in range(1 << steps):
-        tile = pair << 1
-        places.append(sum(((tile >> bit) & 1) << (steps - 1 - j) for j, bit in enumerate(order)))
-    return tuple(places)
 
 
 def per_device(groups, tiles, features, occupancy, link_weights, basis_cols):
@@ -178,7 +211,6 @@
     bits = tiles.bit_length() - 1
     orders = bit_orders(bits)
     tile = lax.axis_index("tile")
-    core = lax.rem(tile, 2)
 
     def exchange(values, partner):
         pairs = []
@@ -195,29 +227,32 @@
     if groups > 2:
         halo_cols.append(exchange(cols[1], lambda g, t: (g - 1 + 2 * (g % 2), t)))
     halo_row_a = exchange(row_a, lambda g, t: (g, t ^ 1))
-    send, held = partial_product(
-        tuple(block_places(order) for order in orders),
-        share, masked, proj, (halo_row_a, halo_row_b), halo_cols, link_weights,
+    sends, keeps = partial_product(
+        orders, share, masked, proj, (halo_row_a, halo_row_b), halo_cols, link_weights
     )
-    got = exchange(send, lambda g, t: (g, t ^ 1))
+    parity = tile_parity()
     pick = functools.partial(lax.dynamic_index_in_dim, axis=0, keepdims=False)
-    for j in range(bits - 1):
-        bit = jnp.where(core == 0, orders[0][j], orders[1][j])
-        mine = lax.rem(lax.shift_right_logical(tile, bit), 2)
-        halves = (2, held.shape[0] // 2) + held.shape[1:]
-        held, got = held.reshape(halves), got.reshape(halves)
-        send = (pick(held, 1 - mine) + pick(got, 1 - mine).astype(F32)).astype(BF16)
-        held = pick(held, mine) + pick(got, mine).astype(F32)
-        got = exchange(send, lambda g, t: (g, t ^ (1 << orders[t % 2][j])))
-    held, got = held[0], got[0]
-    total = held + got.astype(F32)
-    step = 1
-    while step < groups:
-        send = total.astype(BF16)
-        got = exchange(send, lambda g, t: (g ^ step, t))
-        total = send.astype(F32) + got.astype(F32)
-        step *= 2
-    return total * (1.0 / math.sqrt(lat * lon * groups * tiles))
+
+    def reduced(held, send):
+        got = exchange(send, lambda g, t: (g, t ^ 1))
+        for j in range(bits - 1):
+            bit = jnp.where(parity == 0, orders[0][j], orders[1][j])
+            mine = lax.rem(lax.shift_right_logical(tile, bit), 2)
+            halves = (2, held.shape[0] // 2) + held.shape[1:]
+            held, got = held.reshape(halves), got.reshape(halves)
+            send = (pick(held, 1 - mine) + pick(got, 1 - mine).astype(F32)).astype(BF16)
+            held = pick(held, mine) + pick(got, mine).astype(F32)
+            got = exchange(send, lambda g, t: (g, t ^ (1 << orders[bin(t).count("1") & 1][j]) ^ 1))
+        total = held[0] + got[0].astype(F32)
+        step = 1
+        while step < groups:
+            send = total.astype(BF16)
+            got = exchange(send, lambda g, t: (g ^ step, t))
+            total = send.astype(F32) + got.astype(F32)
+            step *= 2
+        return total * (1.0 / math.sqrt(lat * lon * groups * tiles))
+
+    return jnp.concatenate([reduced(held, send) for held, send in zip(keeps, sends)], axis=0)
 
 
 def solution(mesh):

time: 37.4 us -> 35.6 us (0.952)
  waiting for transfers between devices: 15.8 us -> 9.77 us
  starting transfers between devices: 15.6 us -> 19.7 us
    ppermute x8 -> x13, waiting for transfers between devices: 15.8 us -> 9.77 us  [exchange(): return lax.ppermute(values, AXES, pairs)]
    ppermute x8 -> x13, starting transfers between devices: 15.6 us -> 19.7 us  [exchange(): return lax.ppermute(values, AXES, pairs)]
    concatenate x0 -> x1, other arithmetic: none -> 0.67 us  [per_device(): jnp.concatenate([reduced(held, send) for held, send in zip(keeps, sends)]...]
    mul x1 -> x2, other arithmetic: 0.68 us -> 0.02 us  [reduced(): return total * (1.0 / math.sqrt(lat * lon * groups * tiles))]
  transfers between devices with their start and end apart: 8 -> 13, of which waited for: 6 -> 7; matrix products, arithmetic and copies ran while one was open for 0% -> 1% of each run, Pallas kernels for 0% -> 0%
where the time goes in v2:
time: 35.6 us; the launch traced here: 35.5 us
  starting transfers between devices  19.7 us (55%)
  waiting for transfers between devices  9.77 us (27%)
  Pallas kernels  5.02 us (14%)
  other arithmetic  0.89 us (2%)
    ppermute x13, starting transfers between devices, exchange(): return lax.ppermute(values, AXES, pairs)  19.7 us
    ppermute x13, waiting for transfers between devices, exchange(): return lax.ppermute(values, AXES, pairs)  9.77 us
    pallas_call x1, Pallas kernels, project(): pl.pallas_call(project_kernel, out_shape=(pltpu.VMEM((lat, lon, words), B...  3.37 us
    pallas_call x1, Pallas kernels, partial_product(): pl.pallas_call(functools.partial(partial_kernel, orders), out_shape=(pltp...  1.64 us
  transfers between devices with their start and end apart: 13, of which 7 were waited for; matrix products, arithmetic and copies ran while one was open for 1% of the time, Pallas kernels for 0%

profile of v2, /device:TPU:0, one launch (start us, length us, event | category | flops | bytes accessed | tf_op | source)
XLA Modules:
  0.0 35.5 jit_solution(15135949695040245744)
XLA Ops:
  0.0 0.0 copy-start
  0.0 3.4 %shard_map.46 = (bf16[24,32,2048]{2,1,0:T(8,128)(2,1)S(1)}, bf16[24,32,256]{2,1,0:T(8,128)(2,1)S(1)}, bf16[32,256]{1,0:T(8,128)(2,1)S(1)}, bf16[32,256]{1,0:T(8,128)(2,1)S(1)}, bf16[24,256]{1,0:T(8,128)(2,1)S(1)}) custom-call(s32[12,1,16]{2,1,0:T(1,128)} %occ_hbm.1, bf16[24,32,2048]{2,1,0:T(8,128)(2,1)} %feat_hbm.1, bf16[2048,256]{1,0:T(8,128)(2,1)} %basis_hbm.1), custom_call_target="tpu_custom_call" | custom-call | flops 805306368 | bytes 3145728 | tf_op jit(solution)/shard_map/pallas_call | solution.py:75
  3.4 0.6 %collective-permute-start = (bf16[32,256]{1,0:T(8,128)(2,1)S(1)}, bf16[32,256]{1,0:T(8,128)(2,1)S(1)}, u32[]{:S(2)}, u32[]{:S(2)}) collective-permute-start(bf16[32,256]{1,0:T(8,128)(2,1)S(1)} %get-tuple-element.16), channel_id=1, source_target_pairs={{0,1},{1,0},{2,3},{3,2},{4,5},{5,4},{6,7},{7,6},{8,9},{9,8},{10,11... | collective-permute-start | bytes 49160 | tf_op jit(solution)/shard_map/ppermute | solution.py:222
  3.9 0.7 %collective-permute-start.1 = (bf16[32,256]{1,0:T(8,128)(2,1)S(1)}, bf16[32,256]{1,0:T(8,128)(2,1)S(1)}, u32[]{:S(2)}, u32[]{:S(2)}) collective-permute-start(bf16[32,256]{1,0:T(8,128)(2,1)S(1)} %get-tuple-element.17), channel_id=1, source_target_pairs={{1,2},{2,1},{3,4},{4,3},{5,6},{6,5},{7,8},{8,7},{9,10},{10,9},{11,... | collective-permute-start | bytes 49160 | tf_op jit(solution)/shard_map/ppermute | solution.py:222
  4.6 2.6 %collective-permute-start.2 = (bf16[24,256]{1,0:T(8,128)(2,1)S(1)}, bf16[24,256]{1,0:T(8,128)(2,1)S(1)}, u32[]{:S(2)}, u32[]{:S(2)}) collective-permute-start(bf16[24,256]{1,0:T(8,128)(2,1)S(1)} %get-tuple-element.18), channel_id=1, source_target_pairs={{0,16},{1,17},{2,18},{3,19},{4,20},{5,21},{6,22},{7,23},{8,24},{9,... | collective-permute-start | bytes 36872 | tf_op jit(solution)/shard_map/ppermute | solution.py:222
  7.2 1.7 %collective-permute-done.2.rest_0_ = bf16[24,256]{1,0:T(8,128)(2,1)S(1)} collective-permute-done((bf16[24,256]{1,0:T(8,128)(2,1)S(1)}, bf16[24,256]{1,0:T(8,128)(2,1)S(1)}, u32[]{:S(2)}, u32[]{:S(2)}) %collective-permute-start.2) | collective-permute-done | bytes 12320 | tf_op jit(solution)/shard_map/ppermute | solution.py:222
  8.8 0.0 collective-permute-done.halo_row_a
  8.8 0.0 collective-permute-done.1.halo_row_b
  8.8 0.0 copy-done
  8.9 1.6 %shard_map.47 = (bf16[8,64,256]{2,1,0:T(8,128)(2,1)S(1)}, bf16[8,64,256]{2,1,0:T(8,128)(2,1)S(1)}, f32[8,64,256]{2,1,0:T(8,128)S(1)}, f32[8,64,256]{2,1,0:T(8,128)S(1)}) custom-call(bf16[24,32,2048]{2,1,0:T(8,128)(2,1)S(1)} %get-tuple-element.14.masked, bf16[24,32,256]{2,1,0:T(8,128)(2,1)S(1)} %get-tuple-element.15.proj, ...), custom_call_target="tpu_custom_call" | custom-call | flops 805306368 | bytes 3145728 | tf_op jit(solution)/shard_map/pallas_call | solution.py:188
  10.5 2.3 %collective-permute-start.8 = (bf16[8,64,256]{2,1,0:T(8,128)(2,1)S(1)}, bf16[8,64,256]{2,1,0:T(8,128)(2,1)S(1)}, u32[]{:S(2)}, u32[]{:S(2)}) collective-permute-start(bf16[8,64,256]{2,1,0:T(8,128)(2,1)S(1)} %get-tuple-element.22), channel_id=1, source_target_pairs={{0,1},{1,0},{2,3},{3,2},{4,5},{5,4},{6,7},{7,6},{8,9},{9,8},{10,11... | collective-permute-start | bytes 786440 | tf_op jit(solution)/shard_map/ppermute | solution.py:222
  12.8 0.1 collective-permute-start.3
  12.9 1.1 %collective-permute-done.8 = bf16[8,64,256]{2,1,0:T(8,128)(2,1)S(1)} collective-permute-done((bf16[8,64,256]{2,1,0:T(8,128)(2,1)S(1)}, bf16[8,64,256]{2,1,0:T(8,128)(2,1)S(1)}, u32[]{:S(2)}, u32[]{:S(2)}) %collective-permute-start.8) | collective-permute-done | bytes 262176 | tf_op jit(solution)/shard_map/ppermute | solution.py:222
  14.0 0.1 fusion.1
  14.1 1.8 %collective-permute-start.9 = (bf16[4,64,256]{2,1,0:T(8,128)(2,1)S(1)}, bf16[4,64,256]{2,1,0:T(8,128)(2,1)S(1)}, u32[]{:S(2)}, u32[]{:S(2)}) collective-permute-start(bf16[4,64,256]{2,1,0:T(8,128)(2,1)S(1)} %get-tuple-element.25), channel_id=1, source_target_pairs={{0,3},{1,4},{2,7},{3,0},{4,1},{5,6},{6,5},{7,2},{8,13},{9,10},{10,... | collective-permute-start | bytes 393224 | tf_op jit(solution)/shard_map/ppermute | solution.py:222
  15.9 0.0 collective-permute-done.3
  15.9 0.1 fusion
  15.9 0.3 collective-permute-start.4
  16.3 2.3 %collective-permute-done.9 = bf16[4,64,256]{2,1,0:T(8,128)(2,1)S(1)} collective-permute-done((bf16[4,64,256]{2,1,0:T(8,128)(2,1)S(1)}, bf16[4,64,256]{2,1,0:T(8,128)(2,1)S(1)}, u32[]{:S(2)}, u32[]{:S(2)}) %collective-permute-start.9) | collective-permute-done | bytes 131104 | tf_op jit(solution)/shard_map/ppermute | solution.py:222
  18.6 3.0 %collective-permute-start.10 = (bf16[2,64,256]{2,1,0:T(8,128)(2,1)S(1)}, bf16[2,64,256]{2,1,0:T(8,128)(2,1)S(1)}, u32[]{:S(2)}, u32[]{:S(2)}) collective-permute-start(bf16[2,64,256]{2,1,0:T(8,128)(2,1)S(1)} %get-tuple-element.29), channel_id=1, source_target_pairs={{0,5},{1,2},{2,1},{3,6},{4,7},{5,0},{6,3},{7,4},{8,11},{9,12},{10,... | collective-permute-start | bytes 196616 | tf_op jit(solution)/shard_map/ppermute | solution.py:222
  21.6 0.0 collective-permute-done.4
  21.6 1.1 %collective-permute-start.5 = (bf16[2,64,256]{2,1,0:T(8,128)(2,1)S(1)}, bf16[2,64,256]{2,1,0:T(8,128)(2,1)S(1)}, u32[]{:S(2)}, u32[]{:S(2)}) collective-permute-start(bf16[2,64,256]{2,1,0:T(8,128)(2,1)S(1)} %get-tuple-element.27), channel_id=1, source_target_pairs={{0,5},{1,2},{2,1},{3,6},{4,7},{5,0},{6,3},{7,4},{8,11},{9,12},{10,... | collective-permute-start | bytes 196616 | tf_op jit(solution)/shard_map/ppermute | solution.py:222
  22.7 0.8 %collective-permute-done.10 = bf16[2,64,256]{2,1,0:T(8,128)(2,1)S(1)} collective-permute-done((bf16[2,64,256]{2,1,0:T(8,128)(2,1)S(1)}, bf16[2,64,256]{2,1,0:T(8,128)(2,1)S(1)}, u32[]{:S(2)}, u32[]{:S(2)}) %collective-permute-start.10) | collective-permute-done | bytes 65568 | tf_op jit(solution)/shard_map/ppermute | solution.py:222
  23.6 2.8 %collective-permute-start.11 = (bf16[1,64,256]{2,1,0:T(8,128)(2,1)S(1)}, bf16[1,64,256]{2,1,0:T(8,128)(2,1)S(1)}, u32[]{:S(2)}, u32[]{:S(2)}) collective-permute-start(bf16[1,64,256]{2,1,0:T(8,128)(2,1)S(1)} %fusion.4), channel_id=1, source_target_pairs={{0,9},{1,8},{2,11},{3,10},{4,13},{5,12},{6,15},{7,14},{8,1},{9,0},... | collective-permute-start | bytes 98312 | tf_op jit(solution)/shard_map/ppermute | solution.py:222
  26.4 0.0 collective-permute-done.5
  26.4 1.3 %collective-permute-start.6 = (bf16[1,64,256]{2,1,0:T(8,128)(2,1)S(1)}, bf16[1,64,256]{2,1,0:T(8,128)(2,1)S(1)}, u32[]{:S(2)}, u32[]{:S(2)}) collective-permute-start(bf16[1,64,256]{2,1,0:T(8,128)(2,1)S(1)} %fusion.7), channel_id=1, source_target_pairs={{0,9},{1,8},{2,11},{3,10},{4,13},{5,12},{6,15},{7,14},{8,1},{9,0},... | collective-permute-start | bytes 98312 | tf_op jit(solution)/shard_map/ppermute | solution.py:222
  27.7 0.2 collective-permute-done.11
  28.0 1.6 %collective-permute-start.12 = (bf16[64,256]{1,0:T(8,128)(2,1)S(1)}, bf16[64,256]{1,0:T(8,128)(2,1)S(1)}, u32[]{:S(2)}, u32[]{:S(2)}) collective-permute-start(bf16[64,256]{1,0:T(8,128)(2,1)S(1)} %fusion.11), channel_id=1, source_target_pairs={{0,16},{1,17},{2,18},{3,19},{4,20},{5,21},{6,22},{7,23},{8,24},{9,... | collective-permute-start | bytes 98312 | tf_op jit(solution)/shard_map/ppermute | solution.py:222
  29.6 1.2 %collective-permute-done.6 = bf16[1,64,256]{2,1,0:T(8,128)(2,1)S(1)} collective-permute-done((bf16[1,64,256]{2,1,0:T(8,128)(2,1)S(1)}, bf16[1,64,256]{2,1,0:T(8,128)(2,1)S(1)}, u32[]{:S(2)}, u32[]{:S(2)}) %collective-permute-start.6) | collective-permute-done | bytes 32800 | tf_op jit(solution)/shard_map/ppermute | solution.py:222
  30.8 1.6 %collective-permute-start.7 = (bf16[64,256]{1,0:T(8,128)(2,1)S(1)}, bf16[64,256]{1,0:T(8,128)(2,1)S(1)}, u32[]{:S(2)}, u32[]{:S(2)}) collective-permute-start(bf16[64,256]{1,0:T(8,128)(2,1)S(1)} %fusion.10), channel_id=1, source_target_pairs={{0,16},{1,17},{2,18},{3,19},{4,20},{5,21},{6,22},{7,23},{8,24},{9,... | collective-permute-start | bytes 98312 | tf_op jit(solution)/shard_map/ppermute | solution.py:222
  32.4 0.0 collective-permute-done.12
  32.4 2.4 %collective-permute-done.7 = bf16[64,256]{1,0:T(8,128)(2,1)S(1)} collective-permute-done((bf16[64,256]{1,0:T(8,128)(2,1)S(1)}, bf16[64,256]{1,0:T(8,128)(2,1)S(1)}, u32[]{:S(2)}, u32[]{:S(2)}) %collective-permute-start.7) | collective-permute-done | bytes 32800 | tf_op jit(solution)/shard_map/ppermute | solution.py:222
  34.8 0.7 %pad_maximum_fusion = f32[128,256]{1,0:T(8,128)} fusion(f32[64,256]{1,0:T(8,128)S(1)} %add_multiply_fusion, f32[64,256]{1,0:T(8,128)S(1)} %add_multiply_fusion.1), kind=kLoop, calls=%fused_computation.6 | loop fusion | flops 32768 | bytes 262144 | tf_op jit(solution)/shard_map/concatenate | solution.py:255
  (8 shorter events, 0.1 us)
Async XLA Ops:
  0.0 8.8 %copy-start = (s32[4,24,32]{2,1,0:T(8,128)S(1)}, s32[4,24,32]{2,1,0:T(8,128)}, u32[]{:S(2)}) copy-start(s32[4,24,32]{2,1,0:T(8,128)} %rest_1_.1) | copy-start | bytes 36868
  3.4 5.5 %collective-permute-start = (bf16[32,256]{1,0:T(8,128)(2,1)S(1)}, bf16[32,256]{1,0:T(8,128)(2,1)S(1)}, u32[]{:S(2)}, u32[]{:S(2)}) collective-permute-start(bf16[32,256]{1,0:T(8,128)(2,1)S(1)} %get-tuple-element.16), channel_id=1, source_target_pairs={{0,1},{1,0},{2,3},{3,2},{4,5},{5,4},{6,7},{7,6},{8,9},{9,8},{10,11... | collective-permute-start | bytes 49160 | tf_op jit(solution)/shard_map/ppermute | solution.py:222
  3.9 4.9 %collective-permute-start.1 = (bf16[32,256]{1,0:T(8,128)(2,1)S(1)}, bf16[32,256]{1,0:T(8,128)(2,1)S(1)}, u32[]{:S(2)}, u32[]{:S(2)}) collective-permute-start(bf16[32,256]{1,0:T(8,128)(2,1)S(1)} %get-tuple-element.17), channel_id=1, source_target_pairs={{1,2},{2,1},{3,4},{4,3},{5,6},{6,5},{7,8},{8,7},{9,10},{10,9},{11,... | collective-permute-start | bytes 49160 | tf_op jit(solution)/shard_map/ppermute | solution.py:222
  4.6 4.2 %collective-permute-start.2 = (bf16[24,256]{1,0:T(8,128)(2,1)S(1)}, bf16[24,256]{1,0:T(8,128)(2,1)S(1)}, u32[]{:S(2)}, u32[]{:S(2)}) collective-permute-start(bf16[24,256]{1,0:T(8,128)(2,1)S(1)} %get-tuple-element.18), channel_id=1, source_target_pairs={{0,16},{1,17},{2,18},{3,19},{4,20},{5,21},{6,22},{7,23},{8,24},{9,... | collective-permute-start | bytes 36872 | tf_op jit(solution)/shard_map/ppermute | solution.py:222
  10.5 3.5 %collective-permute-start.8 = (bf16[8,64,256]{2,1,0:T(8,128)(2,1)S(1)}, bf16[8,64,256]{2,1,0:T(8,128)(2,1)S(1)}, u32[]{:S(2)}, u32[]{:S(2)}) collective-permute-start(bf16[8,64,256]{2,1,0:T(8,128)(2,1)S(1)} %get-tuple-element.22), channel_id=1, source_target_pairs={{0,1},{1,0},{2,3},{3,2},{4,5},{5,4},{6,7},{7,6},{8,9},{9,8},{10,11... | collective-permute-start | bytes 786440 | tf_op jit(solution)/shard_map/ppermute | solution.py:222
  12.8 3.0 %collective-permute-start.3 = (bf16[8,64,256]{2,1,0:T(8,128)(2,1)S(1)}, bf16[8,64,256]{2,1,0:T(8,128)(2,1)S(1)}, u32[]{:S(2)}, u32[]{:S(2)}) collective-permute-start(bf16[8,64,256]{2,1,0:T(8,128)(2,1)S(1)} %get-tuple-element.20), channel_id=1, source_target_pairs={{0,1},{1,0},{2,3},{3,2},{4,5},{5,4},{6,7},{7,6},{8,9},{9,8},{10,11... | collective-permute-start | bytes 786440 | tf_op jit(solution)/shard_map/ppermute | solution.py:222
  14.1 4.5 %collective-permute-start.9 = (bf16[4,64,256]{2,1,0:T(8,128)(2,1)S(1)}, bf16[4,64,256]{2,1,0:T(8,128)(2,1)S(1)}, u32[]{:S(2)}, u32[]{:S(2)}) collective-permute-start(bf16[4,64,256]{2,1,0:T(8,128)(2,1)S(1)} %get-tuple-element.25), channel_id=1, source_target_pairs={{0,3},{1,4},{2,7},{3,0},{4,1},{5,6},{6,5},{7,2},{8,13},{9,10},{10,... | collective-permute-start | bytes 393224 | tf_op jit(solution)/shard_map/ppermute | solution.py:222
  15.9 5.7 %collective-permute-start.4 = (bf16[4,64,256]{2,1,0:T(8,128)(2,1)S(1)}, bf16[4,64,256]{2,1,0:T(8,128)(2,1)S(1)}, u32[]{:S(2)}, u32[]{:S(2)}) collective-permute-start(bf16[4,64,256]{2,1,0:T(8,128)(2,1)S(1)} %get-tuple-element.23), channel_id=1, source_target_pairs={{0,3},{1,4},{2,7},{3,0},{4,1},{5,6},{6,5},{7,2},{8,13},{9,10},{10,... | collective-permute-start | bytes 393224 | tf_op jit(solution)/shard_map/ppermute | solution.py:222
  18.6 5.0 %collective-permute-start.10 = (bf16[2,64,256]{2,1,0:T(8,128)(2,1)S(1)}, bf16[2,64,256]{2,1,0:T(8,128)(2,1)S(1)}, u32[]{:S(2)}, u32[]{:S(2)}) collective-permute-start(bf16[2,64,256]{2,1,0:T(8,128)(2,1)S(1)} %get-tuple-element.29), channel_id=1, source_target_pairs={{0,5},{1,2},{2,1},{3,6},{4,7},{5,0},{6,3},{7,4},{8,11},{9,12},{10,... | collective-permute-start | bytes 196616 | tf_op jit(solution)/shard_map/ppermute | solution.py:222
  21.6 4.8 %collective-permute-start.5 = (bf16[2,64,256]{2,1,0:T(8,128)(2,1)S(1)}, bf16[2,64,256]{2,1,0:T(8,128)(2,1)S(1)}, u32[]{:S(2)}, u32[]{:S(2)}) collective-permute-start(bf16[2,64,256]{2,1,0:T(8,128)(2,1)S(1)} %get-tuple-element.27), channel_id=1, source_target_pairs={{0,5},{1,2},{2,1},{3,6},{4,7},{5,0},{6,3},{7,4},{8,11},{9,12},{10,... | collective-permute-start | bytes 196616 | tf_op jit(solution)/shard_map/ppermute | solution.py:222
  23.6 4.4 %collective-permute-start.11 = (bf16[1,64,256]{2,1,0:T(8,128)(2,1)S(1)}, bf16[1,64,256]{2,1,0:T(8,128)(2,1)S(1)}, u32[]{:S(2)}, u32[]{:S(2)}) collective-permute-start(bf16[1,64,256]{2,1,0:T(8,128)(2,1)S(1)} %fusion.4), channel_id=1, source_target_pairs={{0,9},{1,8},{2,11},{3,10},{4,13},{5,12},{6,15},{7,14},{8,1},{9,0},... | collective-permute-start | bytes 98312 | tf_op jit(solution)/shard_map/ppermute | solution.py:222
  26.4 4.4 %collective-permute-start.6 = (bf16[1,64,256]{2,1,0:T(8,128)(2,1)S(1)}, bf16[1,64,256]{2,1,0:T(8,128)(2,1)S(1)}, u32[]{:S(2)}, u32[]{:S(2)}) collective-permute-start(bf16[1,64,256]{2,1,0:T(8,128)(2,1)S(1)} %fusion.7), channel_id=1, source_target_pairs={{0,9},{1,8},{2,11},{3,10},{4,13},{5,12},{6,15},{7,14},{8,1},{9,0},... | collective-permute-start | bytes 98312 | tf_op jit(solution)/shard_map/ppermute | solution.py:222
  28.0 4.4 %collective-permute-start.12 = (bf16[64,256]{1,0:T(8,128)(2,1)S(1)}, bf16[64,256]{1,0:T(8,128)(2,1)S(1)}, u32[]{:S(2)}, u32[]{:S(2)}) collective-permute-start(bf16[64,256]{1,0:T(8,128)(2,1)S(1)} %fusion.11), channel_id=1, source_target_pairs={{0,16},{1,17},{2,18},{3,19},{4,20},{5,21},{6,22},{7,23},{8,24},{9,... | collective-permute-start | bytes 98312 | tf_op jit(solution)/shard_map/ppermute | solution.py:222
  30.8 4.0 %collective-permute-start.7 = (bf16[64,256]{1,0:T(8,128)(2,1)S(1)}, bf16[64,256]{1,0:T(8,128)(2,1)S(1)}, u32[]{:S(2)}, u32[]{:S(2)}) collective-permute-start(bf16[64,256]{1,0:T(8,128)(2,1)S(1)} %fusion.10), channel_id=1, source_target_pairs={{0,16},{1,17},{2,18},{3,19},{4,20},{5,21},{6,22},{7,23},{8,24},{9,... | collective-permute-start | bytes 98312 | tf_op jit(solution)/shard_map/ppermute | solution.py:222

commit v3 on v2

--- a/solution.py
+++ b/solution.py
@@ -162,19 +162,26 @@
     return parity
 
 
+def ends(axis):
+    place = lax.axis_index(axis)
+    return place == 0, place == lax.axis_size(axis) - 1
+
+
 def partial_kernel(orders, masked, proj, halo_row_a, halo_row_b, *rest):
     *rest, smooth = rest
     rest, sends, keeps = rest[:-2 * CHUNKS], rest[-2 * CHUNKS:-CHUNKS], rest[-CHUNKS:]
     *halo_cols, links = rest
     row_a, row_b = halo_row_a[...].astype(F32), halo_row_b[...].astype(F32)
     odd = lax.rem(lax.axis_index("tile"), 2)
-    north = jnp.where(odd == 0, row_b, row_a)
-    south = jnp.where(odd == 0, row_a, row_b)
+    first, last = ends("tile")
+    north = jnp.where(first, 0.0, jnp.where(odd == 0, row_b, row_a))
+    south = jnp.where(last, 0.0, jnp.where(odd == 0, row_a, row_b))
     col_a = halo_cols[0][...].astype(F32)
     col_b = halo_cols[1][...].astype(F32) if len(halo_cols) > 1 else jnp.zeros_like(col_a)
     even = lax.rem(lax.axis_index("grp"), 2) == 0
-    west = jnp.where(even, col_b, col_a)
-    east = jnp.where(even, col_a, col_b)
+    first, last = ends("grp")
+    west = jnp.where(first, 0.0, jnp.where(even, col_b, col_a))
+    east = jnp.where(last, 0.0, jnp.where(even, col_a, col_b))
     smooth_rows(proj, north, south, west, east, links, smooth)
     values = smooth[...]
     half_blocks(orders, 1, masked, values, sends)
@@ -217,8 +224,9 @@
         for g in range(groups):
             for t in range(tiles):
                 to_g, to_t = partner(g, t)
-                if 0 <= to_g < groups and 0 <= to_t < tiles:
-                    pairs.append((g * tiles + t, to_g * tiles + to_t))
+                if not 0 <= to_t < tiles:
+                    to_g, to_t = g ^ 1, t
+                pairs.append((g * tiles + t, to_g % groups * tiles + to_t))
         return lax.ppermute(values, AXES, pairs)
 
     masked, proj, row_a, row_b, *cols = project(occupancy, features, basis_cols, 1 if groups <= 2 else 2)

time: 35.6 us -> 33.6 us (0.944)
  starting transfers between devices: 19.7 us -> 15.4 us
  waiting for transfers between devices: 9.77 us -> 12.1 us
    ppermute x13, starting transfers between devices: 19.7 us -> 15.4 us  [exchange(): return lax.ppermute(values, AXES, pairs)]
    ppermute x13, waiting for transfers between devices: 9.77 us -> 12.1 us  [exchange(): return lax.ppermute(values, AXES, pairs)]
where the time goes in v3:
time: 33.6 us; the launch traced here: 33.5 us
  starting transfers between devices  15.4 us (46%)
  waiting for transfers between devices  12.1 us (36%)
  Pallas kernels  5.01 us (15%)
  other arithmetic  0.89 us (3%)
    ppermute x13, starting transfers between devices, exchange(): return lax.ppermute(values, AXES, pairs)  15.4 us
    ppermute x13, waiting for transfers between devices, exchange(): return lax.ppermute(values, AXES, pairs)  12.1 us
    pallas_call x1, Pallas kernels, project(): pl.pallas_call(project_kernel, out_shape=(pltpu.VMEM((lat, lon, words), B...  3.37 us
    pallas_call x1, Pallas kernels, partial_product(): pl.pallas_call(functools.partial(partial_kernel, orders), out_shape=(pltp...  1.64 us
  transfers between devices with their start and end apart: 13, of which 7 were waited for; matrix products, arithmetic and copies ran while one was open for 1% of the time, Pallas kernels for 0%

profile of v3, /device:TPU:0, one launch (start us, length us, event | category | flops | bytes accessed | tf_op | source)
XLA Modules:
  0.0 33.5 jit_solution(15324537740487220361)
XLA Ops:
  0.0 0.0 copy-start
  0.0 3.4 %shard_map.46 = (bf16[24,32,2048]{2,1,0:T(8,128)(2,1)S(1)}, bf16[24,32,256]{2,1,0:T(8,128)(2,1)S(1)}, bf16[32,256]{1,0:T(8,128)(2,1)S(1)}, bf16[32,256]{1,0:T(8,128)(2,1)S(1)}, bf16[24,256]{1,0:T(8,128)(2,1)S(1)}) custom-call(s32[12,1,16]{2,1,0:T(1,128)} %occ_hbm.1, bf16[24,32,2048]{2,1,0:T(8,128)(2,1)} %feat_hbm.1, bf16[2048,256]{1,0:T(8,128)(2,1)} %basis_hbm.1), custom_call_target="tpu_custom_call" | custom-call | flops 805306368 | bytes 3145728 | tf_op jit(solution)/shard_map/pallas_call | solution.py:75
  3.4 0.6 %collective-permute-start = (bf16[32,256]{1,0:T(8,128)(2,1)S(1)}, bf16[32,256]{1,0:T(8,128)(2,1)S(1)}, u32[]{:S(2)}, u32[]{:S(2)}) collective-permute-start(bf16[32,256]{1,0:T(8,128)(2,1)S(1)} %get-tuple-element.16), channel_id=1, source_target_pairs={{0,1},{1,0},{2,3},{3,2},{4,5},{5,4},{6,7},{7,6},{8,9},{9,8},{10,11... | collective-permute-start | bytes 49160 | tf_op jit(solution)/shard_map/ppermute | solution.py:230
  3.9 2.6 %collective-permute-start.1 = (bf16[32,256]{1,0:T(8,128)(2,1)S(1)}, bf16[32,256]{1,0:T(8,128)(2,1)S(1)}, u32[]{:S(2)}, u32[]{:S(2)}) collective-permute-start(bf16[32,256]{1,0:T(8,128)(2,1)S(1)} %get-tuple-element.17), channel_id=1, source_target_pairs={{0,16},{1,2},{2,1},{3,4},{4,3},{5,6},{6,5},{7,8},{8,7},{9,10},{10,... | collective-permute-start | bytes 49160 | tf_op jit(solution)/shard_map/ppermute | solution.py:230
  6.5 0.1 collective-permute-start.2
  6.6 3.6 %collective-permute-done.2.rest_0_ = bf16[24,256]{1,0:T(8,128)(2,1)S(1)} collective-permute-done((bf16[24,256]{1,0:T(8,128)(2,1)S(1)}, bf16[24,256]{1,0:T(8,128)(2,1)S(1)}, u32[]{:S(2)}, u32[]{:S(2)}) %collective-permute-start.2) | collective-permute-done | bytes 12320 | tf_op jit(solution)/shard_map/ppermute | solution.py:230
  10.2 0.0 collective-permute-done.halo_row_a
  10.2 0.0 collective-permute-done.1.halo_row_b
  10.2 0.0 copy-done
  10.2 1.6 %shard_map.47 = (bf16[8,64,256]{2,1,0:T(8,128)(2,1)S(1)}, bf16[8,64,256]{2,1,0:T(8,128)(2,1)S(1)}, f32[8,64,256]{2,1,0:T(8,128)S(1)}, f32[8,64,256]{2,1,0:T(8,128)S(1)}) custom-call(bf16[24,32,2048]{2,1,0:T(8,128)(2,1)S(1)} %get-tuple-element.14.masked, bf16[24,32,256]{2,1,0:T(8,128)(2,1)S(1)} %get-tuple-element.15.proj, ...), custom_call_target="tpu_custom_call" | custom-call | flops 805306368 | bytes 3145728 | tf_op jit(solution)/shard_map/pallas_call | solution.py:195
  11.8 0.1 collective-permute-start.8
  11.9 0.5 %collective-permute-start.3 = (bf16[8,64,256]{2,1,0:T(8,128)(2,1)S(1)}, bf16[8,64,256]{2,1,0:T(8,128)(2,1)S(1)}, u32[]{:S(2)}, u32[]{:S(2)}) collective-permute-start(bf16[8,64,256]{2,1,0:T(8,128)(2,1)S(1)} %get-tuple-element.20), channel_id=1, source_target_pairs={{0,1},{1,0},{2,3},{3,2},{4,5},{5,4},{6,7},{7,6},{8,9},{9,8},{10,11... | collective-permute-start | bytes 786440 | tf_op jit(solution)/shard_map/ppermute | solution.py:230
  12.4 1.0 %collective-permute-done.8 = bf16[8,64,256]{2,1,0:T(8,128)(2,1)S(1)} collective-permute-done((bf16[8,64,256]{2,1,0:T(8,128)(2,1)S(1)}, bf16[8,64,256]{2,1,0:T(8,128)(2,1)S(1)}, u32[]{:S(2)}, u32[]{:S(2)}) %collective-permute-start.8) | collective-permute-done | bytes 262176 | tf_op jit(solution)/shard_map/ppermute | solution.py:230
  13.4 0.1 fusion.1
  13.5 0.5 %collective-permute-start.9 = (bf16[4,64,256]{2,1,0:T(8,128)(2,1)S(1)}, bf16[4,64,256]{2,1,0:T(8,128)(2,1)S(1)}, u32[]{:S(2)}, u32[]{:S(2)}) collective-permute-start(bf16[4,64,256]{2,1,0:T(8,128)(2,1)S(1)} %get-tuple-element.25), channel_id=1, source_target_pairs={{0,3},{1,4},{2,7},{3,0},{4,1},{5,6},{6,5},{7,2},{8,13},{9,10},{10,... | collective-permute-start | bytes 393224 | tf_op jit(solution)/shard_map/ppermute | solution.py:230
  14.0 0.0 collective-permute-done.3
  14.0 0.1 fusion
  14.1 1.4 %collective-permute-start.4 = (bf16[4,64,256]{2,1,0:T(8,128)(2,1)S(1)}, bf16[4,64,256]{2,1,0:T(8,128)(2,1)S(1)}, u32[]{:S(2)}, u32[]{:S(2)}) collective-permute-start(bf16[4,64,256]{2,1,0:T(8,128)(2,1)S(1)} %get-tuple-element.23), channel_id=1, source_target_pairs={{0,3},{1,4},{2,7},{3,0},{4,1},{5,6},{6,5},{7,2},{8,13},{9,10},{10,... | collective-permute-start | bytes 393224 | tf_op jit(solution)/shard_map/ppermute | solution.py:230
  15.4 2.5 %collective-permute-done.9 = bf16[4,64,256]{2,1,0:T(8,128)(2,1)S(1)} collective-permute-done((bf16[4,64,256]{2,1,0:T(8,128)(2,1)S(1)}, bf16[4,64,256]{2,1,0:T(8,128)(2,1)S(1)}, u32[]{:S(2)}, u32[]{:S(2)}) %collective-permute-start.9) | collective-permute-done | bytes 131104 | tf_op jit(solution)/shard_map/ppermute | solution.py:230
  18.0 1.6 %collective-permute-start.10 = (bf16[2,64,256]{2,1,0:T(8,128)(2,1)S(1)}, bf16[2,64,256]{2,1,0:T(8,128)(2,1)S(1)}, u32[]{:S(2)}, u32[]{:S(2)}) collective-permute-start(bf16[2,64,256]{2,1,0:T(8,128)(2,1)S(1)} %get-tuple-element.29), channel_id=1, source_target_pairs={{0,5},{1,2},{2,1},{3,6},{4,7},{5,0},{6,3},{7,4},{8,11},{9,12},{10,... | collective-permute-start | bytes 196616 | tf_op jit(solution)/shard_map/ppermute | solution.py:230
  19.6 0.0 collective-permute-done.4
  19.7 1.1 %collective-permute-start.5 = (bf16[2,64,256]{2,1,0:T(8,128)(2,1)S(1)}, bf16[2,64,256]{2,1,0:T(8,128)(2,1)S(1)}, u32[]{:S(2)}, u32[]{:S(2)}) collective-permute-start(bf16[2,64,256]{2,1,0:T(8,128)(2,1)S(1)} %get-tuple-element.27), channel_id=1, source_target_pairs={{0,5},{1,2},{2,1},{3,6},{4,7},{5,0},{6,3},{7,4},{8,11},{9,12},{10,... | collective-permute-start | bytes 196616 | tf_op jit(solution)/shard_map/ppermute | solution.py:230
  20.7 1.0 %collective-permute-done.10 = bf16[2,64,256]{2,1,0:T(8,128)(2,1)S(1)} collective-permute-done((bf16[2,64,256]{2,1,0:T(8,128)(2,1)S(1)}, bf16[2,64,256]{2,1,0:T(8,128)(2,1)S(1)}, u32[]{:S(2)}, u32[]{:S(2)}) %collective-permute-start.10) | collective-permute-done | bytes 65568 | tf_op jit(solution)/shard_map/ppermute | solution.py:230
  21.8 2.6 %collective-permute-start.11 = (bf16[1,64,256]{2,1,0:T(8,128)(2,1)S(1)}, bf16[1,64,256]{2,1,0:T(8,128)(2,1)S(1)}, u32[]{:S(2)}, u32[]{:S(2)}) collective-permute-start(bf16[1,64,256]{2,1,0:T(8,128)(2,1)S(1)} %fusion.4), channel_id=1, source_target_pairs={{0,9},{1,8},{2,11},{3,10},{4,13},{5,12},{6,15},{7,14},{8,1},{9,0},... | collective-permute-start | bytes 98312 | tf_op jit(solution)/shard_map/ppermute | solution.py:230
  24.4 0.0 collective-permute-done.5
  24.4 1.3 %collective-permute-start.6 = (bf16[1,64,256]{2,1,0:T(8,128)(2,1)S(1)}, bf16[1,64,256]{2,1,0:T(8,128)(2,1)S(1)}, u32[]{:S(2)}, u32[]{:S(2)}) collective-permute-start(bf16[1,64,256]{2,1,0:T(8,128)(2,1)S(1)} %fusion.7), channel_id=1, source_target_pairs={{0,9},{1,8},{2,11},{3,10},{4,13},{5,12},{6,15},{7,14},{8,1},{9,0},... | collective-permute-start | bytes 98312 | tf_op jit(solution)/shard_map/ppermute | solution.py:230
  25.8 0.3 collective-permute-done.11
  26.1 1.5 %collective-permute-start.12 = (bf16[64,256]{1,0:T(8,128)(2,1)S(1)}, bf16[64,256]{1,0:T(8,128)(2,1)S(1)}, u32[]{:S(2)}, u32[]{:S(2)}) collective-permute-start(bf16[64,256]{1,0:T(8,128)(2,1)S(1)} %fusion.11), channel_id=1, source_target_pairs={{0,16},{1,17},{2,18},{3,19},{4,20},{5,21},{6,22},{7,23},{8,24},{9,... | collective-permute-start | bytes 98312 | tf_op jit(solution)/shard_map/ppermute | solution.py:230
  27.6 1.2 %collective-permute-done.6 = bf16[1,64,256]{2,1,0:T(8,128)(2,1)S(1)} collective-permute-done((bf16[1,64,256]{2,1,0:T(8,128)(2,1)S(1)}, bf16[1,64,256]{2,1,0:T(8,128)(2,1)S(1)}, u32[]{:S(2)}, u32[]{:S(2)}) %collective-permute-start.6) | collective-permute-done | bytes 32800 | tf_op jit(solution)/shard_map/ppermute | solution.py:230
  28.8 1.6 %collective-permute-start.7 = (bf16[64,256]{1,0:T(8,128)(2,1)S(1)}, bf16[64,256]{1,0:T(8,128)(2,1)S(1)}, u32[]{:S(2)}, u32[]{:S(2)}) collective-permute-start(bf16[64,256]{1,0:T(8,128)(2,1)S(1)} %fusion.10), channel_id=1, source_target_pairs={{0,16},{1,17},{2,18},{3,19},{4,20},{5,21},{6,22},{7,23},{8,24},{9,... | collective-permute-start | bytes 98312 | tf_op jit(solution)/shard_map/ppermute | solution.py:230
  30.4 0.0 collective-permute-done.12
  30.4 2.4 %collective-permute-done.7 = bf16[64,256]{1,0:T(8,128)(2,1)S(1)} collective-permute-done((bf16[64,256]{1,0:T(8,128)(2,1)S(1)}, bf16[64,256]{1,0:T(8,128)(2,1)S(1)}, u32[]{:S(2)}, u32[]{:S(2)}) %collective-permute-start.7) | collective-permute-done | bytes 32800 | tf_op jit(solution)/shard_map/ppermute | solution.py:230
  32.8 0.7 %pad_maximum_fusion = f32[128,256]{1,0:T(8,128)} fusion(f32[64,256]{1,0:T(8,128)S(1)} %add_multiply_fusion, f32[64,256]{1,0:T(8,128)S(1)} %add_multiply_fusion.1), kind=kLoop, calls=%fused_computation.6 | loop fusion | flops 32768 | bytes 262144 | tf_op jit(solution)/shard_map/concatenate | solution.py:263
  (8 shorter events, 0.1 us)
Async XLA Ops:
  0.0 10.2 %copy-start = (s32[4,24,32]{2,1,0:T(8,128)S(1)}, s32[4,24,32]{2,1,0:T(8,128)}, u32[]{:S(2)}) copy-start(s32[4,24,32]{2,1,0:T(8,128)} %rest_1_.1) | copy-start | bytes 36868
  3.4 6.8 %collective-permute-start = (bf16[32,256]{1,0:T(8,128)(2,1)S(1)}, bf16[32,256]{1,0:T(8,128)(2,1)S(1)}, u32[]{:S(2)}, u32[]{:S(2)}) collective-permute-start(bf16[32,256]{1,0:T(8,128)(2,1)S(1)} %get-tuple-element.16), channel_id=1, source_target_pairs={{0,1},{1,0},{2,3},{3,2},{4,5},{5,4},{6,7},{7,6},{8,9},{9,8},{10,11... | collective-permute-start | bytes 49160 | tf_op jit(solution)/shard_map/ppermute | solution.py:230
  3.9 6.3 %collective-permute-start.1 = (bf16[32,256]{1,0:T(8,128)(2,1)S(1)}, bf16[32,256]{1,0:T(8,128)(2,1)S(1)}, u32[]{:S(2)}, u32[]{:S(2)}) collective-permute-start(bf16[32,256]{1,0:T(8,128)(2,1)S(1)} %get-tuple-element.17), channel_id=1, source_target_pairs={{0,16},{1,2},{2,1},{3,4},{4,3},{5,6},{6,5},{7,8},{8,7},{9,10},{10,... | collective-permute-start | bytes 49160 | tf_op jit(solution)/shard_map/ppermute | solution.py:230
  6.5 3.7 %collective-permute-start.2 = (bf16[24,256]{1,0:T(8,128)(2,1)S(1)}, bf16[24,256]{1,0:T(8,128)(2,1)S(1)}, u32[]{:S(2)}, u32[]{:S(2)}) collective-permute-start(bf16[24,256]{1,0:T(8,128)(2,1)S(1)} %get-tuple-element.18), channel_id=1, source_target_pairs={{0,16},{1,17},{2,18},{3,19},{4,20},{5,21},{6,22},{7,23},{8,24},{9,... | collective-permute-start | bytes 36872 | tf_op jit(solution)/shard_map/ppermute | solution.py:230
  11.8 1.6 %collective-permute-start.8 = (bf16[8,64,256]{2,1,0:T(8,128)(2,1)S(1)}, bf16[8,64,256]{2,1,0:T(8,128)(2,1)S(1)}, u32[]{:S(2)}, u32[]{:S(2)}) collective-permute-start(bf16[8,64,256]{2,1,0:T(8,128)(2,1)S(1)} %get-tuple-element.22), channel_id=1, source_target_pairs={{0,1},{1,0},{2,3},{3,2},{4,5},{5,4},{6,7},{7,6},{8,9},{9,8},{10,11... | collective-permute-start | bytes 786440 | tf_op jit(solution)/shard_map/ppermute | solution.py:230
  11.9 2.1 %collective-permute-start.3 = (bf16[8,64,256]{2,1,0:T(8,128)(2,1)S(1)}, bf16[8,64,256]{2,1,0:T(8,128)(2,1)S(1)}, u32[]{:S(2)}, u32[]{:S(2)}) collective-permute-start(bf16[8,64,256]{2,1,0:T(8,128)(2,1)S(1)} %get-tuple-element.20), channel_id=1, source_target_pairs={{0,1},{1,0},{2,3},{3,2},{4,5},{5,4},{6,7},{7,6},{8,9},{9,8},{10,11... | collective-permute-start | bytes 786440 | tf_op jit(solution)/shard_map/ppermute | solution.py:230
  13.5 4.5 %collective-permute-start.9 = (bf16[4,64,256]{2,1,0:T(8,128)(2,1)S(1)}, bf16[4,64,256]{2,1,0:T(8,128)(2,1)S(1)}, u32[]{:S(2)}, u32[]{:S(2)}) collective-permute-start(bf16[4,64,256]{2,1,0:T(8,128)(2,1)S(1)} %get-tuple-element.25), channel_id=1, source_target_pairs={{0,3},{1,4},{2,7},{3,0},{4,1},{5,6},{6,5},{7,2},{8,13},{9,10},{10,... | collective-permute-start | bytes 393224 | tf_op jit(solution)/shard_map/ppermute | solution.py:230
  14.1 5.6 %collective-permute-start.4 = (bf16[4,64,256]{2,1,0:T(8,128)(2,1)S(1)}, bf16[4,64,256]{2,1,0:T(8,128)(2,1)S(1)}, u32[]{:S(2)}, u32[]{:S(2)}) collective-permute-start(bf16[4,64,256]{2,1,0:T(8,128)(2,1)S(1)} %get-tuple-element.23), channel_id=1, source_target_pairs={{0,3},{1,4},{2,7},{3,0},{4,1},{5,6},{6,5},{7,2},{8,13},{9,10},{10,... | collective-permute-start | bytes 393224 | tf_op jit(solution)/shard_map/ppermute | solution.py:230
  18.0 3.8 %collective-permute-start.10 = (bf16[2,64,256]{2,1,0:T(8,128)(2,1)S(1)}, bf16[2,64,256]{2,1,0:T(8,128)(2,1)S(1)}, u32[]{:S(2)}, u32[]{:S(2)}) collective-permute-start(bf16[2,64,256]{2,1,0:T(8,128)(2,1)S(1)} %get-tuple-element.29), channel_id=1, source_target_pairs={{0,5},{1,2},{2,1},{3,6},{4,7},{5,0},{6,3},{7,4},{8,11},{9,12},{10,... | collective-permute-start | bytes 196616 | tf_op jit(solution)/shard_map/ppermute | solution.py:230
  19.7 4.8 %collective-permute-start.5 = (bf16[2,64,256]{2,1,0:T(8,128)(2,1)S(1)}, bf16[2,64,256]{2,1,0:T(8,128)(2,1)S(1)}, u32[]{:S(2)}, u32[]{:S(2)}) collective-permute-start(bf16[2,64,256]{2,1,0:T(8,128)(2,1)S(1)} %get-tuple-element.27), channel_id=1, source_target_pairs={{0,5},{1,2},{2,1},{3,6},{4,7},{5,0},{6,3},{7,4},{8,11},{9,12},{10,... | collective-permute-start | bytes 196616 | tf_op jit(solution)/shard_map/ppermute | solution.py:230
  21.8 4.3 %collective-permute-start.11 = (bf16[1,64,256]{2,1,0:T(8,128)(2,1)S(1)}, bf16[1,64,256]{2,1,0:T(8,128)(2,1)S(1)}, u32[]{:S(2)}, u32[]{:S(2)}) collective-permute-start(bf16[1,64,256]{2,1,0:T(8,128)(2,1)S(1)} %fusion.4), channel_id=1, source_target_pairs={{0,9},{1,8},{2,11},{3,10},{4,13},{5,12},{6,15},{7,14},{8,1},{9,0},... | collective-permute-start | bytes 98312 | tf_op jit(solution)/shard_map/ppermute | solution.py:230
  24.4 4.4 %collective-permute-start.6 = (bf16[1,64,256]{2,1,0:T(8,128)(2,1)S(1)}, bf16[1,64,256]{2,1,0:T(8,128)(2,1)S(1)}, u32[]{:S(2)}, u32[]{:S(2)}) collective-permute-start(bf16[1,64,256]{2,1,0:T(8,128)(2,1)S(1)} %fusion.7), channel_id=1, source_target_pairs={{0,9},{1,8},{2,11},{3,10},{4,13},{5,12},{6,15},{7,14},{8,1},{9,0},... | collective-permute-start | bytes 98312 | tf_op jit(solution)/shard_map/ppermute | solution.py:230
  26.1 4.3 %collective-permute-start.12 = (bf16[64,256]{1,0:T(8,128)(2,1)S(1)}, bf16[64,256]{1,0:T(8,128)(2,1)S(1)}, u32[]{:S(2)}, u32[]{:S(2)}) collective-permute-start(bf16[64,256]{1,0:T(8,128)(2,1)S(1)} %fusion.11), channel_id=1, source_target_pairs={{0,16},{1,17},{2,18},{3,19},{4,20},{5,21},{6,22},{7,23},{8,24},{9,... | collective-permute-start | bytes 98312 | tf_op jit(solution)/shard_map/ppermute | solution.py:230
  28.8 4.0 %collective-permute-start.7 = (bf16[64,256]{1,0:T(8,128)(2,1)S(1)}, bf16[64,256]{1,0:T(8,128)(2,1)S(1)}, u32[]{:S(2)}, u32[]{:S(2)}) collective-permute-start(bf16[64,256]{1,0:T(8,128)(2,1)S(1)} %fusion.10), channel_id=1, source_target_pairs={{0,16},{1,17},{2,18},{3,19},{4,20},{5,21},{6,22},{7,23},{8,24},{9,... | collective-permute-start | bytes 98312 | tf_op jit(solution)/shard_map/ppermute | solution.py:230

commit v4 on v3

--- a/solution.py
+++ b/solution.py
@@ -14,40 +14,53 @@
 IN_HBM = pl.BlockSpec(memory_space=pltpu.HBM)
 IN_VMEM = pl.BlockSpec(memory_space=pltpu.VMEM)
 KERNEL_VMEM = 24 << 20
-WORD_CHUNK = 512
+WORD_CHUNKS = (0.375, 0.375, 0.25)
 CHUNKS = 2
 
 
-def project_kernel(occ_hbm, feat_hbm, basis_hbm, masked, proj, *rest):
-    *edges, basis, total, occ, sems = rest
+def word_chunks(words):
+    sizes = [int(words * part) for part in WORD_CHUNKS]
+    return [(sum(sizes[:k]), size) for k, size in enumerate(sizes)]
+
+
+def project_kernel(occ_hbm, links_hbm, feat_hbm, basis_hbm, masked, proj, shares, *rest):
+    *edges, basis, total, links, occ, sems = rest
     row_a, row_b = edges[:2]
     lat, lon, words = masked.shape
-    blocks = occ.shape[2]
-    block = words // blocks
-    chunk = min(WORD_CHUNK, words)
-    count = words // chunk
-    occ_copy = pltpu.make_async_copy(occ_hbm, occ, sems.at[2 * count])
+    block = words // occ.shape[2]
+    chunks = word_chunks(words)
+    count = len(chunks)
+    links_copy = pltpu.make_async_copy(links_hbm, links, sems.at[2 * count])
+    occ_copy = pltpu.make_async_copy(occ_hbm, occ, sems.at[2 * count + 1])
+    links_copy.start()
     occ_copy.start()
     copies = []
-    for k in range(count):
-        part = pl.ds(k * chunk, chunk)
+    for k, (start, size) in enumerate(chunks):
+        part = pl.ds(start, size)
         basis_copy = pltpu.make_async_copy(basis_hbm.at[part], basis.at[part], sems.at[count + k])
         feat_copy = pltpu.make_async_copy(feat_hbm.at[:, :, part], masked.at[:, :, part], sems.at[k])
         basis_copy.start()
         feat_copy.start()
         copies.append((basis_copy, feat_copy))
+    links_copy.wait()
+    weights = links[...].astype(F32)
+    weights = weights / jnp.maximum(jnp.sum(weights, axis=0), 1.0)
+    for k in range(4):
+        column = jnp.transpose(weights[k])
+        for i in range(lat):
+            shares[k, pl.ds(i * lon, lon), :] = jnp.broadcast_to(column[:, i:i + 1], (lon, shares.shape[2]))
     occ_copy.wait()
-    for k in range(count):
+    for k, (start, size) in enumerate(chunks):
         copies[k][0].wait()
         copies[k][1].wait()
         for i in range(lat // 2):
-            for b in range(k * chunk // block, (k + 1) * chunk // block):
+            for b in range(start // block, (start + size) // block):
                 gate = occ[i, 0, b].astype(F32).astype(BF16)
                 spot = (pl.ds(2 * i, 2), slice(None), pl.ds(b * block, block))
                 masked[spot] = masked[spot] * gate
-        part = pl.ds(k * chunk, chunk)
+        part = pl.ds(start, size)
         term = jnp.dot(
-            masked[:, :, part].reshape(lat * lon, chunk), basis[part, :], preferred_element_type=F32
+            masked[:, :, part].reshape(lat * lon, size), basis[part, :], preferred_element_type=F32
         )
         if k:
             term = total[...] + term
@@ -67,26 +80,30 @@
         edges[3][...] = jnp.where(even, west, east).astype(BF16)
 
 
-def project(occupancy, features, basis_cols, columns):
+def project(occupancy, link_weights, features, basis_cols, columns):
     lat, lon, words = features.shape
     rank = basis_cols.shape[1]
-    count = words // min(WORD_CHUNK, words)
-    operands = [pltpu.with_memory_space_constraint(v, pltpu.HBM) for v in (occupancy, features, basis_cols)]
+    operands = [
+        pltpu.with_memory_space_constraint(v, pltpu.HBM)
+        for v in (occupancy, link_weights, features, basis_cols)
+    ]
     return pl.pallas_call(
         project_kernel,
         out_shape=(
             pltpu.VMEM((lat, lon, words), BF16),
             pltpu.VMEM((lat, lon, rank), BF16),
+            pltpu.VMEM((4, lat * lon, min(rank, 128)), F32),
             pltpu.VMEM((lon, rank), BF16),
             pltpu.VMEM((lon, rank), BF16),
         ) + (pltpu.VMEM((lat, rank), BF16),) * columns,
-        in_specs=[IN_HBM] * 3,
-        out_specs=(IN_VMEM,) * (4 + columns),
+        in_specs=[IN_HBM] * 4,
+        out_specs=(IN_VMEM,) * (5 + columns),
         scratch_shapes=[
             pltpu.VMEM(basis_cols.shape, BF16),
             pltpu.VMEM((lat * lon, rank), F32),
+            pltpu.VMEM(link_weights.shape, jnp.int32),
             pltpu.SMEM(occupancy.shape, jnp.int32),
-            pltpu.SemaphoreType.DMA((2 * count + 1,)),
+            pltpu.SemaphoreType.DMA((2 * len(word_chunks(words)) + 2,)),
         ],
         compiler_params=pltpu.CompilerParams(vmem_limit_bytes=KERNEL_VMEM),
         cost_estimate=pl.CostEstimate(
@@ -95,11 +112,9 @@
     )(*operands)
 
 
-def smooth_rows(proj, north, south, west, east, links, smooth):
+def smooth_rows(proj, north, south, west, east, shares, smooth):
     lat, lon, rank = proj.shape
-    weights = links[...].astype(F32)
-    weights = weights / jnp.maximum(jnp.sum(weights, axis=0), 1.0)
-    columns = [jnp.transpose(weights[k]) for k in range(4)]
+    wide = rank // shares.shape[2]
     place = lax.broadcasted_iota(jnp.int32, (lon, rank), 0)
     for i in range(lat):
         row = proj[i].astype(F32)
@@ -107,7 +122,7 @@
         below = proj[i + 1].astype(F32) if i < lat - 1 else south
         left = jnp.where(place == 0, west[i:i + 1, :], pltpu.roll(row, 1, 0))
         right = jnp.where(place == lon - 1, east[i:i + 1, :], pltpu.roll(row, lon - 1, 0))
-        link = [jnp.broadcast_to(columns[k][:, i:i + 1], (lon, rank)) for k in range(4)]
+        link = [jnp.tile(shares[k, pl.ds(i * lon, lon), :], (1, wide)) for k in range(4)]
         value = link[0] * above + link[1] * below + link[2] * left + link[3] * right
         smooth[pl.ds(i * lon, lon), :] = value.astype(BF16)
 
@@ -170,7 +185,7 @@
 def partial_kernel(orders, masked, proj, halo_row_a, halo_row_b, *rest):
     *rest, smooth = rest
     rest, sends, keeps = rest[:-2 * CHUNKS], rest[-2 * CHUNKS:-CHUNKS], rest[-CHUNKS:]
-    *halo_cols, links = rest
+    *halo_cols, shares = rest
     row_a, row_b = halo_row_a[...].astype(F32), halo_row_b[...].astype(F32)
     odd = lax.rem(lax.axis_index("tile"), 2)
     first, last = ends("tile")
@@ -182,13 +197,13 @@
     first, last = ends("grp")
     west = jnp.where(first, 0.0, jnp.where(even, col_b, col_a))
     east = jnp.where(last, 0.0, jnp.where(even, col_a, col_b))
-    smooth_rows(proj, north, south, west, east, links, smooth)
+    smooth_rows(proj, north, south, west, east, shares, smooth)
     values = smooth[...]
     half_blocks(orders, 1, masked, values, sends)
     half_blocks(orders, 0, masked, values, keeps)
 
 
-def partial_product(orders, share, masked, proj, rows, cols, link_weights):
+def partial_product(orders, share, masked, proj, rows, cols, shares):
     lat, lon, words = masked.shape
     rank = proj.shape[2]
     shape = (words // share // 2, share // CHUNKS, rank)
@@ -202,7 +217,7 @@
         cost_estimate=pl.CostEstimate(
             flops=2 * lat * lon * words * rank, bytes_accessed=2 * lat * lon * words, transcendentals=0
         ),
-    )(masked, proj, *rows, *cols, link_weights)
+    )(masked, proj, *rows, *cols, shares)
     return outs[:CHUNKS], outs[CHUNKS:]
 
 
@@ -229,14 +244,16 @@
                 pairs.append((g * tiles + t, to_g % groups * tiles + to_t))
         return lax.ppermute(values, AXES, pairs)
 
-    masked, proj, row_a, row_b, *cols = project(occupancy, features, basis_cols, 1 if groups <= 2 else 2)
+    masked, proj, shares, row_a, row_b, *cols = project(
+        occupancy, link_weights, features, basis_cols, 1 if groups <= 2 else 2
+    )
     halo_row_b = exchange(row_b, lambda g, t: (g, t - 1 + 2 * (t % 2)))
     halo_cols = [exchange(cols[0], lambda g, t: (g + 1 - 2 * (g % 2), t))]
     if groups > 2:
         halo_cols.append(exchange(cols[1], lambda g, t: (g - 1 + 2 * (g % 2), t)))
     halo_row_a = exchange(row_a, lambda g, t: (g, t ^ 1))
     sends, keeps = partial_product(
-        orders, share, masked, proj, (halo_row_a, halo_row_b), halo_cols, link_weights
+        orders, share, masked, proj, (halo_row_a, halo_row_b), halo_cols, shares
     )
     parity = tile_parity()
     pick = functools.partial(lax.dynamic_index_in_dim, axis=0, keepdims=False)

time: 33.6 us -> 33.3 us (level)
  no operation moved by 1% of the time
where the time goes in v4:
time: 33.3 us; the launch traced here: 33.2 us
  starting transfers between devices  15.4 us (46%)
  waiting for transfers between devices  12.1 us (36%)
  Pallas kernels  4.69 us (14%)
  other arithmetic  0.89 us (3%)
    ppermute x13, starting transfers between devices, exchange(): return lax.ppermute(values, AXES, pairs)  15.4 us
    ppermute x13, waiting for transfers between devices, exchange(): return lax.ppermute(values, AXES, pairs)  12.1 us
    pallas_call x1, Pallas kernels, project(): pl.pallas_call(project_kernel, out_shape=(pltpu.VMEM((lat, lon, words), B...  3.33 us
    pallas_call x1, Pallas kernels, partial_product(): pl.pallas_call(functools.partial(partial_kernel, orders), out_shape=(pltp...  1.36 us
  transfers between devices with their start and end apart: 13, of which 7 were waited for; matrix products, arithmetic and copies ran while one was open for 1% of the time, Pallas kernels for 0%

profile of v4, /device:TPU:0, one launch (start us, length us, event | category | flops | bytes accessed | tf_op | source)
XLA Modules:
  0.0 33.2 jit_solution(5797223358844062057)
XLA Ops:
  0.0 3.3 %shard_map.46 = (bf16[24,32,2048]{2,1,0:T(8,128)(2,1)S(1)}, bf16[24,32,256]{2,1,0:T(8,128)(2,1)S(1)}, f32[4,768,128]{2,1,0:T(8,128)S(1)}, bf16[32,256]{1,0:T(8,1...) custom-call(s32[12,1,16]{2,1,0:T(1,128)} %occ_hbm.1, s32[4,24,32]{2,1,0:T(8,128)} %links_hbm.1, ...), custom_call_target="tpu_custom_call" | custom-call | flops 805306368 | bytes 3145728 | tf_op jit(solution)/shard_map/pallas_call | solution.py:90
  3.3 0.6 %collective-permute-start = (bf16[32,256]{1,0:T(8,128)(2,1)S(1)}, bf16[32,256]{1,0:T(8,128)(2,1)S(1)}, u32[]{:S(2)}, u32[]{:S(2)}) collective-permute-start(bf16[32,256]{1,0:T(8,128)(2,1)S(1)} %get-tuple-element.17), channel_id=1, source_target_pairs={{0,1},{1,0},{2,3},{3,2},{4,5},{5,4},{6,7},{7,6},{8,9},{9,8},{10,11... | collective-permute-start | bytes 49160 | tf_op jit(solution)/shard_map/ppermute | solution.py:245
  3.9 2.6 %collective-permute-start.1 = (bf16[32,256]{1,0:T(8,128)(2,1)S(1)}, bf16[32,256]{1,0:T(8,128)(2,1)S(1)}, u32[]{:S(2)}, u32[]{:S(2)}) collective-permute-start(bf16[32,256]{1,0:T(8,128)(2,1)S(1)} %get-tuple-element.18), channel_id=1, source_target_pairs={{0,16},{1,2},{2,1},{3,4},{4,3},{5,6},{6,5},{7,8},{8,7},{9,10},{10,... | collective-permute-start | bytes 49160 | tf_op jit(solution)/shard_map/ppermute | solution.py:245
  6.5 0.1 collective-permute-start.2
  6.5 3.6 %collective-permute-done.2.rest_0_ = bf16[24,256]{1,0:T(8,128)(2,1)S(1)} collective-permute-done((bf16[24,256]{1,0:T(8,128)(2,1)S(1)}, bf16[24,256]{1,0:T(8,128)(2,1)S(1)}, u32[]{:S(2)}, u32[]{:S(2)}) %collective-permute-start.2) | collective-permute-done | bytes 12320 | tf_op jit(solution)/shard_map/ppermute | solution.py:245
  10.1 0.0 collective-permute-done.halo_row_a
  10.2 0.0 collective-permute-done.1.halo_row_b
  10.2 1.4 %shard_map.47 = (bf16[8,64,256]{2,1,0:T(8,128)(2,1)S(1)}, bf16[8,64,256]{2,1,0:T(8,128)(2,1)S(1)}, f32[8,64,256]{2,1,0:T(8,128)S(1)}, f32[8,64,256]{2,1,0:T(8,128)S(1)}) custom-call(bf16[24,32,2048]{2,1,0:T(8,128)(2,1)S(1)} %get-tuple-element.15.masked, bf16[24,32,256]{2,1,0:T(8,128)(2,1)S(1)} %get-tuple-element.16.proj, ...), custom_call_target="tpu_custom_call" | custom-call | flops 805306368 | bytes 3145728 | tf_op jit(solution)/shard_map/pallas_call | solution.py:210
  11.5 0.1 collective-permute-start.8
  11.6 0.5 %collective-permute-start.3 = (bf16[8,64,256]{2,1,0:T(8,128)(2,1)S(1)}, bf16[8,64,256]{2,1,0:T(8,128)(2,1)S(1)}, u32[]{:S(2)}, u32[]{:S(2)}) collective-permute-start(bf16[8,64,256]{2,1,0:T(8,128)(2,1)S(1)} %get-tuple-element.22), channel_id=1, source_target_pairs={{0,1},{1,0},{2,3},{3,2},{4,5},{5,4},{6,7},{7,6},{8,9},{9,8},{10,11... | collective-permute-start | bytes 786440 | tf_op jit(solution)/shard_map/ppermute | solution.py:245
  12.1 1.0 %collective-permute-done.8 = bf16[8,64,256]{2,1,0:T(8,128)(2,1)S(1)} collective-permute-done((bf16[8,64,256]{2,1,0:T(8,128)(2,1)S(1)}, bf16[8,64,256]{2,1,0:T(8,128)(2,1)S(1)}, u32[]{:S(2)}, u32[]{:S(2)}) %collective-permute-start.8) | collective-permute-done | bytes 262176 | tf_op jit(solution)/shard_map/ppermute | solution.py:245
  13.1 0.1 fusion.1
  13.2 0.5 %collective-permute-start.9 = (bf16[4,64,256]{2,1,0:T(8,128)(2,1)S(1)}, bf16[4,64,256]{2,1,0:T(8,128)(2,1)S(1)}, u32[]{:S(2)}, u32[]{:S(2)}) collective-permute-start(bf16[4,64,256]{2,1,0:T(8,128)(2,1)S(1)} %get-tuple-element.27), channel_id=1, source_target_pairs={{0,3},{1,4},{2,7},{3,0},{4,1},{5,6},{6,5},{7,2},{8,13},{9,10},{10,... | collective-permute-start | bytes 393224 | tf_op jit(solution)/shard_map/ppermute | solution.py:245
  13.7 0.0 collective-permute-done.3
  13.7 0.1 fusion
  13.7 1.4 %collective-permute-start.4 = (bf16[4,64,256]{2,1,0:T(8,128)(2,1)S(1)}, bf16[4,64,256]{2,1,0:T(8,128)(2,1)S(1)}, u32[]{:S(2)}, u32[]{:S(2)}) collective-permute-start(bf16[4,64,256]{2,1,0:T(8,128)(2,1)S(1)} %get-tuple-element.25), channel_id=1, source_target_pairs={{0,3},{1,4},{2,7},{3,0},{4,1},{5,6},{6,5},{7,2},{8,13},{9,10},{10,... | collective-permute-start | bytes 393224 | tf_op jit(solution)/shard_map/ppermute | solution.py:245
  15.1 2.5 %collective-permute-done.9 = bf16[4,64,256]{2,1,0:T(8,128)(2,1)S(1)} collective-permute-done((bf16[4,64,256]{2,1,0:T(8,128)(2,1)S(1)}, bf16[4,64,256]{2,1,0:T(8,128)(2,1)S(1)}, u32[]{:S(2)}, u32[]{:S(2)}) %collective-permute-start.9) | collective-permute-done | bytes 131104 | tf_op jit(solution)/shard_map/ppermute | solution.py:245
  17.7 1.6 %collective-permute-start.10 = (bf16[2,64,256]{2,1,0:T(8,128)(2,1)S(1)}, bf16[2,64,256]{2,1,0:T(8,128)(2,1)S(1)}, u32[]{:S(2)}, u32[]{:S(2)}) collective-permute-start(bf16[2,64,256]{2,1,0:T(8,128)(2,1)S(1)} %get-tuple-element.31), channel_id=1, source_target_pairs={{0,5},{1,2},{2,1},{3,6},{4,7},{5,0},{6,3},{7,4},{8,11},{9,12},{10,... | collective-permute-start | bytes 196616 | tf_op jit(solution)/shard_map/ppermute | solution.py:245
  19.3 0.0 collective-permute-done.4
  19.3 1.1 %collective-permute-start.5 = (bf16[2,64,256]{2,1,0:T(8,128)(2,1)S(1)}, bf16[2,64,256]{2,1,0:T(8,128)(2,1)S(1)}, u32[]{:S(2)}, u32[]{:S(2)}) collective-permute-start(bf16[2,64,256]{2,1,0:T(8,128)(2,1)S(1)} %get-tuple-element.29), channel_id=1, source_target_pairs={{0,5},{1,2},{2,1},{3,6},{4,7},{5,0},{6,3},{7,4},{8,11},{9,12},{10,... | collective-permute-start | bytes 196616 | tf_op jit(solution)/shard_map/ppermute | solution.py:245
  20.4 1.0 %collective-permute-done.10 = bf16[2,64,256]{2,1,0:T(8,128)(2,1)S(1)} collective-permute-done((bf16[2,64,256]{2,1,0:T(8,128)(2,1)S(1)}, bf16[2,64,256]{2,1,0:T(8,128)(2,1)S(1)}, u32[]{:S(2)}, u32[]{:S(2)}) %collective-permute-start.10) | collective-permute-done | bytes 65568 | tf_op jit(solution)/shard_map/ppermute | solution.py:245
  21.4 2.6 %collective-permute-start.11 = (bf16[1,64,256]{2,1,0:T(8,128)(2,1)S(1)}, bf16[1,64,256]{2,1,0:T(8,128)(2,1)S(1)}, u32[]{:S(2)}, u32[]{:S(2)}) collective-permute-start(bf16[1,64,256]{2,1,0:T(8,128)(2,1)S(1)} %fusion.4), channel_id=1, source_target_pairs={{0,9},{1,8},{2,11},{3,10},{4,13},{5,12},{6,15},{7,14},{8,1},{9,0},... | collective-permute-start | bytes 98312 | tf_op jit(solution)/shard_map/ppermute | solution.py:245
  24.1 0.0 collective-permute-done.5
  24.1 1.3 %collective-permute-start.6 = (bf16[1,64,256]{2,1,0:T(8,128)(2,1)S(1)}, bf16[1,64,256]{2,1,0:T(8,128)(2,1)S(1)}, u32[]{:S(2)}, u32[]{:S(2)}) collective-permute-start(bf16[1,64,256]{2,1,0:T(8,128)(2,1)S(1)} %fusion.7), channel_id=1, source_target_pairs={{0,9},{1,8},{2,11},{3,10},{4,13},{5,12},{6,15},{7,14},{8,1},{9,0},... | collective-permute-start | bytes 98312 | tf_op jit(solution)/shard_map/ppermute | solution.py:245
  25.4 0.3 collective-permute-done.11
  25.8 1.5 %collective-permute-start.12 = (bf16[64,256]{1,0:T(8,128)(2,1)S(1)}, bf16[64,256]{1,0:T(8,128)(2,1)S(1)}, u32[]{:S(2)}, u32[]{:S(2)}) collective-permute-start(bf16[64,256]{1,0:T(8,128)(2,1)S(1)} %fusion.11), channel_id=1, source_target_pairs={{0,16},{1,17},{2,18},{3,19},{4,20},{5,21},{6,22},{7,23},{8,24},{9,... | collective-permute-start | bytes 98312 | tf_op jit(solution)/shard_map/ppermute | solution.py:245
  27.3 1.2 %collective-permute-done.6 = bf16[1,64,256]{2,1,0:T(8,128)(2,1)S(1)} collective-permute-done((bf16[1,64,256]{2,1,0:T(8,128)(2,1)S(1)}, bf16[1,64,256]{2,1,0:T(8,128)(2,1)S(1)}, u32[]{:S(2)}, u32[]{:S(2)}) %collective-permute-start.6) | collective-permute-done | bytes 32800 | tf_op jit(solution)/shard_map/ppermute | solution.py:245
  28.5 1.6 %collective-permute-start.7 = (bf16[64,256]{1,0:T(8,128)(2,1)S(1)}, bf16[64,256]{1,0:T(8,128)(2,1)S(1)}, u32[]{:S(2)}, u32[]{:S(2)}) collective-permute-start(bf16[64,256]{1,0:T(8,128)(2,1)S(1)} %fusion.10), channel_id=1, source_target_pairs={{0,16},{1,17},{2,18},{3,19},{4,20},{5,21},{6,22},{7,23},{8,24},{9,... | collective-permute-start | bytes 98312 | tf_op jit(solution)/shard_map/ppermute | solution.py:245
  30.1 0.0 collective-permute-done.12
  30.1 2.4 %collective-permute-done.7 = bf16[64,256]{1,0:T(8,128)(2,1)S(1)} collective-permute-done((bf16[64,256]{1,0:T(8,128)(2,1)S(1)}, bf16[64,256]{1,0:T(8,128)(2,1)S(1)}, u32[]{:S(2)}, u32[]{:S(2)}) %collective-permute-start.7) | collective-permute-done | bytes 32800 | tf_op jit(solution)/shard_map/ppermute | solution.py:245
  32.5 0.7 %pad_maximum_fusion = f32[128,256]{1,0:T(8,128)} fusion(f32[64,256]{1,0:T(8,128)S(1)} %add_multiply_fusion, f32[64,256]{1,0:T(8,128)S(1)} %add_multiply_fusion.1), kind=kLoop, calls=%fused_computation.6 | loop fusion | flops 32768 | bytes 262144 | tf_op jit(solution)/shard_map/concatenate | solution.py:280
  (8 shorter events, 0.1 us)
Async XLA Ops:
  3.3 6.8 %collective-permute-start = (bf16[32,256]{1,0:T(8,128)(2,1)S(1)}, bf16[32,256]{1,0:T(8,128)(2,1)S(1)}, u32[]{:S(2)}, u32[]{:S(2)}) collective-permute-start(bf16[32,256]{1,0:T(8,128)(2,1)S(1)} %get-tuple-element.17), channel_id=1, source_target_pairs={{0,1},{1,0},{2,3},{3,2},{4,5},{5,4},{6,7},{7,6},{8,9},{9,8},{10,11... | collective-permute-start | bytes 49160 | tf_op jit(solution)/shard_map/ppermute | solution.py:245
  3.9 6.3 %collective-permute-start.1 = (bf16[32,256]{1,0:T(8,128)(2,1)S(1)}, bf16[32,256]{1,0:T(8,128)(2,1)S(1)}, u32[]{:S(2)}, u32[]{:S(2)}) collective-permute-start(bf16[32,256]{1,0:T(8,128)(2,1)S(1)} %get-tuple-element.18), channel_id=1, source_target_pairs={{0,16},{1,2},{2,1},{3,4},{4,3},{5,6},{6,5},{7,8},{8,7},{9,10},{10,... | collective-permute-start | bytes 49160 | tf_op jit(solution)/shard_map/ppermute | solution.py:245
  6.5 3.7 %collective-permute-start.2 = (bf16[24,256]{1,0:T(8,128)(2,1)S(1)}, bf16[24,256]{1,0:T(8,128)(2,1)S(1)}, u32[]{:S(2)}, u32[]{:S(2)}) collective-permute-start(bf16[24,256]{1,0:T(8,128)(2,1)S(1)} %get-tuple-element.19), channel_id=1, source_target_pairs={{0,16},{1,17},{2,18},{3,19},{4,20},{5,21},{6,22},{7,23},{8,24},{9,... | collective-permute-start | bytes 36872 | tf_op jit(solution)/shard_map/ppermute | solution.py:245
  11.5 1.6 %collective-permute-start.8 = (bf16[8,64,256]{2,1,0:T(8,128)(2,1)S(1)}, bf16[8,64,256]{2,1,0:T(8,128)(2,1)S(1)}, u32[]{:S(2)}, u32[]{:S(2)}) collective-permute-start(bf16[8,64,256]{2,1,0:T(8,128)(2,1)S(1)} %get-tuple-element.24), channel_id=1, source_target_pairs={{0,1},{1,0},{2,3},{3,2},{4,5},{5,4},{6,7},{7,6},{8,9},{9,8},{10,11... | collective-permute-start | bytes 786440 | tf_op jit(solution)/shard_map/ppermute | solution.py:245
  11.6 2.1 %collective-permute-start.3 = (bf16[8,64,256]{2,1,0:T(8,128)(2,1)S(1)}, bf16[8,64,256]{2,1,0:T(8,128)(2,1)S(1)}, u32[]{:S(2)}, u32[]{:S(2)}) collective-permute-start(bf16[8,64,256]{2,1,0:T(8,128)(2,1)S(1)} %get-tuple-element.22), channel_id=1, source_target_pairs={{0,1},{1,0},{2,3},{3,2},{4,5},{5,4},{6,7},{7,6},{8,9},{9,8},{10,11... | collective-permute-start | bytes 786440 | tf_op jit(solution)/shard_map/ppermute | solution.py:245
  13.2 4.5 %collective-permute-start.9 = (bf16[4,64,256]{2,1,0:T(8,128)(2,1)S(1)}, bf16[4,64,256]{2,1,0:T(8,128)(2,1)S(1)}, u32[]{:S(2)}, u32[]{:S(2)}) collective-permute-start(bf16[4,64,256]{2,1,0:T(8,128)(2,1)S(1)} %get-tuple-element.27), channel_id=1, source_target_pairs={{0,3},{1,4},{2,7},{3,0},{4,1},{5,6},{6,5},{7,2},{8,13},{9,10},{10,... | collective-permute-start | bytes 393224 | tf_op jit(solution)/shard_map/ppermute | solution.py:245
  13.7 5.6 %collective-permute-start.4 = (bf16[4,64,256]{2,1,0:T(8,128)(2,1)S(1)}, bf16[4,64,256]{2,1,0:T(8,128)(2,1)S(1)}, u32[]{:S(2)}, u32[]{:S(2)}) collective-permute-start(bf16[4,64,256]{2,1,0:T(8,128)(2,1)S(1)} %get-tuple-element.25), channel_id=1, source_target_pairs={{0,3},{1,4},{2,7},{3,0},{4,1},{5,6},{6,5},{7,2},{8,13},{9,10},{10,... | collective-permute-start | bytes 393224 | tf_op jit(solution)/shard_map/ppermute | solution.py:245
  17.7 3.8 %collective-permute-start.10 = (bf16[2,64,256]{2,1,0:T(8,128)(2,1)S(1)}, bf16[2,64,256]{2,1,0:T(8,128)(2,1)S(1)}, u32[]{:S(2)}, u32[]{:S(2)}) collective-permute-start(bf16[2,64,256]{2,1,0:T(8,128)(2,1)S(1)} %get-tuple-element.31), channel_id=1, source_target_pairs={{0,5},{1,2},{2,1},{3,6},{4,7},{5,0},{6,3},{7,4},{8,11},{9,12},{10,... | collective-permute-start | bytes 196616 | tf_op jit(solution)/shard_map/ppermute | solution.py:245
  19.3 4.8 %collective-permute-start.5 = (bf16[2,64,256]{2,1,0:T(8,128)(2,1)S(1)}, bf16[2,64,256]{2,1,0:T(8,128)(2,1)S(1)}, u32[]{:S(2)}, u32[]{:S(2)}) collective-permute-start(bf16[2,64,256]{2,1,0:T(8,128)(2,1)S(1)} %get-tuple-element.29), channel_id=1, source_target_pairs={{0,5},{1,2},{2,1},{3,6},{4,7},{5,0},{6,3},{7,4},{8,11},{9,12},{10,... | collective-permute-start | bytes 196616 | tf_op jit(solution)/shard_map/ppermute | solution.py:245
  21.4 4.3 %collective-permute-start.11 = (bf16[1,64,256]{2,1,0:T(8,128)(2,1)S(1)}, bf16[1,64,256]{2,1,0:T(8,128)(2,1)S(1)}, u32[]{:S(2)}, u32[]{:S(2)}) collective-permute-start(bf16[1,64,256]{2,1,0:T(8,128)(2,1)S(1)} %fusion.4), channel_id=1, source_target_pairs={{0,9},{1,8},{2,11},{3,10},{4,13},{5,12},{6,15},{7,14},{8,1},{9,0},... | collective-permute-start | bytes 98312 | tf_op jit(solution)/shard_map/ppermute | solution.py:245
  24.1 4.4 %collective-permute-start.6 = (bf16[1,64,256]{2,1,0:T(8,128)(2,1)S(1)}, bf16[1,64,256]{2,1,0:T(8,128)(2,1)S(1)}, u32[]{:S(2)}, u32[]{:S(2)}) collective-permute-start(bf16[1,64,256]{2,1,0:T(8,128)(2,1)S(1)} %fusion.7), channel_id=1, source_target_pairs={{0,9},{1,8},{2,11},{3,10},{4,13},{5,12},{6,15},{7,14},{8,1},{9,0},... | collective-permute-start | bytes 98312 | tf_op jit(solution)/shard_map/ppermute | solution.py:245
  25.8 4.3 %collective-permute-start.12 = (bf16[64,256]{1,0:T(8,128)(2,1)S(1)}, bf16[64,256]{1,0:T(8,128)(2,1)S(1)}, u32[]{:S(2)}, u32[]{:S(2)}) collective-permute-start(bf16[64,256]{1,0:T(8,128)(2,1)S(1)} %fusion.11), channel_id=1, source_target_pairs={{0,16},{1,17},{2,18},{3,19},{4,20},{5,21},{6,22},{7,23},{8,24},{9,... | collective-permute-start | bytes 98312 | tf_op jit(solution)/shard_map/ppermute | solution.py:245
  28.5 4.0 %collective-permute-start.7 = (bf16[64,256]{1,0:T(8,128)(2,1)S(1)}, bf16[64,256]{1,0:T(8,128)(2,1)S(1)}, u32[]{:S(2)}, u32[]{:S(2)}) collective-permute-start(bf16[64,256]{1,0:T(8,128)(2,1)S(1)} %fusion.10), channel_id=1, source_target_pairs={{0,16},{1,17},{2,18},{3,19},{4,20},{5,21},{6,22},{7,23},{8,24},{9,... | collective-permute-start | bytes 98312 | tf_op jit(solution)/shard_map/ppermute | solution.py:245

commit v5 on v4

--- a/solution.py
+++ b/solution.py
@@ -15,7 +15,6 @@
 IN_VMEM = pl.BlockSpec(memory_space=pltpu.VMEM)
 KERNEL_VMEM = 24 << 20
 WORD_CHUNKS = (0.375, 0.375, 0.25)
-CHUNKS = 2
 
 
 def word_chunks(words):
@@ -135,29 +134,33 @@
 
 def half_blocks(orders, sent, masked, values, outs):
     lat, lon, words = masked.shape
-    slots, rows = outs[0].shape[:2]
-    share = rows * len(outs)
+    places, share = outs[0].shape[:2]
+    tile = lax.axis_index("tile")
     half = tile_parity() ^ sent
+    own = jnp.where(half == 0, tile_bit(tile, orders[0][-1]), tile_bit(tile, orders[1][-1]))
     contract = (((0,), (0,)), ((), ()))
-
-    def put(slot, term):
-        for k, out in enumerate(outs):
-            out[slot] = term[k * rows:(k + 1) * rows].astype(out.dtype)
-
     if share % 128 == 0:
         count = max(1, 256 // share)
-        for slot in range(0, slots, count):
-            parts = []
-            for at in range(slot, slot + count):
-                first = jnp.where(half == 0, block_of(orders[0], 0, at), block_of(orders[1], 1, at)) * share
-                part = masked[:, :, pl.ds(pl.multiple_of(first, share), share)]
-                parts.append(part.reshape(lat * lon, share))
-            part = jnp.concatenate(parts, axis=1) if count > 1 else parts[0]
-            term = lax.dot_general(part, values, contract, preferred_element_type=F32)
-            for at in range(count):
-                put(slot + at, term[at * share:(at + 1) * share])
+        for forward, out in ((1, outs[0]), (0, outs[1])):
+            last = own ^ forward
+            for place in range(0, places, count):
+                parts = []
+                for at in range(place, place + count):
+                    block = [[block_of(order, h, 2 * at + low) for low in (0, 1)] for h, order in enumerate(orders)]
+                    first = jnp.where(
+                        half == 0,
+                        jnp.where(last == 0, block[0][0], block[0][1]),
+                        jnp.where(last == 0, block[1][0], block[1][1]),
+                    ) * share
+                    part = masked[:, :, pl.ds(pl.multiple_of(first, share), share)]
+                    parts.append(part.reshape(lat * lon, share))
+                part = jnp.concatenate(parts, axis=1) if count > 1 else parts[0]
+                term = lax.dot_general(part, values, contract, preferred_element_type=F32)
+                out[pl.ds(place, count)] = term.astype(out.dtype).reshape(count, share, -1)
         return
-    slot_of = [{block_of(order, h, at) // 2: at for at in range(slots)} for h, order in enumerate(orders)]
+    slot_of = [
+        {block_of(order, h, at) // 2: at for at in range(2 * places)} for h, order in enumerate(orders)
+    ]
     step = 256
     for first in range(0, words, step):
         part = masked[:, :, pl.ds(first, step)].reshape(lat * lon, step)
@@ -166,14 +169,24 @@
             pair = (first + at) // (2 * share)
             odd = bin(pair).count("1") & 1
             low, high = term[at:at + share], term[at + share:at + 2 * share]
-            put(jnp.where(half == 0, slot_of[0][pair], slot_of[1][pair]), jnp.where(half == odd, low, high))
+            value = jnp.where(half == odd, low, high)
+            slot = jnp.where(half == 0, slot_of[0][pair], slot_of[1][pair])
+            for forward, out in ((1, outs[0]), (0, outs[1])):
+
+                @pl.when(lax.rem(slot, 2) == own ^ forward)
+                def _():
+                    out[lax.div(slot, 2)] = value.astype(out.dtype)
+
+
+def tile_bit(tile, bit):
+    return lax.rem(lax.shift_right_logical(tile, bit), 2)
 
 
 def tile_parity():
     tile = lax.axis_index("tile")
     parity = lax.rem(tile, 2)
     for bit in range(1, (lax.axis_size("tile") - 1).bit_length()):
-        parity = parity ^ lax.rem(lax.shift_right_logical(tile, bit), 2)
+        parity = parity ^ tile_bit(tile, bit)
     return parity
 
 
@@ -184,7 +197,7 @@
 
 def partial_kernel(orders, masked, proj, halo_row_a, halo_row_b, *rest):
     *rest, smooth = rest
-    rest, sends, keeps = rest[:-2 * CHUNKS], rest[-2 * CHUNKS:-CHUNKS], rest[-CHUNKS:]
+    rest, sends, keeps = rest[:-4], rest[-4:-2], rest[-2:]
     *halo_cols, shares = rest
     row_a, row_b = halo_row_a[...].astype(F32), halo_row_b[...].astype(F32)
     odd = lax.rem(lax.axis_index("tile"), 2)
@@ -206,19 +219,19 @@
 def partial_product(orders, share, masked, proj, rows, cols, shares):
     lat, lon, words = masked.shape
     rank = proj.shape[2]
-    shape = (words // share // 2, share // CHUNKS, rank)
+    shape = (words // share // 4, share, rank)
     outs = pl.pallas_call(
         functools.partial(partial_kernel, orders),
-        out_shape=(pltpu.VMEM(shape, BF16),) * CHUNKS + (pltpu.VMEM(shape, F32),) * CHUNKS,
+        out_shape=(pltpu.VMEM(shape, BF16),) * 2 + (pltpu.VMEM(shape, F32),) * 2,
         in_specs=[IN_VMEM] * (5 + len(cols)),
-        out_specs=(IN_VMEM,) * (2 * CHUNKS),
+        out_specs=(IN_VMEM,) * 4,
         scratch_shapes=[pltpu.VMEM((lat * lon, rank), BF16)],
         compiler_params=pltpu.CompilerParams(vmem_limit_bytes=KERNEL_VMEM),
         cost_estimate=pl.CostEstimate(
             flops=2 * lat * lon * words * rank, bytes_accessed=2 * lat * lon * words, transcendentals=0
         ),
     )(masked, proj, *rows, *cols, shares)
-    return outs[:CHUNKS], outs[CHUNKS:]
+    return outs[:2], outs[2:]
 
 
 def bit_orders(bits):
@@ -258,26 +271,29 @@
     parity = tile_parity()
     pick = functools.partial(lax.dynamic_index_in_dim, axis=0, keepdims=False)
 
+    def partner_at(j):
+        return lambda g, t: (g, t ^ (1 << orders[bin(t).count("1") & 1][j]) ^ 1)
+
     def reduced(held, send):
         got = exchange(send, lambda g, t: (g, t ^ 1))
-        for j in range(bits - 1):
-            bit = jnp.where(parity == 0, orders[0][j], orders[1][j])
-            mine = lax.rem(lax.shift_right_logical(tile, bit), 2)
+        for j in range(bits - 2):
+            mine = jnp.where(parity == 0, tile_bit(tile, orders[0][j]), tile_bit(tile, orders[1][j]))
             halves = (2, held.shape[0] // 2) + held.shape[1:]
             held, got = held.reshape(halves), got.reshape(halves)
             send = (pick(held, 1 - mine) + pick(got, 1 - mine).astype(F32)).astype(BF16)
             held = pick(held, mine) + pick(got, mine).astype(F32)
-            got = exchange(send, lambda g, t: (g, t ^ (1 << orders[bin(t).count("1") & 1][j]) ^ 1))
-        total = held[0] + got[0].astype(F32)
-        step = 1
-        while step < groups:
-            send = total.astype(BF16)
-            got = exchange(send, lambda g, t: (g ^ step, t))
-            total = send.astype(F32) + got.astype(F32)
-            step *= 2
-        return total * (1.0 / math.sqrt(lat * lon * groups * tiles))
-
-    return jnp.concatenate([reduced(held, send) for held, send in zip(keeps, sends)], axis=0)
+            got = exchange(send, partner_at(j))
+        return held[0] + got[0].astype(F32)
+
+    forward = exchange(reduced(keeps[0], sends[0]).astype(BF16), partner_at(bits - 2))
+    total = reduced(keeps[1], sends[1]) + forward.astype(F32)
+    step = 1
+    while step < groups:
+        send = total.astype(BF16)
+        got = exchange(send, lambda g, t: (g ^ step, t))
+        total = send.astype(F32) + got.astype(F32)
+        step *= 2
+    return total * (1.0 / math.sqrt(lat * lon * groups * tiles))
 
 
 def solution(mesh):

time: 33.3 us -> 31.7 us (0.952); the launches traced: 33.2 us -> 31.2 us
  starting transfers between devices: 15.4 us -> 12.7 us
  waiting for transfers between devices: 12.1 us -> 12.9 us
    ppermute x13 -> x11, starting transfers between devices: 15.4 us -> 12.7 us  [exchange(): return lax.ppermute(values, AXES, pairs)]
    ppermute x13 -> x11, waiting for transfers between devices: 12.1 us -> 12.9 us  [exchange(): return lax.ppermute(values, AXES, pairs)]
    concatenate x1 -> x0, other arithmetic: 0.67 us -> none  [per_device(): jnp.concatenate([reduced(held, send) for held, send in zip(keeps, sends)]...]
    mul x2 -> x1, other arithmetic: 0.02 us -> 0.68 us  [per_device(): return total * (1.0 / math.sqrt(lat * lon * groups * tiles))]
  transfers between devices with their start and end apart: 13 -> 11, of which waited for: 7 -> 6; matrix products, arithmetic and copies ran while one was open for 1% -> 1% of each run, Pallas kernels for 0% -> 0%
where the time goes in v5:
time: 31.7 us; the launch traced here: 31.2 us
  waiting for transfers between devices  12.9 us (41%)
  starting transfers between devices  12.7 us (40%)
  Pallas kernels  4.69 us (15%)
  other arithmetic  0.87 us (3%)
    ppermute x11, waiting for transfers between devices, exchange(): return lax.ppermute(values, AXES, pairs)  12.9 us
    ppermute x11, starting transfers between devices, exchange(): return lax.ppermute(values, AXES, pairs)  12.7 us
    pallas_call x1, Pallas kernels, project(): pl.pallas_call(project_kernel, out_shape=(pltpu.VMEM((lat, lon, words), B...  3.33 us
    pallas_call x1, Pallas kernels, partial_product(): pl.pallas_call(functools.partial(partial_kernel, orders), out_shape=(pltp...  1.36 us
    mul x1, other arithmetic, per_device(): return total * (1.0 / math.sqrt(lat * lon * groups * tiles))  0.68 us
  transfers between devices with their start and end apart: 11, of which 6 were waited for; matrix products, arithmetic and copies ran while one was open for 1% of the time, Pallas kernels for 0%

profile of v5, /device:TPU:0, one launch (start us, length us, event | category | flops | bytes accessed | tf_op | source)
XLA Modules:
  0.0 31.2 jit_solution(7235686305584722125)
XLA Ops:
  0.0 3.3 %shard_map.46 = (bf16[24,32,2048]{2,1,0:T(8,128)(2,1)S(1)}, bf16[24,32,256]{2,1,0:T(8,128)(2,1)S(1)}, f32[4,768,128]{2,1,0:T(8,128)S(1)}, bf16[32,256]{1,0:T(8,1...) custom-call(s32[12,1,16]{2,1,0:T(1,128)} %occ_hbm.1, s32[4,24,32]{2,1,0:T(8,128)} %links_hbm.1, ...), custom_call_target="tpu_custom_call" | custom-call | flops 805306368 | bytes 3145728 | tf_op jit(solution)/shard_map/pallas_call | solution.py:89
  3.3 0.6 %collective-permute-start = (bf16[32,256]{1,0:T(8,128)(2,1)S(1)}, bf16[32,256]{1,0:T(8,128)(2,1)S(1)}, u32[]{:S(2)}, u32[]{:S(2)}) collective-permute-start(bf16[32,256]{1,0:T(8,128)(2,1)S(1)} %get-tuple-element.17), channel_id=1, source_target_pairs={{0,1},{1,0},{2,3},{3,2},{4,5},{5,4},{6,7},{7,6},{8,9},{9,8},{10,11... | collective-permute-start | bytes 49160 | tf_op jit(solution)/shard_map/ppermute | solution.py:258
  3.9 2.6 %collective-permute-start.1 = (bf16[32,256]{1,0:T(8,128)(2,1)S(1)}, bf16[32,256]{1,0:T(8,128)(2,1)S(1)}, u32[]{:S(2)}, u32[]{:S(2)}) collective-permute-start(bf16[32,256]{1,0:T(8,128)(2,1)S(1)} %get-tuple-element.18), channel_id=1, source_target_pairs={{0,16},{1,2},{2,1},{3,4},{4,3},{5,6},{6,5},{7,8},{8,7},{9,10},{10,... | collective-permute-start | bytes 49160 | tf_op jit(solution)/shard_map/ppermute | solution.py:258
  6.5 0.1 collective-permute-start.2
  6.5 3.6 %collective-permute-done.2.rest_0_ = bf16[24,256]{1,0:T(8,128)(2,1)S(1)} collective-permute-done((bf16[24,256]{1,0:T(8,128)(2,1)S(1)}, bf16[24,256]{1,0:T(8,128)(2,1)S(1)}, u32[]{:S(2)}, u32[]{:S(2)}) %collective-permute-start.2) | collective-permute-done | bytes 12320 | tf_op jit(solution)/shard_map/ppermute | solution.py:258
  10.1 0.0 collective-permute-done.halo_row_a
  10.2 0.0 collective-permute-done.1.halo_row_b
  10.2 1.4 %shard_map.47 = (bf16[4,128,256]{2,1,0:T(8,128)(2,1)S(1)}, bf16[4,128,256]{2,1,0:T(8,128)(2,1)S(1)}, f32[4,128,256]{2,1,0:T(8,128)S(1)}, f32[4,128,256]{2,1,0:T(8,128)S(1)}) custom-call(bf16[24,32,2048]{2,1,0:T(8,128)(2,1)S(1)} %get-tuple-element.15.masked, bf16[24,32,256]{2,1,0:T(8,128)(2,1)S(1)} %get-tuple-element.16.proj, ...), custom_call_target="tpu_custom_call" | custom-call | flops 805306368 | bytes 3145728 | tf_op jit(solution)/shard_map/pallas_call | solution.py:223
  11.5 0.1 collective-permute-start.6
  11.6 0.5 %collective-permute-start.3 = (bf16[4,128,256]{2,1,0:T(8,128)(2,1)S(1)}, bf16[4,128,256]{2,1,0:T(8,128)(2,1)S(1)}, u32[]{:S(2)}, u32[]{:S(2)}) collective-permute-start(bf16[4,128,256]{2,1,0:T(8,128)(2,1)S(1)} %get-tuple-element.22), channel_id=1, source_target_pairs={{0,1},{1,0},{2,3},{3,2},{4,5},{5,4},{6,7},{7,6},{8,9},{9,8},{10,11... | collective-permute-start | bytes 786440 | tf_op jit(solution)/shard_map/ppermute | solution.py:258
  12.1 1.0 %collective-permute-done.6 = bf16[4,128,256]{2,1,0:T(8,128)(2,1)S(1)} collective-permute-done((bf16[4,128,256]{2,1,0:T(8,128)(2,1)S(1)}, bf16[4,128,256]{2,1,0:T(8,128)(2,1)S(1)}, u32[]{:S(2)}, u32[]{:S(2)}) %collective-permute-start.6) | collective-permute-done | bytes 262176 | tf_op jit(solution)/shard_map/ppermute | solution.py:258
  13.1 0.1 fusion.1
  13.2 0.5 %collective-permute-start.7 = (bf16[2,128,256]{2,1,0:T(8,128)(2,1)S(1)}, bf16[2,128,256]{2,1,0:T(8,128)(2,1)S(1)}, u32[]{:S(2)}, u32[]{:S(2)}) collective-permute-start(bf16[2,128,256]{2,1,0:T(8,128)(2,1)S(1)} %get-tuple-element.27), channel_id=1, source_target_pairs={{0,3},{1,4},{2,7},{3,0},{4,1},{5,6},{6,5},{7,2},{8,13},{9,10},{10,... | collective-permute-start | bytes 393224 | tf_op jit(solution)/shard_map/ppermute | solution.py:258
  13.7 0.0 collective-permute-done.3
  13.7 0.1 fusion
  13.7 1.4 %collective-permute-start.4 = (bf16[2,128,256]{2,1,0:T(8,128)(2,1)S(1)}, bf16[2,128,256]{2,1,0:T(8,128)(2,1)S(1)}, u32[]{:S(2)}, u32[]{:S(2)}) collective-permute-start(bf16[2,128,256]{2,1,0:T(8,128)(2,1)S(1)} %get-tuple-element.25), channel_id=1, source_target_pairs={{0,3},{1,4},{2,7},{3,0},{4,1},{5,6},{6,5},{7,2},{8,13},{9,10},{10,... | collective-permute-start | bytes 393224 | tf_op jit(solution)/shard_map/ppermute | solution.py:258
  15.1 2.5 %collective-permute-done.7 = bf16[2,128,256]{2,1,0:T(8,128)(2,1)S(1)} collective-permute-done((bf16[2,128,256]{2,1,0:T(8,128)(2,1)S(1)}, bf16[2,128,256]{2,1,0:T(8,128)(2,1)S(1)}, u32[]{:S(2)}, u32[]{:S(2)}) %collective-permute-start.7) | collective-permute-done | bytes 131104 | tf_op jit(solution)/shard_map/ppermute | solution.py:258
  17.7 1.6 %collective-permute-start.8 = (bf16[1,128,256]{2,1,0:T(8,128)(2,1)S(1)}, bf16[1,128,256]{2,1,0:T(8,128)(2,1)S(1)}, u32[]{:S(2)}, u32[]{:S(2)}) collective-permute-start(bf16[1,128,256]{2,1,0:T(8,128)(2,1)S(1)} %fusion.2), channel_id=1, source_target_pairs={{0,5},{1,2},{2,1},{3,6},{4,7},{5,0},{6,3},{7,4},{8,11},{9,12},{10,... | collective-permute-start | bytes 196616 | tf_op jit(solution)/shard_map/ppermute | solution.py:258
  19.3 0.0 collective-permute-done.4
  19.3 1.1 %collective-permute-start.5 = (bf16[1,128,256]{2,1,0:T(8,128)(2,1)S(1)}, bf16[1,128,256]{2,1,0:T(8,128)(2,1)S(1)}, u32[]{:S(2)}, u32[]{:S(2)}) collective-permute-start(bf16[1,128,256]{2,1,0:T(8,128)(2,1)S(1)} %fusion.6), channel_id=1, source_target_pairs={{0,5},{1,2},{2,1},{3,6},{4,7},{5,0},{6,3},{7,4},{8,11},{9,12},{10,... | collective-permute-start | bytes 196616 | tf_op jit(solution)/shard_map/ppermute | solution.py:258
  20.4 1.0 %collective-permute-done.8 = bf16[1,128,256]{2,1,0:T(8,128)(2,1)S(1)} collective-permute-done((bf16[1,128,256]{2,1,0:T(8,128)(2,1)S(1)}, bf16[1,128,256]{2,1,0:T(8,128)(2,1)S(1)}, u32[]{:S(2)}, u32[]{:S(2)}) %collective-permute-start.8) | collective-permute-done | bytes 65568 | tf_op jit(solution)/shard_map/ppermute | solution.py:258
  21.4 2.7 %collective-permute-start.9 = (bf16[128,256]{1,0:T(8,128)(2,1)S(1)}, bf16[128,256]{1,0:T(8,128)(2,1)S(1)}, u32[]{:S(2)}, u32[]{:S(2)}) collective-permute-start(bf16[128,256]{1,0:T(8,128)(2,1)S(1)} %fusion.8), channel_id=1, source_target_pairs={{0,9},{1,8},{2,11},{3,10},{4,13},{5,12},{6,15},{7,14},{8,1},{9,0},... | collective-permute-start | bytes 196616 | tf_op jit(solution)/shard_map/ppermute | solution.py:258
  24.1 0.0 collective-permute-done.5
  24.1 2.1 %collective-permute-done.9 = bf16[128,256]{1,0:T(8,128)(2,1)S(1)} collective-permute-done((bf16[128,256]{1,0:T(8,128)(2,1)S(1)}, bf16[128,256]{1,0:T(8,128)(2,1)S(1)}, u32[]{:S(2)}, u32[]{:S(2)}) %collective-permute-start.9) | collective-permute-done | bytes 65568 | tf_op jit(solution)/shard_map/ppermute | solution.py:258
  26.2 1.7 %collective-permute-start.10 = (bf16[128,256]{1,0:T(8,128)(2,1)S(1)}, bf16[128,256]{1,0:T(8,128)(2,1)S(1)}, u32[]{:S(2)}, u32[]{:S(2)}) collective-permute-start(bf16[128,256]{1,0:T(8,128)(2,1)S(1)} %fusion.5), channel_id=1, source_target_pairs={{0,16},{1,17},{2,18},{3,19},{4,20},{5,21},{6,22},{7,23},{8,24},{9,... | collective-permute-start | bytes 196616 | tf_op jit(solution)/shard_map/ppermute | solution.py:258
  27.9 2.7 %collective-permute-done.10 = bf16[128,256]{1,0:T(8,128)(2,1)S(1)} collective-permute-done((bf16[128,256]{1,0:T(8,128)(2,1)S(1)}, bf16[128,256]{1,0:T(8,128)(2,1)S(1)}, u32[]{:S(2)}, u32[]{:S(2)}) %collective-permute-start.10) | collective-permute-done | bytes 65568 | tf_op jit(solution)/shard_map/ppermute | solution.py:258
  30.6 0.7 %add_multiply_fusion = f32[128,256]{1,0:T(8,128)} fusion(bf16[128,256]{1,0:T(8,128)(2,1)S(1)} %collective-permute-done.10, bf16[128,256]{1,0:T(8,128)(2,1)S(1)} %fusion.5), kind=kLoop, calls=%fused_computation.17 | loop fusion | flops 131072 | bytes 262144 | tf_op jit(solution)/shard_map/mul | solution.py:296
  (4 shorter events, 0.1 us)
Async XLA Ops:
  3.3 6.8 %collective-permute-start = (bf16[32,256]{1,0:T(8,128)(2,1)S(1)}, bf16[32,256]{1,0:T(8,128)(2,1)S(1)}, u32[]{:S(2)}, u32[]{:S(2)}) collective-permute-start(bf16[32,256]{1,0:T(8,128)(2,1)S(1)} %get-tuple-element.17), channel_id=1, source_target_pairs={{0,1},{1,0},{2,3},{3,2},{4,5},{5,4},{6,7},{7,6},{8,9},{9,8},{10,11... | collective-permute-start | bytes 49160 | tf_op jit(solution)/shard_map/ppermute | solution.py:258
  3.9 6.3 %collective-permute-start.1 = (bf16[32,256]{1,0:T(8,128)(2,1)S(1)}, bf16[32,256]{1,0:T(8,128)(2,1)S(1)}, u32[]{:S(2)}, u32[]{:S(2)}) collective-permute-start(bf16[32,256]{1,0:T(8,128)(2,1)S(1)} %get-tuple-element.18), channel_id=1, source_target_pairs={{0,16},{1,2},{2,1},{3,4},{4,3},{5,6},{6,5},{7,8},{8,7},{9,10},{10,... | collective-permute-start | bytes 49160 | tf_op jit(solution)/shard_map/ppermute | solution.py:258
  6.5 3.7 %collective-permute-start.2 = (bf16[24,256]{1,0:T(8,128)(2,1)S(1)}, bf16[24,256]{1,0:T(8,128)(2,1)S(1)}, u32[]{:S(2)}, u32[]{:S(2)}) collective-permute-start(bf16[24,256]{1,0:T(8,128)(2,1)S(1)} %get-tuple-element.19), channel_id=1, source_target_pairs={{0,16},{1,17},{2,18},{3,19},{4,20},{5,21},{6,22},{7,23},{8,24},{9,... | collective-permute-start | bytes 36872 | tf_op jit(solution)/shard_map/ppermute | solution.py:258
  11.5 1.6 %collective-permute-start.6 = (bf16[4,128,256]{2,1,0:T(8,128)(2,1)S(1)}, bf16[4,128,256]{2,1,0:T(8,128)(2,1)S(1)}, u32[]{:S(2)}, u32[]{:S(2)}) collective-permute-start(bf16[4,128,256]{2,1,0:T(8,128)(2,1)S(1)} %get-tuple-element.24), channel_id=1, source_target_pairs={{0,1},{1,0},{2,3},{3,2},{4,5},{5,4},{6,7},{7,6},{8,9},{9,8},{10,11... | collective-permute-start | bytes 786440 | tf_op jit(solution)/shard_map/ppermute | solution.py:258
  11.6 2.1 %collective-permute-start.3 = (bf16[4,128,256]{2,1,0:T(8,128)(2,1)S(1)}, bf16[4,128,256]{2,1,0:T(8,128)(2,1)S(1)}, u32[]{:S(2)}, u32[]{:S(2)}) collective-permute-start(bf16[4,128,256]{2,1,0:T(8,128)(2,1)S(1)} %get-tuple-element.22), channel_id=1, source_target_pairs={{0,1},{1,0},{2,3},{3,2},{4,5},{5,4},{6,7},{7,6},{8,9},{9,8},{10,11... | collective-permute-start | bytes 786440 | tf_op jit(solution)/shard_map/ppermute | solution.py:258
  13.2 4.5 %collective-permute-start.7 = (bf16[2,128,256]{2,1,0:T(8,128)(2,1)S(1)}, bf16[2,128,256]{2,1,0:T(8,128)(2,1)S(1)}, u32[]{:S(2)}, u32[]{:S(2)}) collective-permute-start(bf16[2,128,256]{2,1,0:T(8,128)(2,1)S(1)} %get-tuple-element.27), channel_id=1, source_target_pairs={{0,3},{1,4},{2,7},{3,0},{4,1},{5,6},{6,5},{7,2},{8,13},{9,10},{10,... | collective-permute-start | bytes 393224 | tf_op jit(solution)/shard_map/ppermute | solution.py:258
  13.7 5.6 %collective-permute-start.4 = (bf16[2,128,256]{2,1,0:T(8,128)(2,1)S(1)}, bf16[2,128,256]{2,1,0:T(8,128)(2,1)S(1)}, u32[]{:S(2)}, u32[]{:S(2)}) collective-permute-start(bf16[2,128,256]{2,1,0:T(8,128)(2,1)S(1)} %get-tuple-element.25), channel_id=1, source_target_pairs={{0,3},{1,4},{2,7},{3,0},{4,1},{5,6},{6,5},{7,2},{8,13},{9,10},{10,... | collective-permute-start | bytes 393224 | tf_op jit(solution)/shard_map/ppermute | solution.py:258
  17.7 3.8 %collective-permute-start.8 = (bf16[1,128,256]{2,1,0:T(8,128)(2,1)S(1)}, bf16[1,128,256]{2,1,0:T(8,128)(2,1)S(1)}, u32[]{:S(2)}, u32[]{:S(2)}) collective-permute-start(bf16[1,128,256]{2,1,0:T(8,128)(2,1)S(1)} %fusion.2), channel_id=1, source_target_pairs={{0,5},{1,2},{2,1},{3,6},{4,7},{5,0},{6,3},{7,4},{8,11},{9,12},{10,... | collective-permute-start | bytes 196616 | tf_op jit(solution)/shard_map/ppermute | solution.py:258
  19.3 4.8 %collective-permute-start.5 = (bf16[1,128,256]{2,1,0:T(8,128)(2,1)S(1)}, bf16[1,128,256]{2,1,0:T(8,128)(2,1)S(1)}, u32[]{:S(2)}, u32[]{:S(2)}) collective-permute-start(bf16[1,128,256]{2,1,0:T(8,128)(2,1)S(1)} %fusion.6), channel_id=1, source_target_pairs={{0,5},{1,2},{2,1},{3,6},{4,7},{5,0},{6,3},{7,4},{8,11},{9,12},{10,... | collective-permute-start | bytes 196616 | tf_op jit(solution)/shard_map/ppermute | solution.py:258
  21.4 4.7 %collective-permute-start.9 = (bf16[128,256]{1,0:T(8,128)(2,1)S(1)}, bf16[128,256]{1,0:T(8,128)(2,1)S(1)}, u32[]{:S(2)}, u32[]{:S(2)}) collective-permute-start(bf16[128,256]{1,0:T(8,128)(2,1)S(1)} %fusion.8), channel_id=1, source_target_pairs={{0,9},{1,8},{2,11},{3,10},{4,13},{5,12},{6,15},{7,14},{8,1},{9,0},... | collective-permute-start | bytes 196616 | tf_op jit(solution)/shard_map/ppermute | solution.py:258
  26.2 4.3 %collective-permute-start.10 = (bf16[128,256]{1,0:T(8,128)(2,1)S(1)}, bf16[128,256]{1,0:T(8,128)(2,1)S(1)}, u32[]{:S(2)}, u32[]{:S(2)}) collective-permute-start(bf16[128,256]{1,0:T(8,128)(2,1)S(1)} %fusion.5), channel_id=1, source_target_pairs={{0,16},{1,17},{2,18},{3,19},{4,20},{5,21},{6,22},{7,23},{8,24},{9,... | collective-permute-start | bytes 196616 | tf_op jit(solution)/shard_map/ppermute | solution.py:258

commit v6 on v5

--- a/solution.py
+++ b/solution.py
@@ -235,8 +235,9 @@
 
 
 def bit_orders(bits):
-    plain = list(range(1, bits))
-    turned = plain[1::-1] + plain[2:]
+    base = list(range(1, bits))
+    plain = base[:1] + base[:0:-1]
+    turned = base[1::-1] + base[2:]
     return plain, turned
 
 
@@ -285,14 +286,22 @@
             got = exchange(send, partner_at(j))
         return held[0] + got[0].astype(F32)
 
-    forward = exchange(reduced(keeps[0], sends[0]).astype(BF16), partner_at(bits - 2))
-    total = reduced(keeps[1], sends[1]) + forward.astype(F32)
-    step = 1
-    while step < groups:
-        send = total.astype(BF16)
-        got = exchange(send, lambda g, t: (g ^ step, t))
-        total = send.astype(F32) + got.astype(F32)
-        step *= 2
+    onward = reduced(keeps[0], sends[0]).astype(BF16)
+    partner = partner_at(bits - 2)
+    forward = exchange(onward, partner)
+    if groups == 2:
+        across = exchange(onward, lambda g, t: (g ^ 1, partner(g, t)[1]))
+        own = reduced(keeps[1], sends[1]).astype(BF16)
+        other = exchange(own, lambda g, t: (g ^ 1, t))
+        total = (own.astype(F32) + other.astype(F32)) + (forward.astype(F32) + across.astype(F32))
+    else:
+        total = reduced(keeps[1], sends[1]) + forward.astype(F32)
+        step = 1
+        while step < groups:
+            send = total.astype(BF16)
+            got = exchange(send, lambda g, t: (g ^ step, t))
+            total = send.astype(F32) + got.astype(F32)
+            step *= 2
     return total * (1.0 / math.sqrt(lat * lon * groups * tiles))
 
 

time: 31.7 us -> 30.7 us (0.968); the launches traced: 31.2 us -> 30.6 us
  waiting for transfers between devices: 12.9 us -> 11.3 us
  starting transfers between devices: 12.7 us -> 13.6 us
    ppermute x11 -> x12, waiting for transfers between devices: 12.9 us -> 11.3 us  [exchange(): return lax.ppermute(values, AXES, pairs)]
    ppermute x11 -> x12, starting transfers between devices: 12.7 us -> 13.6 us  [exchange(): return lax.ppermute(values, AXES, pairs)]
  transfers between devices with their start and end apart: 11 -> 12, of which waited for: 6 -> 7; matrix products, arithmetic and copies ran while one was open for 1% -> 1% of each run, Pallas kernels for 0% -> 0%
where the time goes in v6:
time: 30.7 us; the launch traced here: 30.6 us
  starting transfers between devices  13.6 us (44%)
  waiting for transfers between devices  11.3 us (37%)
  Pallas kernels  4.7 us (15%)
  other arithmetic  0.88 us (3%)
    ppermute x12, starting transfers between devices, exchange(): return lax.ppermute(values, AXES, pairs)  13.6 us
    ppermute x12, waiting for transfers between devices, exchange(): return lax.ppermute(values, AXES, pairs)  11.3 us
    pallas_call x1, Pallas kernels, project(): pl.pallas_call(project_kernel, out_shape=(pltpu.VMEM((lat, lon, words), B...  3.33 us
    pallas_call x1, Pallas kernels, partial_product(): pl.pallas_call(functools.partial(partial_kernel, orders), out_shape=(pltp...  1.36 us
    mul x1, other arithmetic, per_device(): return total * (1.0 / math.sqrt(lat * lon * groups * tiles))  0.69 us
  transfers between devices with their start and end apart: 12, of which 7 were waited for; matrix products, arithmetic and copies ran while one was open for 1% of the time, Pallas kernels for 0%

profile of v6, /device:TPU:0, one launch (start us, length us, event | category | flops | bytes accessed | tf_op | source)
XLA Modules:
  0.0 30.6 jit_solution(4177569962867613352)
XLA Ops:
  0.0 3.3 %shard_map.46 = (bf16[24,32,2048]{2,1,0:T(8,128)(2,1)S(1)}, bf16[24,32,256]{2,1,0:T(8,128)(2,1)S(1)}, f32[4,768,128]{2,1,0:T(8,128)S(1)}, bf16[32,256]{1,0:T(8,1...) custom-call(s32[12,1,16]{2,1,0:T(1,128)} %occ_hbm.1, s32[4,24,32]{2,1,0:T(8,128)} %links_hbm.1, ...), custom_call_target="tpu_custom_call" | custom-call | flops 805306368 | bytes 3145728 | tf_op jit(solution)/shard_map/pallas_call | solution.py:89
  3.3 0.6 %collective-permute-start = (bf16[32,256]{1,0:T(8,128)(2,1)S(1)}, bf16[32,256]{1,0:T(8,128)(2,1)S(1)}, u32[]{:S(2)}, u32[]{:S(2)}) collective-permute-start(bf16[32,256]{1,0:T(8,128)(2,1)S(1)} %get-tuple-element.17), channel_id=1, source_target_pairs={{0,1},{1,0},{2,3},{3,2},{4,5},{5,4},{6,7},{7,6},{8,9},{9,8},{10,11... | collective-permute-start | bytes 49160 | tf_op jit(solution)/shard_map/ppermute | solution.py:259
  3.9 2.6 %collective-permute-start.1 = (bf16[32,256]{1,0:T(8,128)(2,1)S(1)}, bf16[32,256]{1,0:T(8,128)(2,1)S(1)}, u32[]{:S(2)}, u32[]{:S(2)}) collective-permute-start(bf16[32,256]{1,0:T(8,128)(2,1)S(1)} %get-tuple-element.18), channel_id=1, source_target_pairs={{0,16},{1,2},{2,1},{3,4},{4,3},{5,6},{6,5},{7,8},{8,7},{9,10},{10,... | collective-permute-start | bytes 49160 | tf_op jit(solution)/shard_map/ppermute | solution.py:259
  6.5 0.1 collective-permute-start.2
  6.5 3.6 %collective-permute-done.2.rest_0_ = bf16[24,256]{1,0:T(8,128)(2,1)S(1)} collective-permute-done((bf16[24,256]{1,0:T(8,128)(2,1)S(1)}, bf16[24,256]{1,0:T(8,128)(2,1)S(1)}, u32[]{:S(2)}, u32[]{:S(2)}) %collective-permute-start.2) | collective-permute-done | bytes 12320 | tf_op jit(solution)/shard_map/ppermute | solution.py:259
  10.1 0.0 collective-permute-done.halo_row_a
  10.2 0.0 collective-permute-done.1.halo_row_b
  10.2 1.4 %shard_map.47 = (bf16[4,128,256]{2,1,0:T(8,128)(2,1)S(1)}, bf16[4,128,256]{2,1,0:T(8,128)(2,1)S(1)}, f32[4,128,256]{2,1,0:T(8,128)S(1)}, f32[4,128,256]{2,1,0:T(8,128)S(1)}) custom-call(bf16[24,32,2048]{2,1,0:T(8,128)(2,1)S(1)} %get-tuple-element.15.masked, bf16[24,32,256]{2,1,0:T(8,128)(2,1)S(1)} %get-tuple-element.16.proj, ...), custom_call_target="tpu_custom_call" | custom-call | flops 805306368 | bytes 3145728 | tf_op jit(solution)/shard_map/pallas_call | solution.py:223
  11.5 0.1 collective-permute-start.7
  11.6 0.5 %collective-permute-start.3 = (bf16[4,128,256]{2,1,0:T(8,128)(2,1)S(1)}, bf16[4,128,256]{2,1,0:T(8,128)(2,1)S(1)}, u32[]{:S(2)}, u32[]{:S(2)}) collective-permute-start(bf16[4,128,256]{2,1,0:T(8,128)(2,1)S(1)} %get-tuple-element.22), channel_id=1, source_target_pairs={{0,1},{1,0},{2,3},{3,2},{4,5},{5,4},{6,7},{7,6},{8,9},{9,8},{10,11... | collective-permute-start | bytes 786440 | tf_op jit(solution)/shard_map/ppermute | solution.py:259
  12.1 1.0 %collective-permute-done.7 = bf16[4,128,256]{2,1,0:T(8,128)(2,1)S(1)} collective-permute-done((bf16[4,128,256]{2,1,0:T(8,128)(2,1)S(1)}, bf16[4,128,256]{2,1,0:T(8,128)(2,1)S(1)}, u32[]{:S(2)}, u32[]{:S(2)}) %collective-permute-start.7) | collective-permute-done | bytes 262176 | tf_op jit(solution)/shard_map/ppermute | solution.py:259
  13.1 0.1 fusion.1
  13.2 0.5 %collective-permute-start.8 = (bf16[2,128,256]{2,1,0:T(8,128)(2,1)S(1)}, bf16[2,128,256]{2,1,0:T(8,128)(2,1)S(1)}, u32[]{:S(2)}, u32[]{:S(2)}) collective-permute-start(bf16[2,128,256]{2,1,0:T(8,128)(2,1)S(1)} %get-tuple-element.27), channel_id=1, source_target_pairs={{0,3},{1,4},{2,7},{3,0},{4,1},{5,6},{6,5},{7,2},{8,13},{9,10},{10,... | collective-permute-start | bytes 393224 | tf_op jit(solution)/shard_map/ppermute | solution.py:259
  13.7 0.0 collective-permute-done.3
  13.7 0.1 fusion
  13.7 1.4 %collective-permute-start.4 = (bf16[2,128,256]{2,1,0:T(8,128)(2,1)S(1)}, bf16[2,128,256]{2,1,0:T(8,128)(2,1)S(1)}, u32[]{:S(2)}, u32[]{:S(2)}) collective-permute-start(bf16[2,128,256]{2,1,0:T(8,128)(2,1)S(1)} %get-tuple-element.25), channel_id=1, source_target_pairs={{0,3},{1,4},{2,7},{3,0},{4,1},{5,6},{6,5},{7,2},{8,13},{9,10},{10,... | collective-permute-start | bytes 393224 | tf_op jit(solution)/shard_map/ppermute | solution.py:259
  15.1 2.5 %collective-permute-done.8 = bf16[2,128,256]{2,1,0:T(8,128)(2,1)S(1)} collective-permute-done((bf16[2,128,256]{2,1,0:T(8,128)(2,1)S(1)}, bf16[2,128,256]{2,1,0:T(8,128)(2,1)S(1)}, u32[]{:S(2)}, u32[]{:S(2)}) %collective-permute-start.8) | collective-permute-done | bytes 131104 | tf_op jit(solution)/shard_map/ppermute | solution.py:259
  17.7 2.6 %collective-permute-start.9 = (bf16[1,128,256]{2,1,0:T(8,128)(2,1)S(1)}, bf16[1,128,256]{2,1,0:T(8,128)(2,1)S(1)}, u32[]{:S(2)}, u32[]{:S(2)}) collective-permute-start(bf16[1,128,256]{2,1,0:T(8,128)(2,1)S(1)} %fusion.2), channel_id=1, source_target_pairs={{0,9},{1,2},{2,1},{3,10},{4,7},{5,12},{6,15},{7,4},{8,11},{9,0},{1... | collective-permute-start | bytes 196616 | tf_op jit(solution)/shard_map/ppermute | solution.py:259
  20.3 0.0 collective-permute-done.4
  20.3 1.1 %collective-permute-start.5 = (bf16[1,128,256]{2,1,0:T(8,128)(2,1)S(1)}, bf16[1,128,256]{2,1,0:T(8,128)(2,1)S(1)}, u32[]{:S(2)}, u32[]{:S(2)}) collective-permute-start(bf16[1,128,256]{2,1,0:T(8,128)(2,1)S(1)} %fusion.5), channel_id=1, source_target_pairs={{0,9},{1,2},{2,1},{3,10},{4,7},{5,12},{6,15},{7,4},{8,11},{9,0},{1... | collective-permute-start | bytes 196616 | tf_op jit(solution)/shard_map/ppermute | solution.py:259
  21.5 0.9 %collective-permute-done.9 = bf16[1,128,256]{2,1,0:T(8,128)(2,1)S(1)} collective-permute-done((bf16[1,128,256]{2,1,0:T(8,128)(2,1)S(1)}, bf16[1,128,256]{2,1,0:T(8,128)(2,1)S(1)}, u32[]{:S(2)}, u32[]{:S(2)}) %collective-permute-start.9) | collective-permute-done | bytes 65568 | tf_op jit(solution)/shard_map/ppermute | solution.py:259
  22.3 2.5 %collective-permute-start.11 = (bf16[128,256]{1,0:T(8,128)(2,1)S(1)}, bf16[128,256]{1,0:T(8,128)(2,1)S(1)}, u32[]{:S(2)}, u32[]{:S(2)}) collective-permute-start(bf16[128,256]{1,0:T(8,128)(2,1)S(1)} %fusion.9), channel_id=1, source_target_pairs={{0,21},{1,24},{2,27},{3,22},{4,29},{5,16},{6,19},{7,30},{8,17},{9,... | collective-permute-start | bytes 196616 | tf_op jit(solution)/shard_map/ppermute | solution.py:259
  24.9 0.1 collective-permute-start.10
  25.0 0.0 collective-permute-done.5
  25.1 1.5 %collective-permute-start.6 = (bf16[128,256]{1,0:T(8,128)(2,1)S(1)}, bf16[128,256]{1,0:T(8,128)(2,1)S(1)}, u32[]{:S(2)}, u32[]{:S(2)}) collective-permute-start(bf16[128,256]{1,0:T(8,128)(2,1)S(1)} %fusion.8), channel_id=1, source_target_pairs={{0,16},{1,17},{2,18},{3,19},{4,20},{5,21},{6,22},{7,23},{8,24},{9,... | collective-permute-start | bytes 196616 | tf_op jit(solution)/shard_map/ppermute | solution.py:259
  26.6 0.8 %collective-permute-done.11 = bf16[128,256]{1,0:T(8,128)(2,1)S(1)} collective-permute-done((bf16[128,256]{1,0:T(8,128)(2,1)S(1)}, bf16[128,256]{1,0:T(8,128)(2,1)S(1)}, u32[]{:S(2)}, u32[]{:S(2)}) %collective-permute-start.11) | collective-permute-done | bytes 65568 | tf_op jit(solution)/shard_map/ppermute | solution.py:259
  27.4 1.5 %collective-permute-done.10 = bf16[128,256]{1,0:T(8,128)(2,1)S(1)} collective-permute-done((bf16[128,256]{1,0:T(8,128)(2,1)S(1)}, bf16[128,256]{1,0:T(8,128)(2,1)S(1)}, u32[]{:S(2)}, u32[]{:S(2)}) %collective-permute-start.10) | collective-permute-done | bytes 65568 | tf_op jit(solution)/shard_map/ppermute | solution.py:259
  28.9 1.0 %collective-permute-done.6 = bf16[128,256]{1,0:T(8,128)(2,1)S(1)} collective-permute-done((bf16[128,256]{1,0:T(8,128)(2,1)S(1)}, bf16[128,256]{1,0:T(8,128)(2,1)S(1)}, u32[]{:S(2)}, u32[]{:S(2)}) %collective-permute-start.6) | collective-permute-done | bytes 65568 | tf_op jit(solution)/shard_map/ppermute | solution.py:259
  29.9 0.7 %add_multiply_fusion = f32[128,256]{1,0:T(8,128)} fusion(bf16[128,256]{1,0:T(8,128)(2,1)S(1)} %collective-permute-done.11, bf16[128,256]{1,0:T(8,128)(2,1)S(1)} %collective-permute-done.10, bf16[128,256]{1,0:T(8,128)(2,1)S(1)} %collective-permute-done.6, bf16[128,256]{1,0:T(8,128)(2,1)S(1)} %fusion.8), kind=kLoop, calls=%fused_computation.16 | loop fusion | flops 262144 | bytes 393216 | tf_op jit(solution)/shard_map/mul | solution.py:305
  (4 shorter events, 0.1 us)
Async XLA Ops:
  3.3 6.8 %collective-permute-start = (bf16[32,256]{1,0:T(8,128)(2,1)S(1)}, bf16[32,256]{1,0:T(8,128)(2,1)S(1)}, u32[]{:S(2)}, u32[]{:S(2)}) collective-permute-start(bf16[32,256]{1,0:T(8,128)(2,1)S(1)} %get-tuple-element.17), channel_id=1, source_target_pairs={{0,1},{1,0},{2,3},{3,2},{4,5},{5,4},{6,7},{7,6},{8,9},{9,8},{10,11... | collective-permute-start | bytes 49160 | tf_op jit(solution)/shard_map/ppermute | solution.py:259
  3.9 6.3 %collective-permute-start.1 = (bf16[32,256]{1,0:T(8,128)(2,1)S(1)}, bf16[32,256]{1,0:T(8,128)(2,1)S(1)}, u32[]{:S(2)}, u32[]{:S(2)}) collective-permute-start(bf16[32,256]{1,0:T(8,128)(2,1)S(1)} %get-tuple-element.18), channel_id=1, source_target_pairs={{0,16},{1,2},{2,1},{3,4},{4,3},{5,6},{6,5},{7,8},{8,7},{9,10},{10,... | collective-permute-start | bytes 49160 | tf_op jit(solution)/shard_map/ppermute | solution.py:259
  6.5 3.7 %collective-permute-start.2 = (bf16[24,256]{1,0:T(8,128)(2,1)S(1)}, bf16[24,256]{1,0:T(8,128)(2,1)S(1)}, u32[]{:S(2)}, u32[]{:S(2)}) collective-permute-start(bf16[24,256]{1,0:T(8,128)(2,1)S(1)} %get-tuple-element.19), channel_id=1, source_target_pairs={{0,16},{1,17},{2,18},{3,19},{4,20},{5,21},{6,22},{7,23},{8,24},{9,... | collective-permute-start | bytes 36872 | tf_op jit(solution)/shard_map/ppermute | solution.py:259
  11.5 1.6 %collective-permute-start.7 = (bf16[4,128,256]{2,1,0:T(8,128)(2,1)S(1)}, bf16[4,128,256]{2,1,0:T(8,128)(2,1)S(1)}, u32[]{:S(2)}, u32[]{:S(2)}) collective-permute-start(bf16[4,128,256]{2,1,0:T(8,128)(2,1)S(1)} %get-tuple-element.24), channel_id=1, source_target_pairs={{0,1},{1,0},{2,3},{3,2},{4,5},{5,4},{6,7},{7,6},{8,9},{9,8},{10,11... | collective-permute-start | bytes 786440 | tf_op jit(solution)/shard_map/ppermute | solution.py:259
  11.6 2.1 %collective-permute-start.3 = (bf16[4,128,256]{2,1,0:T(8,128)(2,1)S(1)}, bf16[4,128,256]{2,1,0:T(8,128)(2,1)S(1)}, u32[]{:S(2)}, u32[]{:S(2)}) collective-permute-start(bf16[4,128,256]{2,1,0:T(8,128)(2,1)S(1)} %get-tuple-element.22), channel_id=1, source_target_pairs={{0,1},{1,0},{2,3},{3,2},{4,5},{5,4},{6,7},{7,6},{8,9},{9,8},{10,11... | collective-permute-start | bytes 786440 | tf_op jit(solution)/shard_map/ppermute | solution.py:259
  13.2 4.5 %collective-permute-start.8 = (bf16[2,128,256]{2,1,0:T(8,128)(2,1)S(1)}, bf16[2,128,256]{2,1,0:T(8,128)(2,1)S(1)}, u32[]{:S(2)}, u32[]{:S(2)}) collective-permute-start(bf16[2,128,256]{2,1,0:T(8,128)(2,1)S(1)} %get-tuple-element.27), channel_id=1, source_target_pairs={{0,3},{1,4},{2,7},{3,0},{4,1},{5,6},{6,5},{7,2},{8,13},{9,10},{10,... | collective-permute-start | bytes 393224 | tf_op jit(solution)/shard_map/ppermute | solution.py:259
  13.7 6.6 %collective-permute-start.4 = (bf16[2,128,256]{2,1,0:T(8,128)(2,1)S(1)}, bf16[2,128,256]{2,1,0:T(8,128)(2,1)S(1)}, u32[]{:S(2)}, u32[]{:S(2)}) collective-permute-start(bf16[2,128,256]{2,1,0:T(8,128)(2,1)S(1)} %get-tuple-element.25), channel_id=1, source_target_pairs={{0,3},{1,4},{2,7},{3,0},{4,1},{5,6},{6,5},{7,2},{8,13},{9,10},{10,... | collective-permute-start | bytes 393224 | tf_op jit(solution)/shard_map/ppermute | solution.py:259
  17.7 4.7 %collective-permute-start.9 = (bf16[1,128,256]{2,1,0:T(8,128)(2,1)S(1)}, bf16[1,128,256]{2,1,0:T(8,128)(2,1)S(1)}, u32[]{:S(2)}, u32[]{:S(2)}) collective-permute-start(bf16[1,128,256]{2,1,0:T(8,128)(2,1)S(1)} %fusion.2), channel_id=1, source_target_pairs={{0,9},{1,2},{2,1},{3,10},{4,7},{5,12},{6,15},{7,4},{8,11},{9,0},{1... | collective-permute-start | bytes 196616 | tf_op jit(solution)/shard_map/ppermute | solution.py:259
  20.3 4.7 %collective-permute-start.5 = (bf16[1,128,256]{2,1,0:T(8,128)(2,1)S(1)}, bf16[1,128,256]{2,1,0:T(8,128)(2,1)S(1)}, u32[]{:S(2)}, u32[]{:S(2)}) collective-permute-start(bf16[1,128,256]{2,1,0:T(8,128)(2,1)S(1)} %fusion.5), channel_id=1, source_target_pairs={{0,9},{1,2},{2,1},{3,10},{4,7},{5,12},{6,15},{7,4},{8,11},{9,0},{1... | collective-permute-start | bytes 196616 | tf_op jit(solution)/shard_map/ppermute | solution.py:259
  22.3 5.0 %collective-permute-start.11 = (bf16[128,256]{1,0:T(8,128)(2,1)S(1)}, bf16[128,256]{1,0:T(8,128)(2,1)S(1)}, u32[]{:S(2)}, u32[]{:S(2)}) collective-permute-start(bf16[128,256]{1,0:T(8,128)(2,1)S(1)} %fusion.9), channel_id=1, source_target_pairs={{0,21},{1,24},{2,27},{3,22},{4,29},{5,16},{6,19},{7,30},{8,17},{9,... | collective-permute-start | bytes 196616 | tf_op jit(solution)/shard_map/ppermute | solution.py:259
  24.9 4.0 %collective-permute-start.10 = (bf16[128,256]{1,0:T(8,128)(2,1)S(1)}, bf16[128,256]{1,0:T(8,128)(2,1)S(1)}, u32[]{:S(2)}, u32[]{:S(2)}) collective-permute-start(bf16[128,256]{1,0:T(8,128)(2,1)S(1)} %fusion.9), channel_id=1, source_target_pairs={{0,5},{1,8},{2,11},{3,6},{4,13},{5,0},{6,3},{7,14},{8,1},{9,12},{1... | collective-permute-start | bytes 196616 | tf_op jit(solution)/shard_map/ppermute | solution.py:259
  25.1 4.8 %collective-permute-start.6 = (bf16[128,256]{1,0:T(8,128)(2,1)S(1)}, bf16[128,256]{1,0:T(8,128)(2,1)S(1)}, u32[]{:S(2)}, u32[]{:S(2)}) collective-permute-start(bf16[128,256]{1,0:T(8,128)(2,1)S(1)} %fusion.8), channel_id=1, source_target_pairs={{0,16},{1,17},{2,18},{3,19},{4,20},{5,21},{6,22},{7,23},{8,24},{9,... | collective-permute-start | bytes 196616 | tf_op jit(solution)/shard_map/ppermute | solution.py:259

commit v7 on v6

--- a/solution.py
+++ b/solution.py
@@ -115,15 +115,15 @@
     lat, lon, rank = proj.shape
     wide = rank // shares.shape[2]
     place = lax.broadcasted_iota(jnp.int32, (lon, rank), 0)
+    above, row = north, proj[0].astype(F32)
     for i in range(lat):
-        row = proj[i].astype(F32)
-        above = proj[i - 1].astype(F32) if i else north
         below = proj[i + 1].astype(F32) if i < lat - 1 else south
         left = jnp.where(place == 0, west[i:i + 1, :], pltpu.roll(row, 1, 0))
         right = jnp.where(place == lon - 1, east[i:i + 1, :], pltpu.roll(row, lon - 1, 0))
         link = [jnp.tile(shares[k, pl.ds(i * lon, lon), :], (1, wide)) for k in range(4)]
         value = link[0] * above + link[1] * below + link[2] * left + link[3] * right
         smooth[pl.ds(i * lon, lon), :] = value.astype(BF16)
+        above, row = row, below
 
 
 def block_of(order, half, slot):
@@ -140,7 +140,7 @@
     own = jnp.where(half == 0, tile_bit(tile, orders[0][-1]), tile_bit(tile, orders[1][-1]))
     contract = (((0,), (0,)), ((), ()))
     if share % 128 == 0:
-        count = max(1, 256 // share)
+        count = min(places, max(1, 512 // share))
         for forward, out in ((1, outs[0]), (0, outs[1])):
             last = own ^ forward
             for place in range(0, places, count):

time: 30.7 us -> 30.6 us (level)
  no operation moved by 1% of the time
where the time goes in v7:
time: 30.6 us; the launch traced here: 30.5 us
  starting transfers between devices  13.6 us (44%)
  waiting for transfers between devices  11.4 us (37%)
  Pallas kernels  4.59 us (15%)
  other arithmetic  0.88 us (3%)
    ppermute x12, starting transfers between devices, exchange(): return lax.ppermute(values, AXES, pairs)  13.6 us
    ppermute x12, waiting for transfers between devices, exchange(): return lax.ppermute(values, AXES, pairs)  11.4 us
    pallas_call x1, Pallas kernels, project(): pl.pallas_call(project_kernel, out_shape=(pltpu.VMEM((lat, lon, words), B...  3.33 us
    pallas_call x1, Pallas kernels, partial_product(): pl.pallas_call(functools.partial(partial_kernel, orders), out_shape=(pltp...  1.25 us
    mul x1, other arithmetic, per_device(): return total * (1.0 / math.sqrt(lat * lon * groups * tiles))  0.69 us
  transfers between devices with their start and end apart: 12, of which 7 were waited for; matrix products, arithmetic and copies ran while one was open for 1% of the time, Pallas kernels for 0%

profile of v7, /device:TPU:0, one launch (start us, length us, event | category | flops | bytes accessed | tf_op | source)
XLA Modules:
  0.0 30.5 jit_solution(8595188122611468020)
XLA Ops:
  0.0 3.3 %shard_map.46 = (bf16[24,32,2048]{2,1,0:T(8,128)(2,1)S(1)}, bf16[24,32,256]{2,1,0:T(8,128)(2,1)S(1)}, f32[4,768,128]{2,1,0:T(8,128)S(1)}, bf16[32,256]{1,0:T(8,1...) custom-call(s32[12,1,16]{2,1,0:T(1,128)} %occ_hbm.1, s32[4,24,32]{2,1,0:T(8,128)} %links_hbm.1, ...), custom_call_target="tpu_custom_call" | custom-call | flops 805306368 | bytes 3145728 | tf_op jit(solution)/shard_map/pallas_call | solution.py:89
  3.3 0.6 %collective-permute-start = (bf16[32,256]{1,0:T(8,128)(2,1)S(1)}, bf16[32,256]{1,0:T(8,128)(2,1)S(1)}, u32[]{:S(2)}, u32[]{:S(2)}) collective-permute-start(bf16[32,256]{1,0:T(8,128)(2,1)S(1)} %get-tuple-element.17), channel_id=1, source_target_pairs={{0,1},{1,0},{2,3},{3,2},{4,5},{5,4},{6,7},{7,6},{8,9},{9,8},{10,11... | collective-permute-start | bytes 49160 | tf_op jit(solution)/shard_map/ppermute | solution.py:259
  3.9 2.6 %collective-permute-start.1 = (bf16[32,256]{1,0:T(8,128)(2,1)S(1)}, bf16[32,256]{1,0:T(8,128)(2,1)S(1)}, u32[]{:S(2)}, u32[]{:S(2)}) collective-permute-start(bf16[32,256]{1,0:T(8,128)(2,1)S(1)} %get-tuple-element.18), channel_id=1, source_target_pairs={{0,16},{1,2},{2,1},{3,4},{4,3},{5,6},{6,5},{7,8},{8,7},{9,10},{10,... | collective-permute-start | bytes 49160 | tf_op jit(solution)/shard_map/ppermute | solution.py:259
  6.5 0.1 collective-permute-start.2
  6.5 3.6 %collective-permute-done.2.rest_0_ = bf16[24,256]{1,0:T(8,128)(2,1)S(1)} collective-permute-done((bf16[24,256]{1,0:T(8,128)(2,1)S(1)}, bf16[24,256]{1,0:T(8,128)(2,1)S(1)}, u32[]{:S(2)}, u32[]{:S(2)}) %collective-permute-start.2) | collective-permute-done | bytes 12320 | tf_op jit(solution)/shard_map/ppermute | solution.py:259
  10.1 0.0 collective-permute-done.halo_row_a
  10.2 0.0 collective-permute-done.1.halo_row_b
  10.2 1.3 %shard_map.47 = (bf16[4,128,256]{2,1,0:T(8,128)(2,1)S(1)}, bf16[4,128,256]{2,1,0:T(8,128)(2,1)S(1)}, f32[4,128,256]{2,1,0:T(8,128)S(1)}, f32[4,128,256]{2,1,0:T(8,128)S(1)}) custom-call(bf16[24,32,2048]{2,1,0:T(8,128)(2,1)S(1)} %get-tuple-element.15.masked, bf16[24,32,256]{2,1,0:T(8,128)(2,1)S(1)} %get-tuple-element.16.proj, ...), custom_call_target="tpu_custom_call" | custom-call | flops 805306368 | bytes 3145728 | tf_op jit(solution)/shard_map/pallas_call | solution.py:223
  11.4 0.1 collective-permute-start.7
  11.5 0.5 %collective-permute-start.3 = (bf16[4,128,256]{2,1,0:T(8,128)(2,1)S(1)}, bf16[4,128,256]{2,1,0:T(8,128)(2,1)S(1)}, u32[]{:S(2)}, u32[]{:S(2)}) collective-permute-start(bf16[4,128,256]{2,1,0:T(8,128)(2,1)S(1)} %get-tuple-element.22), channel_id=1, source_target_pairs={{0,1},{1,0},{2,3},{3,2},{4,5},{5,4},{6,7},{7,6},{8,9},{9,8},{10,11... | collective-permute-start | bytes 786440 | tf_op jit(solution)/shard_map/ppermute | solution.py:259
  12.0 1.0 %collective-permute-done.7 = bf16[4,128,256]{2,1,0:T(8,128)(2,1)S(1)} collective-permute-done((bf16[4,128,256]{2,1,0:T(8,128)(2,1)S(1)}, bf16[4,128,256]{2,1,0:T(8,128)(2,1)S(1)}, u32[]{:S(2)}, u32[]{:S(2)}) %collective-permute-start.7) | collective-permute-done | bytes 262176 | tf_op jit(solution)/shard_map/ppermute | solution.py:259
  13.0 0.1 fusion.1
  13.1 0.5 %collective-permute-start.8 = (bf16[2,128,256]{2,1,0:T(8,128)(2,1)S(1)}, bf16[2,128,256]{2,1,0:T(8,128)(2,1)S(1)}, u32[]{:S(2)}, u32[]{:S(2)}) collective-permute-start(bf16[2,128,256]{2,1,0:T(8,128)(2,1)S(1)} %get-tuple-element.27), channel_id=1, source_target_pairs={{0,3},{1,4},{2,7},{3,0},{4,1},{5,6},{6,5},{7,2},{8,13},{9,10},{10,... | collective-permute-start | bytes 393224 | tf_op jit(solution)/shard_map/ppermute | solution.py:259
  13.6 0.0 collective-permute-done.3
  13.6 0.1 fusion
  13.6 1.4 %collective-permute-start.4 = (bf16[2,128,256]{2,1,0:T(8,128)(2,1)S(1)}, bf16[2,128,256]{2,1,0:T(8,128)(2,1)S(1)}, u32[]{:S(2)}, u32[]{:S(2)}) collective-permute-start(bf16[2,128,256]{2,1,0:T(8,128)(2,1)S(1)} %get-tuple-element.25), channel_id=1, source_target_pairs={{0,3},{1,4},{2,7},{3,0},{4,1},{5,6},{6,5},{7,2},{8,13},{9,10},{10,... | collective-permute-start | bytes 393224 | tf_op jit(solution)/shard_map/ppermute | solution.py:259
  15.0 2.5 %collective-permute-done.8 = bf16[2,128,256]{2,1,0:T(8,128)(2,1)S(1)} collective-permute-done((bf16[2,128,256]{2,1,0:T(8,128)(2,1)S(1)}, bf16[2,128,256]{2,1,0:T(8,128)(2,1)S(1)}, u32[]{:S(2)}, u32[]{:S(2)}) %collective-permute-start.8) | collective-permute-done | bytes 131104 | tf_op jit(solution)/shard_map/ppermute | solution.py:259
  17.6 2.7 %collective-permute-start.9 = (bf16[1,128,256]{2,1,0:T(8,128)(2,1)S(1)}, bf16[1,128,256]{2,1,0:T(8,128)(2,1)S(1)}, u32[]{:S(2)}, u32[]{:S(2)}) collective-permute-start(bf16[1,128,256]{2,1,0:T(8,128)(2,1)S(1)} %fusion.2), channel_id=1, source_target_pairs={{0,9},{1,2},{2,1},{3,10},{4,7},{5,12},{6,15},{7,4},{8,11},{9,0},{1... | collective-permute-start | bytes 196616 | tf_op jit(solution)/shard_map/ppermute | solution.py:259
  20.2 0.0 collective-permute-done.4
  20.2 1.1 %collective-permute-start.5 = (bf16[1,128,256]{2,1,0:T(8,128)(2,1)S(1)}, bf16[1,128,256]{2,1,0:T(8,128)(2,1)S(1)}, u32[]{:S(2)}, u32[]{:S(2)}) collective-permute-start(bf16[1,128,256]{2,1,0:T(8,128)(2,1)S(1)} %fusion.5), channel_id=1, source_target_pairs={{0,9},{1,2},{2,1},{3,10},{4,7},{5,12},{6,15},{7,4},{8,11},{9,0},{1... | collective-permute-start | bytes 196616 | tf_op jit(solution)/shard_map/ppermute | solution.py:259
  21.3 0.9 %collective-permute-done.9 = bf16[1,128,256]{2,1,0:T(8,128)(2,1)S(1)} collective-permute-done((bf16[1,128,256]{2,1,0:T(8,128)(2,1)S(1)}, bf16[1,128,256]{2,1,0:T(8,128)(2,1)S(1)}, u32[]{:S(2)}, u32[]{:S(2)}) %collective-permute-start.9) | collective-permute-done | bytes 65568 | tf_op jit(solution)/shard_map/ppermute | solution.py:259
  22.2 2.6 %collective-permute-start.11 = (bf16[128,256]{1,0:T(8,128)(2,1)S(1)}, bf16[128,256]{1,0:T(8,128)(2,1)S(1)}, u32[]{:S(2)}, u32[]{:S(2)}) collective-permute-start(bf16[128,256]{1,0:T(8,128)(2,1)S(1)} %fusion.9), channel_id=1, source_target_pairs={{0,21},{1,24},{2,27},{3,22},{4,29},{5,16},{6,19},{7,30},{8,17},{9,... | collective-permute-start | bytes 196616 | tf_op jit(solution)/shard_map/ppermute | solution.py:259
  24.8 0.1 collective-permute-start.10
  24.9 0.0 collective-permute-done.5
  25.0 1.5 %collective-permute-start.6 = (bf16[128,256]{1,0:T(8,128)(2,1)S(1)}, bf16[128,256]{1,0:T(8,128)(2,1)S(1)}, u32[]{:S(2)}, u32[]{:S(2)}) collective-permute-start(bf16[128,256]{1,0:T(8,128)(2,1)S(1)} %fusion.8), channel_id=1, source_target_pairs={{0,16},{1,17},{2,18},{3,19},{4,20},{5,21},{6,22},{7,23},{8,24},{9,... | collective-permute-start | bytes 196616 | tf_op jit(solution)/shard_map/ppermute | solution.py:259
  26.5 0.8 %collective-permute-done.11 = bf16[128,256]{1,0:T(8,128)(2,1)S(1)} collective-permute-done((bf16[128,256]{1,0:T(8,128)(2,1)S(1)}, bf16[128,256]{1,0:T(8,128)(2,1)S(1)}, u32[]{:S(2)}, u32[]{:S(2)}) %collective-permute-start.11) | collective-permute-done | bytes 65568 | tf_op jit(solution)/shard_map/ppermute | solution.py:259
  27.3 1.5 %collective-permute-done.10 = bf16[128,256]{1,0:T(8,128)(2,1)S(1)} collective-permute-done((bf16[128,256]{1,0:T(8,128)(2,1)S(1)}, bf16[128,256]{1,0:T(8,128)(2,1)S(1)}, u32[]{:S(2)}, u32[]{:S(2)}) %collective-permute-start.10) | collective-permute-done | bytes 65568 | tf_op jit(solution)/shard_map/ppermute | solution.py:259
  28.8 1.0 %collective-permute-done.6 = bf16[128,256]{1,0:T(8,128)(2,1)S(1)} collective-permute-done((bf16[128,256]{1,0:T(8,128)(2,1)S(1)}, bf16[128,256]{1,0:T(8,128)(2,1)S(1)}, u32[]{:S(2)}, u32[]{:S(2)}) %collective-permute-start.6) | collective-permute-done | bytes 65568 | tf_op jit(solution)/shard_map/ppermute | solution.py:259
  29.8 0.7 %add_multiply_fusion = f32[128,256]{1,0:T(8,128)} fusion(bf16[128,256]{1,0:T(8,128)(2,1)S(1)} %collective-permute-done.11, bf16[128,256]{1,0:T(8,128)(2,1)S(1)} %collective-permute-done.10, bf16[128,256]{1,0:T(8,128)(2,1)S(1)} %collective-permute-done.6, bf16[128,256]{1,0:T(8,128)(2,1)S(1)} %fusion.8), kind=kLoop, calls=%fused_computation.16 | loop fusion | flops 262144 | bytes 393216 | tf_op jit(solution)/shard_map/mul | solution.py:305
  (4 shorter events, 0.1 us)
Async XLA Ops:
  3.3 6.8 %collective-permute-start = (bf16[32,256]{1,0:T(8,128)(2,1)S(1)}, bf16[32,256]{1,0:T(8,128)(2,1)S(1)}, u32[]{:S(2)}, u32[]{:S(2)}) collective-permute-start(bf16[32,256]{1,0:T(8,128)(2,1)S(1)} %get-tuple-element.17), channel_id=1, source_target_pairs={{0,1},{1,0},{2,3},{3,2},{4,5},{5,4},{6,7},{7,6},{8,9},{9,8},{10,11... | collective-permute-start | bytes 49160 | tf_op jit(solution)/shard_map/ppermute | solution.py:259
  3.9 6.3 %collective-permute-start.1 = (bf16[32,256]{1,0:T(8,128)(2,1)S(1)}, bf16[32,256]{1,0:T(8,128)(2,1)S(1)}, u32[]{:S(2)}, u32[]{:S(2)}) collective-permute-start(bf16[32,256]{1,0:T(8,128)(2,1)S(1)} %get-tuple-element.18), channel_id=1, source_target_pairs={{0,16},{1,2},{2,1},{3,4},{4,3},{5,6},{6,5},{7,8},{8,7},{9,10},{10,... | collective-permute-start | bytes 49160 | tf_op jit(solution)/shard_map/ppermute | solution.py:259
  6.5 3.7 %collective-permute-start.2 = (bf16[24,256]{1,0:T(8,128)(2,1)S(1)}, bf16[24,256]{1,0:T(8,128)(2,1)S(1)}, u32[]{:S(2)}, u32[]{:S(2)}) collective-permute-start(bf16[24,256]{1,0:T(8,128)(2,1)S(1)} %get-tuple-element.19), channel_id=1, source_target_pairs={{0,16},{1,17},{2,18},{3,19},{4,20},{5,21},{6,22},{7,23},{8,24},{9,... | collective-permute-start | bytes 36872 | tf_op jit(solution)/shard_map/ppermute | solution.py:259
  11.4 1.6 %collective-permute-start.7 = (bf16[4,128,256]{2,1,0:T(8,128)(2,1)S(1)}, bf16[4,128,256]{2,1,0:T(8,128)(2,1)S(1)}, u32[]{:S(2)}, u32[]{:S(2)}) collective-permute-start(bf16[4,128,256]{2,1,0:T(8,128)(2,1)S(1)} %get-tuple-element.24), channel_id=1, source_target_pairs={{0,1},{1,0},{2,3},{3,2},{4,5},{5,4},{6,7},{7,6},{8,9},{9,8},{10,11... | collective-permute-start | bytes 786440 | tf_op jit(solution)/shard_map/ppermute | solution.py:259
  11.5 2.1 %collective-permute-start.3 = (bf16[4,128,256]{2,1,0:T(8,128)(2,1)S(1)}, bf16[4,128,256]{2,1,0:T(8,128)(2,1)S(1)}, u32[]{:S(2)}, u32[]{:S(2)}) collective-permute-start(bf16[4,128,256]{2,1,0:T(8,128)(2,1)S(1)} %get-tuple-element.22), channel_id=1, source_target_pairs={{0,1},{1,0},{2,3},{3,2},{4,5},{5,4},{6,7},{7,6},{8,9},{9,8},{10,11... | collective-permute-start | bytes 786440 | tf_op jit(solution)/shard_map/ppermute | solution.py:259
  13.1 4.5 %collective-permute-start.8 = (bf16[2,128,256]{2,1,0:T(8,128)(2,1)S(1)}, bf16[2,128,256]{2,1,0:T(8,128)(2,1)S(1)}, u32[]{:S(2)}, u32[]{:S(2)}) collective-permute-start(bf16[2,128,256]{2,1,0:T(8,128)(2,1)S(1)} %get-tuple-element.27), channel_id=1, source_target_pairs={{0,3},{1,4},{2,7},{3,0},{4,1},{5,6},{6,5},{7,2},{8,13},{9,10},{10,... | collective-permute-start | bytes 393224 | tf_op jit(solution)/shard_map/ppermute | solution.py:259
  13.6 6.6 %collective-permute-start.4 = (bf16[2,128,256]{2,1,0:T(8,128)(2,1)S(1)}, bf16[2,128,256]{2,1,0:T(8,128)(2,1)S(1)}, u32[]{:S(2)}, u32[]{:S(2)}) collective-permute-start(bf16[2,128,256]{2,1,0:T(8,128)(2,1)S(1)} %get-tuple-element.25), channel_id=1, source_target_pairs={{0,3},{1,4},{2,7},{3,0},{4,1},{5,6},{6,5},{7,2},{8,13},{9,10},{10,... | collective-permute-start | bytes 393224 | tf_op jit(solution)/shard_map/ppermute | solution.py:259
  17.6 4.7 %collective-permute-start.9 = (bf16[1,128,256]{2,1,0:T(8,128)(2,1)S(1)}, bf16[1,128,256]{2,1,0:T(8,128)(2,1)S(1)}, u32[]{:S(2)}, u32[]{:S(2)}) collective-permute-start(bf16[1,128,256]{2,1,0:T(8,128)(2,1)S(1)} %fusion.2), channel_id=1, source_target_pairs={{0,9},{1,2},{2,1},{3,10},{4,7},{5,12},{6,15},{7,4},{8,11},{9,0},{1... | collective-permute-start | bytes 196616 | tf_op jit(solution)/shard_map/ppermute | solution.py:259
  20.2 4.7 %collective-permute-start.5 = (bf16[1,128,256]{2,1,0:T(8,128)(2,1)S(1)}, bf16[1,128,256]{2,1,0:T(8,128)(2,1)S(1)}, u32[]{:S(2)}, u32[]{:S(2)}) collective-permute-start(bf16[1,128,256]{2,1,0:T(8,128)(2,1)S(1)} %fusion.5), channel_id=1, source_target_pairs={{0,9},{1,2},{2,1},{3,10},{4,7},{5,12},{6,15},{7,4},{8,11},{9,0},{1... | collective-permute-start | bytes 196616 | tf_op jit(solution)/shard_map/ppermute | solution.py:259
  22.2 5.0 %collective-permute-start.11 = (bf16[128,256]{1,0:T(8,128)(2,1)S(1)}, bf16[128,256]{1,0:T(8,128)(2,1)S(1)}, u32[]{:S(2)}, u32[]{:S(2)}) collective-permute-start(bf16[128,256]{1,0:T(8,128)(2,1)S(1)} %fusion.9), channel_id=1, source_target_pairs={{0,21},{1,24},{2,27},{3,22},{4,29},{5,16},{6,19},{7,30},{8,17},{9,... | collective-permute-start | bytes 196616 | tf_op jit(solution)/shard_map/ppermute | solution.py:259
  24.8 4.0 %collective-permute-start.10 = (bf16[128,256]{1,0:T(8,128)(2,1)S(1)}, bf16[128,256]{1,0:T(8,128)(2,1)S(1)}, u32[]{:S(2)}, u32[]{:S(2)}) collective-permute-start(bf16[128,256]{1,0:T(8,128)(2,1)S(1)} %fusion.9), channel_id=1, source_target_pairs={{0,5},{1,8},{2,11},{3,6},{4,13},{5,0},{6,3},{7,14},{8,1},{9,12},{1... | collective-permute-start | bytes 196616 | tf_op jit(solution)/shard_map/ppermute | solution.py:259
  25.0 4.8 %collective-permute-start.6 = (bf16[128,256]{1,0:T(8,128)(2,1)S(1)}, bf16[128,256]{1,0:T(8,128)(2,1)S(1)}, u32[]{:S(2)}, u32[]{:S(2)}) collective-permute-start(bf16[128,256]{1,0:T(8,128)(2,1)S(1)} %fusion.8), channel_id=1, source_target_pairs={{0,16},{1,17},{2,18},{3,19},{4,20},{5,21},{6,22},{7,23},{8,24},{9,... | collective-permute-start | bytes 196616 | tf_op jit(solution)/shard_map/ppermute | solution.py:259
